TPU v7x, 128 devices: a whole 4x4x4 slice. The times are simulated.
128 devices in a mesh: wide: 32 (over z, y, x_hi), narrow: 4 (over x_lo, core).
Axes of the slice: x: 4 (x_hi: 2, x_lo: 2; x = x_hi * 2 + x_lo), y: 4, z: 4, core: 2. Of those that a mesh axis runs over, the one named last changes fastest.
Arguments:
- noise: bfloat16 [128, 32, 256], P('wide'), may hold values from -6 to 6
- diagonal_tile_blocks: bfloat16 [128, 256, 256], P(('wide', 'narrow')), may hold values from -0.375 to 0.375
- left_factors: bfloat16 [128, 128, 128, 256], P('wide', 'narrow'), may hold values from -0.046875 to 0.046875
- right_factors: bfloat16 [128, 128, 128, 256], P('wide', 'narrow'), may hold values from -0.375 to 0.375
- ranks: int32 [128, 128], P('wide', 'narrow'), may hold values from 0 to 128, as said below
- owner: int32 [128], replicated, may hold values from 0 to 127, as said below
- courant_x: float32 [128, 256], P('wide', 'narrow'), may hold values from 0.05 to 0.4
- courant_number_second: float32 [128, 256], P('wide', 'narrow'), may hold values from 0.05 to 0.4
- upwind_x: int32 [128, 256], P('wide', 'narrow'), may hold values from 0 to 1
- upwind_y: int32 [128, 256], P('wide', 'narrow'), may hold values from 0 to 1
Outputs:
- tracer: float32 [32, 128, 256], P(None, 'wide', 'narrow')
Inputs may be any that keep to these rules, and one draw needn't show every extreme that they name: owner is a permutation of the tile rows 0 to 127. ranks[p, c] is 0 where c >= owner[p] and at least 1 where c < owner[p].
All inputs are finite; a program needn't handle non-finite values.
Results may differ from a plain program's by a relative error of at most 0.0016.
Values may be sent and summed in bfloat16 or wider, within the bound.
No kernel may reach another device: no remote copies, remote signals or barrier semaphores. Data moves between devices by JAX's collectives and lax.ppermute only.
A program may use at most 64 MiB of HBM per device.

v0:
```python
import jax
import jax.numpy as jnp
import numpy as np
from jax import lax
from jax.sharding import PartitionSpec as P

TSIDE = 16
TX = 8
TY = 16
ITERS = 4


mixing = 0.05


def from_everyone(value, axis):
    count = lax.axis_size(axis)
    return lax.all_to_all(
        jnp.broadcast_to(value[None], (count, *value.shape)), axis, 0, 0, tiled=True
    )


def in_order(tiles, dim):
    tiles = jnp.moveaxis(tiles, 0, dim)
    lengths = tiles.shape
    return tiles.reshape(*lengths[:dim], lengths[dim] * lengths[dim + 1], *lengths[dim + 2 :])


def gathered_copies(value, axis, dim):
    tiles = from_everyone(value, axis)
    return in_order(tiles, dim)


def cut_along(value, dim, count):
    lengths = value.shape
    tiles = value.reshape(*lengths[:dim], count, lengths[dim] // count, *lengths[dim + 1 :])
    return jnp.moveaxis(tiles, dim, 0)


def sum_at_owner(value, axis, dim):
    count = lax.axis_size(axis)
    tiles = lax.all_to_all(cut_along(value, dim, count), axis, 0, 0, tiled=True)
    return jnp.sum(tiles, axis=0)


def with_halo(block, sides, width):
    for axis, dim in sides:
        count = lax.axis_size(axis)
        forward = [(i, i + 1) for i in range(count - 1)]
        forward.append((count - 1, 0))
        backward = [(target, source) for source, target in forward]
        low = lax.ppermute(
            lax.slice_in_dim(block, block.shape[dim] - width, None, axis=dim), axis, forward
        )
        high = lax.ppermute(lax.slice_in_dim(block, 0, width, axis=dim), axis, backward)
        block = jnp.concatenate([low, block, high], axis=dim)
    return block


def morton_table(tiles_x, tiles_y):
    bits_x = tiles_x.bit_length() - 1
    bits_y = tiles_y.bit_length() - 1
    table = np.zeros((tiles_x, tiles_y), np.int32)
    for first in range(tiles_x):
        for second in range(tiles_y):
            morton_code = 0
            position = 0
            for level in range(max(bits_x, bits_y)):
                morton_code = morton_code | (second >> level & 1) << position
                position = position + 1
                if level < bits_x:
                    morton_code = morton_code | (first >> level & 1) << position
                    position = position + 1
            table[first, second] = morton_code
    return table


def advance(
    center, low_x, high_x, low_y, high_y, courant_x, courant_number_second, upwind_x, upwind_y
):
    from_x = jnp.where(upwind_x == 1, low_x, high_x)
    from_y = jnp.where(upwind_y == 1, low_y, high_y)
    return (
        center
        - courant_x * (center - from_x)
        - courant_number_second * (center - from_y)
        + mixing * (low_x + high_x + low_y + high_y - 4.0 * center)
    )


def lookup(indices, table_values):
    total = table_values.shape[0]
    matches = indices[..., None] == jnp.arange(total, dtype=jnp.int32)
    return jnp.sum(jnp.where(matches, table_values, 0), axis=-1)


def per_device(
    noise,
    diagonal_tile_blocks,
    left_factors,
    right_factors,
    ranks,
    owner,
    courant_x,
    courant_number_second,
    upwind_x,
    upwind_y,
):
    all_noise = gathered_copies(noise, "wide", 0)
    col_count = left_factors.shape[1]
    rank_count = left_factors.shape[2]
    col_begin = lax.axis_index("narrow") * col_count
    columns = lax.dynamic_slice_in_dim(all_noise, col_begin, col_count, 0)
    coeff = jnp.einsum("csk,pcrk->pcsr", columns, right_factors, preferred_element_type=jnp.float32)
    levels = lax.broadcasted_iota(jnp.int32, (1, 1, 1, rank_count), 3)
    coeff = jnp.where(levels < ranks[:, :, None, None], coeff, 0.0).astype(jnp.bfloat16)
    partial_value = jnp.einsum(
        "pcsr,pcrk->psk", coeff, left_factors, preferred_element_type=jnp.float32
    )
    row_sums = sum_at_owner(partial_value, "narrow", 0)
    held = row_sums.shape[0]
    device_rank = lax.axis_index("wide") * lax.axis_size("narrow") + lax.axis_index("narrow")
    held_tiles = lax.dynamic_slice_in_dim(owner, device_rank * held, held, 0)
    local_noise_tiles = all_noise[held_tiles]
    diagonal = jnp.einsum(
        "hpg,heg->hpe",
        local_noise_tiles,
        jnp.tril(diagonal_tile_blocks),
        preferred_element_type=jnp.float32,
    )
    samples = row_sums + diagonal
    block_x = courant_x.shape[0]
    block_y = courant_x.shape[1]
    members = samples.shape[1]
    table_np = morton_table(TX, TY)
    total_tiles = owner.shape[0]
    tile_x_np = np.zeros((total_tiles,), np.int32)
    tile_y_np = np.zeros((total_tiles,), np.int32)
    for first in range(TX):
        for second in range(TY):
            tile_x_np[table_np[first, second]] = first
            tile_y_np[table_np[first, second]] = second
    tile_x_of = jnp.asarray(tile_x_np)
    tile_y_of = jnp.asarray(tile_y_np)
    segments_each_tile = TSIDE // block_x
    tiles_per_block = block_y // TSIDE
    narrow_size = lax.axis_size("narrow")
    device_count = lax.axis_size("wide") * narrow_size
    retained_first_axis = lookup(held_tiles, tile_x_of)
    held_y = lookup(held_tiles, tile_y_of)
    piece_index = jnp.arange(segments_each_tile, dtype=jnp.int32)
    target = (
        retained_first_axis[:, None] * segments_each_tile + piece_index[None, :]
    ) * narrow_size + (held_y // tiles_per_block)[:, None]
    select = jnp.arange(device_count, dtype=jnp.int32)[:, None, None] == target[None, :, :]
    pieces = samples.reshape(held, members, segments_each_tile, block_x * TSIDE)
    outgoing = jnp.sum(jnp.where(select[:, :, None, :, None], pieces[None], 0.0), axis=3)
    incoming = lax.all_to_all(outgoing, ("wide", "narrow"), split_axis=0, concat_axis=0, tiled=True)
    source_tiles = owner.reshape(device_count, held)
    source_second_axis = lookup(source_tiles, tile_y_of) % tiles_per_block
    place = (
        jnp.arange(tiles_per_block, dtype=jnp.int32)[:, None, None]
        == source_second_axis[None, :, :]
    )
    incoming = incoming.reshape(device_count, held, members, block_x, TSIDE)
    placed = jnp.sum(jnp.where(place[:, :, :, None, None, None], incoming[None], 0.0), axis=(1, 2))
    current = placed.transpose(1, 2, 0, 3).reshape(members, block_x, block_y)
    stacked = jnp.stack(
        [
            courant_x,
            courant_number_second,
            upwind_x.astype(jnp.float32),
            upwind_y.astype(jnp.float32),
        ]
    )
    padded, coef_padded = (
        with_halo(current, (("wide", 1), ("narrow", 2)), ITERS),
        with_halo(stacked, (("wide", 1), ("narrow", 2)), ITERS),
    )
    flags_x = jnp.where(coef_padded[2] > 0.5, 1, 0)
    flags_y = jnp.where(coef_padded[3] > 0.5, 1, 0)
    for step_index in range(ITERS):
        padded = advance(
            padded,
            jnp.roll(padded, 1, 1),
            jnp.roll(padded, -1, 1),
            jnp.roll(padded, 1, 2),
            jnp.roll(padded, -1, 2),
            coef_padded[0],
            coef_padded[1],
            flags_x,
            flags_y,
        )
    current = padded[:, ITERS : ITERS + block_x, ITERS : ITERS + block_y]
    return current


def solution(mesh):
    placed = (
        P("wide", None, None),
        P(("wide", "narrow"), None, None),
        P("wide", "narrow", None, None),
        P("wide", "narrow", None, None),
        P("wide", "narrow"),
        P(),
        P("wide", "narrow"),
        P("wide", "narrow"),
        P("wide", "narrow"),
        P("wide", "narrow"),
    )
    return jax.shard_map(
        per_device, mesh=mesh, in_specs=placed, out_specs=P(None, "wide", "narrow"), check_vma=False
    )
```

profile of v0, /device:TPU:1, one launch (start us, length us, event | category | flops | bytes accessed | tf_op | source)
XLA Modules:
  0.0 123.5 jit_solution(5116732297669716820)
XLA Ops:
  0.0 2.5 %broadcast_in_dim.128 = bf16[32,4,32,256]{3,2,1,0:T(8,128)(2,1)} broadcast(bf16[4,32,256]{2,1,0:T(8,128)(2,1)} %param.12), dimensions={1,2,3} | broadcast | bytes 2162688 | tf_op jit(solution)/shard_map/broadcast_in_dim | solution.py:19
  2.5 11.3 %all-to-all-start = ((bf16[32,4,32,256]{3,2,1,0:T(8,128)(2,1)}), bf16[32,4,32,256]{3,2,1,0:T(8,128)(2,1)S(1)}, u32[]{:S(2)}, u32[]{:S(2)}) async-start(bf16[32,4,32,256]{3,2,1,0:T(8,128)(2,1)} %broadcast_in_dim.128), calls=%async_computation | async-start | bytes 4194304 | tf_op jit(solution)/shard_map/all_to_all | solution.py:18
  14.5 1.4 %fusion.15 = (s32[]{:T(128)}, s32[]{:T(128)}) fusion(s32[128]{0:T(128)S(1)} %copy-done.6, s32[]{:T(128)} %bitcast, s32[128]{0:T(128)S(1)} %copy-done.5), kind=kLoop, calls=%fused_computation.63 | loop fusion | flops 638 | bytes 1036 | tf_op jit(solution)/shard_map/reduce_sum | solution.py:94
  19.4 23.9 %all-to-all-done = bf16[32,4,32,256]{3,2,1,0:T(8,128)(2,1)S(1)} async-done(((bf16[32,4,32,256]{3,2,1,0:T(8,128)(2,1)}), bf16[32,4,32,256]{3,2,1,0:T(8,128)(2,1)S(1)}, u32[]{:S(2)}, u32[]{:S(2)}) %all-to-all-start) | async-done | bytes 2097184 | tf_op jit(solution)/shard_map/all_to_all | solution.py:18
  43.2 10.4 %convolution_bitcast_fusion = f32[4,1,32,256]{3,2,1,0:T(8,128)} fusion(bf16[4,32,128,256]{3,2,1,0:T(8,128)(2,1)} %param.14, bf16[4,32,128,256]{3,2,1,0:T(8,128)(2,1)} %param.15, pred[4,32,128]{2,1,0:T(8,128)(4,1)S(1)} %iota_compare_fusion.1, bf16[128,32,256]{2,1,0:T(8,128)(2,1)S(1)} %bitcast.50, s32[]{:T(128)S(6)} %select_n.120), kind=kOutput, calls=%fused_computation.4 | convolution fusion | flops 537919488 | bytes 17448964 | tf_op jit(solution)/shard_map/pcsr,pcrk->psk/dot_general | solution.py:117
  53.7 5.4 %all-to-all-start.1 = ((f32[4,1,32,256]{3,2,1,0:T(8,128)}), f32[4,1,32,256]{3,2,1,0:T(8,128)S(1)}, u32[]{:S(2)}, u32[]{:S(2)}) async-start(f32[4,1,32,256]{3,2,1,0:T(8,128)} %convolution_bitcast_fusion), calls=%async_computation.1 | async-start | bytes 262144 | tf_op jit(solution)/shard_map/all_to_all | solution.py:42
  61.2 1.6 %all-to-all-done.1 = f32[4,1,32,256]{3,2,1,0:T(8,128)S(1)} async-done(((f32[4,1,32,256]{3,2,1,0:T(8,128)}), f32[4,1,32,256]{3,2,1,0:T(8,128)S(1)}, u32[]{:S(2)}, u32[]{:S(2)}) %all-to-all-start.1) | async-done | bytes 131104 | tf_op jit(solution)/shard_map/all_to_all | solution.py:42
  63.1 1.3 %select_reduce_fusion.1 = f32[128,32,64]{0,2,1:T(8,128)S(1)} fusion(f32[32,4,64]{2,1,0:T(4,128)S(1)} %broadcast_in_dim.132, pred[128,4]{0,1:T(4,128)(4,1)S(1)} %iota_compare_fusion.3), kind=kLoop, calls=%fused_computation.1 | loop fusion | flops 1835008 | bytes 1081856 | tf_op jit(solution)/shard_map/reduce_sum | solution.py:157
  64.4 1.8 %copy.25 = f32[128,1,32,64]{3,2,1,0:T(8,128)S(1)} copy(f32[128,1,32,64]{0,3,2,1:T(8,128)S(1)} %bitcast.48) | data formatting | bytes 2097152 | tf_op jit(solution)/shard_map/reduce_sum | solution.py:157
  66.2 2.3 %reshape.255 = f32[128,1,2048]{2,1,0:T(1,128)} reshape(f32[128,1,32,64]{3,2,1,0:T(8,128)S(1)} %copy.25) | data formatting | bytes 2097152
  68.5 5.1 %all-to-all-start.2 = ((f32[128,1,2048]{2,1,0:T(1,128)}), f32[128,1,2048]{2,1,0:T(1,128)S(1)}, u32[]{:S(2)}, u32[]{:S(2)}) async-start(f32[128,1,2048]{2,1,0:T(1,128)} %reshape.255), calls=%async_computation.2 | async-start | bytes 2097152 | tf_op jit(solution)/shard_map/all_to_all | solution.py:158
  73.7 3.0 %collective-permute-start.4 = (f32[4,4,64]{2,1,0:T(4,128)S(1)}, f32[4,4,64]{2,1,0:T(4,128)S(1)}, u32[]{:S(2)}, u32[]{:S(2)}) collective-permute-start(f32[4,4,64]{2,1,0:T(4,128)S(1)} %pad_maximum_fusion.18), channel_id=1, source_target_pairs={{0,4},{4,8},{8,12},{12,16},{16,20},{20,24},{24,28},{28,32},{32,36}... | collective-permute-start | bytes 12296 | tf_op jit(solution)/shard_map/ppermute | solution.py:52
  76.6 5.2 %collective-permute-start.5 = (f32[4,4,64]{2,1,0:T(4,128)S(1)}, f32[4,4,64]{2,1,0:T(4,128)S(1)}, u32[]{:S(2)}, u32[]{:S(2)}) collective-permute-start(f32[4,4,64]{2,1,0:T(4,128)S(1)} %pad_maximum_fusion.18), channel_id=1, source_target_pairs={{4,0},{8,4},{12,8},{16,12},{20,16},{24,20},{28,24},{32,28},{36,32}... | collective-permute-start | bytes 12296 | tf_op jit(solution)/shard_map/ppermute | solution.py:55
  82.0 11.0 %collective-permute-done.4 = f32[4,4,64]{2,1,0:T(4,128)S(1)} collective-permute-done((f32[4,4,64]{2,1,0:T(4,128)S(1)}, f32[4,4,64]{2,1,0:T(4,128)S(1)}, u32[]{:S(2)}, u32[]{:S(2)}) %collective-permute-start.4) | collective-permute-done | bytes 4128 | tf_op jit(solution)/shard_map/ppermute | solution.py:52
  93.1 1.3 %collective-permute-start.6 = (f32[4,12,4]{2,1,0:T(8,128)S(1)}, f32[4,12,4]{2,1,0:T(8,128)S(1)}, u32[]{:S(2)}, u32[]{:S(2)}) collective-permute-start(f32[4,12,4]{2,1,0:T(8,128)S(1)} %get-tuple-element.52), channel_id=1, source_target_pairs={{0,1},{1,2},{2,3},{3,0},{4,5},{5,6},{6,7},{7,4},{8,9},{9,10},{10,1... | collective-permute-start | bytes 2312 | tf_op jit(solution)/shard_map/ppermute | solution.py:52
  94.5 0.9 collective-permute-done.6
  95.4 2.3 %collective-permute-done.7 = f32[4,12,4]{2,1,0:T(8,128)S(1)} collective-permute-done((f32[4,12,4]{2,1,0:T(8,128)S(1)}, f32[4,12,4]{2,1,0:T(8,128)S(1)}, u32[]{:S(2)}, u32[]{:S(2)}) %collective-permute-start.7) | collective-permute-done | bytes 800 | tf_op jit(solution)/shard_map/ppermute | solution.py:55
  98.4 3.1 %reduce.7 = f32[128,2048]{1,0:T(8,128)S(1)} reduce(f32[128,1,2048]{2,1,0:T(1,128)S(1)} %all-to-all-done.2, f32[]{:T(128)} %broadcast.261), dimensions={1}, to_apply=%all_to_all.11.reduce_sub_computation | reduce | bytes 2097156 | tf_op jit(solution)/shard_map/all_to_all | solution.py:158
  101.5 0.8 reshape.256
  102.3 1.3 %copy.26 = f32[128,1,32,64]{0,3,2,1:T(8,128)S(1)} copy(f32[128,1,32,64]{3,2,1,0:T(8,128)S(1)} %reshape.256) | data formatting | bytes 2097152 | tf_op jit(solution)/shard_map/all_to_all | solution.py:158
  103.6 1.4 %select_reduce_fusion = f32[4,32,4,16]{3,2,1,0:T(4,128)S(1)} fusion(f32[128,32,4,16]{0,3,2,1:T(8,128)S(1)} %bitcast.49, pred[4,128]{1,0:T(4,128)(4,1)S(1)} %iota_compare_fusion.4), kind=kLoop, calls=%fused_computation | loop fusion | flops 2088960 | bytes 1081856 | tf_op jit(solution)/shard_map/reduce_sum | solution.py:166
  105.2 7.2 %collective-permute-start.1 = (f32[32,4,64]{0,2,1:T(8,128)S(1)}, f32[32,4,64]{0,2,1:T(8,128)S(1)}, u32[]{:S(2)}, u32[]{:S(2)}) collective-permute-start(f32[32,4,64]{0,2,1:T(8,128)S(1)} %bitcast.54), channel_id=1, source_target_pairs={{4,0},{8,4},{12,8},{16,12},{20,16},{24,20},{28,24},{32,28},{36,32}... | collective-permute-start | bytes 98312 | tf_op jit(solution)/shard_map/ppermute | solution.py:55
  112.4 3.8 %collective-permute-done = f32[32,4,64]{0,2,1:T(8,128)S(1)} collective-permute-done((f32[32,4,64]{0,2,1:T(8,128)S(1)}, f32[32,4,64]{0,2,1:T(8,128)S(1)}, u32[]{:S(2)}, u32[]{:S(2)}) %collective-permute-start) | collective-permute-done | bytes 32800 | tf_op jit(solution)/shard_map/ppermute | solution.py:52
  118.1 2.1 %collective-permute-done.3 = f32[32,12,4]{0,2,1:T(4,128)S(1)} collective-permute-done((f32[32,12,4]{0,2,1:T(4,128)S(1)}, f32[32,12,4]{0,2,1:T(4,128)S(1)}, u32[]{:S(2)}, u32[]{:S(2)}) %collective-permute-start.3) | collective-permute-done | bytes 6176 | tf_op jit(solution)/shard_map/ppermute | solution.py:55
  (79 shorter events, 7.4 us)
Async XLA Ops:
  0.0 14.5 %copy-start.6 = (s32[128]{0:T(128)S(1)}, s32[128]{0:T(128)}, u32[]{:S(2)}) copy-start(s32[128]{0:T(128)} %constant.74.clone) | copy-start | bytes 1540
  0.0 14.5 %copy-start.5 = (s32[128]{0:T(128)S(1)}, s32[128]{0:T(128)}, u32[]{:S(2)}) copy-start(s32[128]{0:T(128)} %constant.75.clone) | copy-start | bytes 1540
  0.0 13.9 %copy-start.8 = (s32[128]{0:T(128)S(1)}, s32[128]{0:T(128)}, u32[]{:S(2)}) copy-start(s32[128]{0:T(128)} %param.17) | copy-start | bytes 1540
  0.0 19.2 %copy-start.4 = (s32[4,64]{1,0:T(4,128)S(1)}, s32[4,64]{1,0:T(4,128)}, u32[]{:S(2)}) copy-start(s32[4,64]{1,0:T(4,128)} %param.20) | copy-start | bytes 3076
  0.0 19.2 %copy-start.3 = (s32[4,64]{1,0:T(4,128)S(1)}, s32[4,64]{1,0:T(4,128)}, u32[]{:S(2)}) copy-start(s32[4,64]{1,0:T(4,128)} %param.21) | copy-start | bytes 3076
  0.0 19.3 %copy-start.2 = (s32[4,32]{1,0:T(4,128)S(1)}, s32[4,32]{1,0:T(4,128)}, u32[]{:S(2)}) copy-start(s32[4,32]{1,0:T(4,128)} %param.16) | copy-start | bytes 1540
  2.5 40.7 %all-to-all-start = ((bf16[32,4,32,256]{3,2,1,0:T(8,128)(2,1)}), bf16[32,4,32,256]{3,2,1,0:T(8,128)(2,1)S(1)}, u32[]{:S(2)}, u32[]{:S(2)}) async-start(bf16[32,4,32,256]{3,2,1,0:T(8,128)(2,1)} %broadcast_in_dim.128), calls=%async_computation | async-start | bytes 4194304 | tf_op jit(solution)/shard_map/all_to_all | solution.py:18
  43.2 19.5 %copy-start.7 = (bf16[1,256,256]{2,1,0:T(8,128)(2,1)S(1)}, bf16[1,256,256]{2,1,0:T(8,128)(2,1)}, u32[]{:S(2)}) copy-start(bf16[1,256,256]{2,1,0:T(8,128)(2,1)} %param.13) | copy-start | bytes 393220
  53.7 9.0 %all-to-all-start.1 = ((f32[4,1,32,256]{3,2,1,0:T(8,128)}), f32[4,1,32,256]{3,2,1,0:T(8,128)S(1)}, u32[]{:S(2)}, u32[]{:S(2)}) async-start(f32[4,1,32,256]{3,2,1,0:T(8,128)} %convolution_bitcast_fusion), calls=%async_computation.1 | async-start | bytes 262144 | tf_op jit(solution)/shard_map/all_to_all | solution.py:42
  64.4 9.2 %copy-start = (f32[4,64]{1,0:T(4,128)S(1)}, f32[4,64]{1,0:T(4,128)}, u32[]{:S(2)}) copy-start(f32[4,64]{1,0:T(4,128)} %param.19) | copy-start | bytes 3076
  64.4 9.2 %copy-start.1 = (f32[4,64]{1,0:T(4,128)S(1)}, f32[4,64]{1,0:T(4,128)}, u32[]{:S(2)}) copy-start(f32[4,64]{1,0:T(4,128)} %param.18) | copy-start | bytes 3076
  68.5 29.3 %all-to-all-start.2 = ((f32[128,1,2048]{2,1,0:T(1,128)}), f32[128,1,2048]{2,1,0:T(1,128)S(1)}, u32[]{:S(2)}, u32[]{:S(2)}) async-start(f32[128,1,2048]{2,1,0:T(1,128)} %reshape.255), calls=%async_computation.2 | async-start | bytes 2097152 | tf_op jit(solution)/shard_map/all_to_all | solution.py:158
  73.7 19.4 %collective-permute-start.4 = (f32[4,4,64]{2,1,0:T(4,128)S(1)}, f32[4,4,64]{2,1,0:T(4,128)S(1)}, u32[]{:S(2)}, u32[]{:S(2)}) collective-permute-start(f32[4,4,64]{2,1,0:T(4,128)S(1)} %pad_maximum_fusion.18), channel_id=1, source_target_pairs={{0,4},{4,8},{8,12},{12,16},{16,20},{20,24},{24,28},{28,32},{32,36}... | collective-permute-start | bytes 12296 | tf_op jit(solution)/shard_map/ppermute | solution.py:52
  76.6 16.4 %collective-permute-start.5 = (f32[4,4,64]{2,1,0:T(4,128)S(1)}, f32[4,4,64]{2,1,0:T(4,128)S(1)}, u32[]{:S(2)}, u32[]{:S(2)}) collective-permute-start(f32[4,4,64]{2,1,0:T(4,128)S(1)} %pad_maximum_fusion.18), channel_id=1, source_target_pairs={{4,0},{8,4},{12,8},{16,12},{20,16},{24,20},{28,24},{32,28},{36,32}... | collective-permute-start | bytes 12296 | tf_op jit(solution)/shard_map/ppermute | solution.py:55
  93.1 2.3 %collective-permute-start.6 = (f32[4,12,4]{2,1,0:T(8,128)S(1)}, f32[4,12,4]{2,1,0:T(8,128)S(1)}, u32[]{:S(2)}, u32[]{:S(2)}) collective-permute-start(f32[4,12,4]{2,1,0:T(8,128)S(1)} %get-tuple-element.52), channel_id=1, source_target_pairs={{0,1},{1,2},{2,3},{3,0},{4,5},{5,6},{6,7},{7,4},{8,9},{9,10},{10,1... | collective-permute-start | bytes 2312 | tf_op jit(solution)/shard_map/ppermute | solution.py:52
  94.4 3.3 %collective-permute-start.7 = (f32[4,12,4]{2,1,0:T(8,128)S(1)}, f32[4,12,4]{2,1,0:T(8,128)S(1)}, u32[]{:S(2)}, u32[]{:S(2)}) collective-permute-start(f32[4,12,4]{2,1,0:T(8,128)S(1)} %get-tuple-element.53), channel_id=1, source_target_pairs={{1,0},{2,1},{3,2},{0,3},{5,4},{6,5},{7,6},{4,7},{9,8},{10,9},{11,1... | collective-permute-start | bytes 2312 | tf_op jit(solution)/shard_map/ppermute | solution.py:55
  105.1 11.0 %collective-permute-start = (f32[32,4,64]{0,2,1:T(8,128)S(1)}, f32[32,4,64]{0,2,1:T(8,128)S(1)}, u32[]{:S(2)}, u32[]{:S(2)}) collective-permute-start(f32[32,4,64]{0,2,1:T(8,128)S(1)} %bitcast.53), channel_id=1, source_target_pairs={{0,4},{4,8},{8,12},{12,16},{16,20},{20,24},{24,28},{28,32},{32,36}... | collective-permute-start | bytes 98312 | tf_op jit(solution)/shard_map/ppermute | solution.py:52
  105.2 11.0 %collective-permute-start.1 = (f32[32,4,64]{0,2,1:T(8,128)S(1)}, f32[32,4,64]{0,2,1:T(8,128)S(1)}, u32[]{:S(2)}, u32[]{:S(2)}) collective-permute-start(f32[32,4,64]{0,2,1:T(8,128)S(1)} %bitcast.54), channel_id=1, source_target_pairs={{4,0},{8,4},{12,8},{16,12},{20,16},{24,20},{28,24},{32,28},{36,32}... | collective-permute-start | bytes 98312 | tf_op jit(solution)/shard_map/ppermute | solution.py:55
  116.2 1.7 %collective-permute-start.2 = (f32[32,12,4]{0,2,1:T(4,128)S(1)}, f32[32,12,4]{0,2,1:T(4,128)S(1)}, u32[]{:S(2)}, u32[]{:S(2)}) collective-permute-start(f32[32,12,4]{0,2,1:T(4,128)S(1)} %get-tuple-element.16), channel_id=1, source_target_pairs={{0,1},{1,2},{2,3},{3,0},{4,5},{5,6},{6,7},{7,4},{8,9},{9,10},{10,1... | collective-permute-start | bytes 18440 | tf_op jit(solution)/shard_map/ppermute | solution.py:52
  116.9 3.3 %collective-permute-start.3 = (f32[32,12,4]{0,2,1:T(4,128)S(1)}, f32[32,12,4]{0,2,1:T(4,128)S(1)}, u32[]{:S(2)}, u32[]{:S(2)}) collective-permute-start(f32[32,12,4]{0,2,1:T(4,128)S(1)} %get-tuple-element.17), channel_id=1, source_target_pairs={{1,0},{2,1},{3,2},{0,3},{5,4},{6,5},{7,6},{4,7},{9,8},{10,9},{11,1... | collective-permute-start | bytes 18440 | tf_op jit(solution)/shard_map/ppermute | solution.py:55
where the time goes:
time: 124 us; the launch traced here: 123 us
  waiting for transfers between devices  45.7 us (37%)
  starting transfers between devices  39.7 us (32%)
  local copies, waits for them, and re-layouts  12.9 us (10%)
  matrix products  10.6 us (9%)
  other arithmetic  8.78 us (7%)
  between operations  5.78 us (5%)
    all_to_all x1, waiting for transfers between devices, from_everyone(): lax.all_to_all(jnp.broadcast_to(value[None], (count, *value.shape)), axis...  23.9 us
    ppermute x4, waiting for transfers between devices, with_halo(): lax.ppermute(lax.slice_in_dim(block, block.shape[dim] - width, None, axis...  15.9 us
    ppermute x4, starting transfers between devices, with_halo(): lax.ppermute(lax.slice_in_dim(block, 0, width, axis=dim), axis, backward)  12.9 us
    all_to_all x1, starting transfers between devices, from_everyone(): lax.all_to_all(jnp.broadcast_to(value[None], (count, *value.shape)), axis...  11.3 us
    dot_general x1, matrix products, per_device(): jnp.einsum('pcsr,pcrk->psk', coeff, left_factors, preferred_element_type=...  10.4 us
    all_to_all x1, starting transfers between devices, sum_at_owner(): tiles = lax.all_to_all(cut_along(value, dim, count), axis, 0, 0, tiled=True)  5.45 us
    all_to_all x1, starting transfers between devices, per_device(): lax.all_to_all(outgoing, ('wide', 'narrow'), split_axis=0, concat_axis=0,...  5.07 us
    ppermute x4, starting transfers between devices, with_halo(): lax.ppermute(lax.slice_in_dim(block, block.shape[dim] - width, None, axis...  5 us
  transfers between devices with their start and end apart: 11, of which 8 were waited for; matrix products, arithmetic and copies ran while one was open for 2% of the time, Pallas kernels for 0%

commit v1 on v0

v1 whole, which is shorter than its diff:
```python
import functools

import jax
import jax.numpy as jnp
import numpy as np
from jax import lax
from jax.experimental import pallas as pl
from jax.experimental.pallas import tpu as pltpu
from jax.sharding import PartitionSpec as P

ITERS = 4
MIXING = 0.05
BOTH = ("wide", "narrow")
VMEM = pltpu.VMEM
SMEM = pltpu.SMEM


def specs(*spaces):
    return [pl.BlockSpec(memory_space=space) for space in spaces]


def factor_kernel(info, ranks, noise, right, left, diag, out, coeff, turned):
    rows, cols, rank_max, cells = right.shape
    members = noise.shape[1]
    levels = lax.broadcasted_iota(jnp.int32, (members, rank_max), 1)
    for c in range(cols):
        block = right[:, c].reshape(rows * rank_max, cells)
        product = lax.dot_general(
            noise[c], block, (((1,), (1,)), ((), ())), preferred_element_type=jnp.float32
        )
        for p in range(rows):
            piece = product[:, p * rank_max : (p + 1) * rank_max]
            piece = jnp.where(levels < ranks[p, c], piece, 0.0).astype(jnp.bfloat16)
            coeff[p, :, c * rank_max : (c + 1) * rank_max] = piece
    for p in range(rows):
        total = jnp.dot(
            coeff[p],
            left[p].reshape(cols * rank_max, cells),
            preferred_element_type=jnp.float32,
        )
        local = info[p] - info[rows]
        held = jnp.logical_and(local >= 0, local < cols)
        tile = noise[jnp.clip(local, 0, cols - 1)]
        own = lax.dot_general(
            tile, diag[p], (((1,), (1,)), ((), ())), preferred_element_type=jnp.float32
        )
        total = total + jnp.where(held, own, 0.0)
        for g in range(members // 8):
            for h in range(2):
                turned[pl.ds(64 * g + 2 * p + h, 8, stride=8), :] = total[
                    8 * g : 8 * g + 8, 128 * h : 128 * h + 128
                ]
    for d in range(out.shape[0]):
        member = d % members
        out[d] = turned[8 * member : 8 * member + 8, :]


def spread_kernel(got, cx, cy):
    for tx in range(8):
        quarters = [got[tx * 64 + k * 16 : tx * 64 + k * 16 + 16, :] for k in range(4)]
        for pair in range(2):
            a, b = quarters[2 * pair], quarters[2 * pair + 1]
            lane = lax.broadcasted_iota(jnp.int32, (16, 128), 1)
            first = jnp.where(lane < 64, a, pltpu.roll(b, 64, 1))
            second = jnp.where(lane < 64, pltpu.roll(a, 64, 1), b)
            cx[tx * 16 : tx * 16 + 16, pair * 128 : pair * 128 + 128] = first
            cy[tx * 16 : tx * 16 + 16, pair * 128 : pair * 128 + 128] = second


def stencil_kernel(plane, place, got, cx_ref, cy_ref, out, summed, field_ref):
    total = got[:, 0] + got[:, 1] + got[:, 2] + got[:, 3]
    summed[...] = total.reshape(256, 128)
    target = lax.broadcasted_iota(jnp.int32, (128, 128), 0)
    one_hot = jnp.where(target == place[...], 1.0, 0.0)
    halves = [
        jnp.dot(
            one_hot,
            summed[pl.ds(h, 128, stride=2), :],
            precision=lax.Precision.HIGHEST,
            preferred_element_type=jnp.float32,
        )
        for h in range(2)
    ]
    field = jnp.concatenate(halves, axis=1)
    shape = field.shape
    lane = lax.broadcasted_iota(jnp.int32, shape, 1)
    column = lane % 16
    tile_y = lax.broadcasted_iota(jnp.int32, shape, 0) % 16
    top, bottom = lane < 16, lane >= 240
    left, right = column == 0, column == 15
    first, last = tile_y == 0, tile_y == 15
    cx, cy = cx_ref[...], cy_ref[...]
    low_x_up, low_y_up = cx > 0, cy > 0
    cx, cy = jnp.abs(cx), jnp.abs(cy)
    for _ in range(ITERS):
        down = pltpu.roll(field, 16, 1)
        low_x = jnp.where(top, pltpu.roll(down, 16, 0), down)
        up = pltpu.roll(field, 240, 1)
        high_x = jnp.where(bottom, pltpu.roll(up, 112, 0), up)
        edge = pltpu.roll(field, 241, 1)
        edge = jnp.where(first, pltpu.roll(edge, 113, 0), pltpu.roll(edge, 1, 0))
        low_y = jnp.where(left, edge, pltpu.roll(field, 1, 1))
        edge = pltpu.roll(field, 15, 1)
        edge = jnp.where(last, pltpu.roll(edge, 15, 0), pltpu.roll(edge, 127, 0))
        high_y = jnp.where(right, edge, pltpu.roll(field, 255, 1))
        from_x = jnp.where(low_x_up, low_x, high_x)
        from_y = jnp.where(low_y_up, low_y, high_y)
        field = (
            field
            - cx * (field - from_x)
            - cy * (field - from_y)
            + MIXING * (low_x + high_x + low_y + high_y - 4.0 * field)
        )
    field_ref[...] = field
    mine = field_ref[pl.ds(pl.multiple_of(plane[0] * 32, 32), 32), :]
    for txl in range(2):
        for k in range(4):
            for nd in range(4):
                row = txl * 16 + nd * 4
                half = (k // 2) * 128
                out[txl * 16 + k * 4 + nd] = mine[row : row + 4, half : half + 128]


def block_kernel(parity, got, out):
    lane = lax.broadcasted_iota(jnp.int32, (got.shape[0], 128), 1)
    odd = parity[0] == 1
    pieces = []
    for a in range(4):
        x = got[:, a, :]
        pieces.append(jnp.where(odd, pltpu.roll(x, 64, 1), x))
    for i in range(4):
        line = jnp.zeros(lane.shape, jnp.float32)
        for a in range(4):
            shift = (16 * (a - i)) % 128
            moved = pltpu.roll(pieces[a], shift, 1) if shift else pieces[a]
            line = jnp.where(lane // 16 == a, moved, line)
        out[:, i, :] = line[:, :64]


def shared(value, count):
    return jnp.broadcast_to(value[None], (count, *value.shape))


def per_device(
    noise,
    diagonal_tile_blocks,
    left_factors,
    right_factors,
    ranks,
    owner,
    courant_x,
    courant_number_second,
    upwind_x,
    upwind_y,
):
    wide, narrow = lax.axis_size("wide"), lax.axis_size("narrow")
    group = wide // narrow
    devices = wide * narrow
    w, n = lax.axis_index("wide"), lax.axis_index("narrow")
    plane = w // group
    rows, cols = ranks.shape
    members = noise.shape[1]
    cells = noise.shape[2]

    swap = [
        ((z * group + r) * narrow + b, (b * group + r) * narrow + z)
        for z in range(narrow)
        for r in range(group)
        for b in range(narrow)
    ]
    planes = [[z * group + r for r in range(group)] for z in range(narrow)]
    slabs = [[z * group * narrow + i for i in range(group * narrow)] for z in range(narrow)]

    with jax.named_scope("diagonal_gather"):
        diag = lax.all_to_all(
            shared(jnp.tril(diagonal_tile_blocks[0]), narrow), "narrow", 0, 0, tiled=True
        )
    with jax.named_scope("noise_gather"):
        swapped = lax.ppermute(noise, BOTH, swap)
        columns = lax.all_to_all(
            shared(swapped, group), "wide", 0, 0, axis_index_groups=planes, tiled=True
        ).reshape(group * rows, members, cells)

    with jax.named_scope("coefficient_gather"):
        signed = [
            jnp.where(flag == 1, value, -value)
            .reshape(rows, 4, 16)
            .transpose(1, 0, 2)
            .reshape(4, 64)
            for value, flag in ((courant_x, upwind_x), (courant_number_second, upwind_y))
        ]
        own = jnp.concatenate(signed, axis=1)
        everyone = lax.all_to_all(shared(own, devices), BOTH, 0, 0, tiled=True)
        cx, cy = pl.pallas_call(
            spread_kernel,
            out_shape=[jax.ShapeDtypeStruct((128, 256), jnp.float32)] * 2,
            in_specs=specs(VMEM),
            out_specs=specs(VMEM, VMEM),
        )(everyone.reshape(devices * 4, 128))

    with jax.named_scope("factors"):
        info = jnp.concatenate(
            [lax.dynamic_slice_in_dim(owner, w * rows, rows), (n * cols)[None].astype(jnp.int32)]
        )
        partial_sums = pl.pallas_call(
            factor_kernel,
            out_shape=jax.ShapeDtypeStruct((devices, 8, 128), jnp.float32),
            in_specs=specs(SMEM, SMEM, VMEM, VMEM, VMEM, VMEM),
            out_specs=pl.BlockSpec(memory_space=VMEM),
            scratch_shapes=[
                pltpu.VMEM((rows, members, cols * ranks_max(left_factors)), jnp.bfloat16),
                pltpu.VMEM((members * 8, 128), jnp.float32),
            ],
            compiler_params=pltpu.CompilerParams(vmem_limit_bytes=40 << 20),
        )(info, ranks, columns, right_factors, left_factors, diag)

    with jax.named_scope("member_exchange"):
        got = lax.all_to_all(partial_sums, BOTH, 0, 0, tiled=True)

    with jax.named_scope("stencil"):
        bits = [(owner >> b) & 1 for b in range(7)]
        tile_y = bits[0] | bits[2] << 1 | bits[4] << 2 | bits[6] << 3
        tile_x = bits[1] | bits[3] << 1 | bits[5] << 2
        place = (tile_x * 16 + tile_y)[None]
        blocks = pl.pallas_call(
            stencil_kernel,
            out_shape=jax.ShapeDtypeStruct((members, 4, 128), jnp.float32),
            in_specs=specs(SMEM, VMEM, VMEM, VMEM, VMEM),
            out_specs=pl.BlockSpec(memory_space=VMEM),
            scratch_shapes=[
                pltpu.VMEM((256, 128), jnp.float32),
                pltpu.VMEM((128, 256), jnp.float32),
            ],
        )(plane[None].astype(jnp.int32), place, got.reshape(wide, narrow, 8, 128), cx, cy)

    with jax.named_scope("block_exchange"):
        mine = lax.all_to_all(blocks, BOTH, 0, 0, axis_index_groups=slabs, tiled=True)

    with jax.named_scope("block"):
        return pl.pallas_call(
            block_kernel,
            out_shape=jax.ShapeDtypeStruct((members, 4, 64), jnp.float32),
            in_specs=specs(SMEM, VMEM),
            out_specs=pl.BlockSpec(memory_space=VMEM),
        )((w % 2)[None].astype(jnp.int32), mine)


def ranks_max(factors):
    return factors.shape[2]


def solution(mesh):
    placed = (
        P("wide", None, None),
        P(("wide", "narrow"), None, None),
        P("wide", "narrow", None, None),
        P("wide", "narrow", None, None),
        P("wide", "narrow"),
        P(),
        P("wide", "narrow"),
        P("wide", "narrow"),
        P("wide", "narrow"),
        P("wide", "narrow"),
    )
    return jax.shard_map(
        per_device, mesh=mesh, in_specs=placed, out_specs=P(None, "wide", "narrow"), check_vma=False
    )
```

time: 124 us -> 98.1 us (0.79)
  Pallas kernels: 0 us -> 15.2 us
  waiting for transfers between devices: 45.7 us -> 31.7 us
  matrix products: 10.6 us -> 0 us
  other arithmetic: 8.78 us -> 3.01 us
  between operations: 5.78 us -> 0.09 us
  local copies, waits for them, and re-layouts: 12.9 us -> 8.99 us
  starting transfers between devices: 39.7 us -> 38.4 us
    ppermute x8 -> x1, waiting for transfers between devices: 20.2 us -> 2.22 us  [per_device(): swapped = lax.ppermute(noise, BOTH, swap)]
    pallas_call x0 -> x4, Pallas kernels: none -> 15.2 us  [the longest x1 8.46 us: per_device(): pl.pallas_call(factor_kernel, out_shape=jax.ShapeDtypeStruct((devices, 8,...]
    ppermute x8 -> x1, starting transfers between devices: 17.9 us -> 3.56 us  [per_device(): swapped = lax.ppermute(noise, BOTH, swap)]
    all_to_all x3 -> x5, starting transfers between devices: 21.9 us -> 34.9 us  [the longest x1 9.76 us: per_device(): got = lax.all_to_all(partial_sums, BOTH, 0, 0, tiled=True)]
    dot_general x2 -> x0, matrix products: 10.6 us -> none  [the longest x1 10.4 us: per_device(): jnp.einsum('pcsr,pcrk->psk', coeff, left_factors, preferred_element_type=...]
    reduce_sum x5 -> x0, other arithmetic: 4.22 us -> none  [the longest x2 1.53 us: lookup(): return jnp.sum(jnp.where(matches, table_values, 0), axis=-1)]
    all_to_all x3 -> x5, waiting for transfers between devices: 25.4 us -> 29.4 us  [the longest x1 11.4 us: per_device(): got = lax.all_to_all(partial_sums, BOTH, 0, 0, tiled=True)]
    all_to_all x1 -> x0, other arithmetic: 3.13 us -> none  [per_device(): lax.all_to_all(outgoing, ('wide', 'narrow'), split_axis=0, concat_axis=0,...]
  transfers between devices with their start and end apart: 11 -> 6, of which waited for: 8 -> 5; matrix products, arithmetic and copies ran while one was open for 2% -> 3% of each run, Pallas kernels for 0% -> 11%
where the time goes in v1:
time: 98.1 us; the launch traced here: 97.4 us
  starting transfers between devices  38.4 us (39%)
  waiting for transfers between devices  31.7 us (32%)
  Pallas kernels  15.2 us (15%)
  local copies, waits for them, and re-layouts  8.99 us (9%)
  other arithmetic  3.01 us (3%)
    all_to_all x1, waiting for transfers between devices, per_device(): got = lax.all_to_all(partial_sums, BOTH, 0, 0, tiled=True)  11.4 us
    all_to_all x1, starting transfers between devices, per_device(): got = lax.all_to_all(partial_sums, BOTH, 0, 0, tiled=True)  9.76 us
    all_to_all x1, starting transfers between devices, per_device(): everyone = lax.all_to_all(shared(own, devices), BOTH, 0, 0, tiled=True)  9.15 us
    pallas_call x1, Pallas kernels, per_device(): pl.pallas_call(factor_kernel, out_shape=jax.ShapeDtypeStruct((devices, 8,...  8.46 us
    all_to_all x1, waiting for transfers between devices, per_device(): lax.all_to_all(shared(swapped, group), 'wide', 0, 0, axis_index_groups=pl...  8.45 us
    all_to_all x1, waiting for transfers between devices, per_device(): lax.all_to_all(blocks, BOTH, 0, 0, axis_index_groups=slabs, tiled=True)  7.42 us
    all_to_all x1, starting transfers between devices, per_device(): lax.all_to_all(shared(swapped, group), 'wide', 0, 0, axis_index_groups=pl...  6.73 us
    unnamed x12, local copies, waits for them, and re-layouts  5.49 us
  transfers between devices with their start and end apart: 6, of which 5 were waited for; matrix products, arithmetic and copies ran while one was open for 3% of the time, Pallas kernels for 11%

profile of v1, /device:TPU:1, one launch (start us, length us, event | category | flops | bytes accessed | tf_op | source)
XLA Modules:
  0.0 97.4 jit_solution(5598829871019744723)
XLA Ops:
  0.0 0.9 fusion.1
  0.9 0.8 broadcast_in_dim.43
  1.8 4.9 %all-to-all-start.1 = ((bf16[4,256,256]{2,1,0:T(8,128)(2,1)}), bf16[4,256,256]{2,1,0:T(8,128)(2,1)S(1)}, u32[]{:S(2)}, u32[]{:S(2)}) async-start(bf16[4,256,256]{2,1,0:T(8,128)(2,1)} %broadcast_in_dim.43), calls=%async_computation.1 | async-start | bytes 1048576 | tf_op jit(solution)/shard_map/diagonal_gather/all_to_all | solution.py:175
  6.6 3.6 %collective-permute-start = (bf16[4,32,256]{2,1,0:T(8,128)(2,1)}, bf16[4,32,256]{2,1,0:T(8,128)(2,1)S(1)}, u32[]{:S(2)}, u32[]{:S(2)}) collective-permute-start(bf16[4,32,256]{2,1,0:T(8,128)(2,1)} %param.10), channel_id=1, source_target_pairs={{0,0},{1,32},{2,64},{3,96},{4,4},{5,36},{6,68},{7,100},{8,8},{9,40... | collective-permute-start | bytes 196616 | tf_op jit(solution)/shard_map/noise_gather/ppermute | solution.py:179
  10.2 2.2 %collective-permute-done = bf16[4,32,256]{2,1,0:T(8,128)(2,1)S(1)} collective-permute-done((bf16[4,32,256]{2,1,0:T(8,128)(2,1)}, bf16[4,32,256]{2,1,0:T(8,128)(2,1)S(1)}, u32[]{:S(2)}, u32[]{:S(2)}) %collective-permute-start) | collective-permute-done | bytes 65568 | tf_op jit(solution)/shard_map/noise_gather/ppermute | solution.py:179
  12.4 2.2 %all-to-all-done.1.diag = bf16[4,256,256]{2,1,0:T(8,128)(2,1)S(1)} async-done(((bf16[4,256,256]{2,1,0:T(8,128)(2,1)}), bf16[4,256,256]{2,1,0:T(8,128)(2,1)S(1)}, u32[]{:S(2)}, u32[]{:S(2)}) %all-to-all-start.1) | async-done | bytes 524320 | tf_op jit(solution)/shard_map/diagonal_gather/all_to_all | solution.py:175
  14.6 0.8 broadcast_in_dim.40
  15.4 6.7 %all-to-all-start = ((bf16[8,4,32,256]{3,2,1,0:T(8,128)(2,1)}), bf16[8,4,32,256]{3,2,1,0:T(8,128)(2,1)S(1)}, u32[]{:S(2)}, u32[]{:S(2)}) async-start(bf16[8,4,32,256]{3,2,1,0:T(8,128)(2,1)} %broadcast_in_dim.40), calls=%async_computation | async-start | bytes 1048576 | tf_op jit(solution)/shard_map/noise_gather/all_to_all | solution.py:180
  22.2 0.7 negate_select_fusion.1
  23.1 0.7 negate_select_fusion
  24.0 8.5 %all-to-all-done = bf16[8,4,32,256]{3,2,1,0:T(8,128)(2,1)S(1)} async-done(((bf16[8,4,32,256]{3,2,1,0:T(8,128)(2,1)}), bf16[8,4,32,256]{3,2,1,0:T(8,128)(2,1)S(1)}, u32[]{:S(2)}, u32[]{:S(2)}) %all-to-all-start) | async-done | bytes 524320 | tf_op jit(solution)/shard_map/noise_gather/all_to_all | solution.py:180
  32.5 0.7 broadcast_in_dim.44
  33.2 9.1 %all-to-all-start.3 = ((f32[128,4,128]{2,1,0:T(4,128)}), f32[128,4,128]{2,1,0:T(4,128)S(1)}, u32[]{:S(2)}, u32[]{:S(2)}) async-start(f32[128,4,128]{2,1,0:T(4,128)} %broadcast_in_dim.44), calls=%async_computation.3 | async-start | bytes 524288 | tf_op jit(solution)/shard_map/coefficient_gather/all_to_all | solution.py:193
  42.4 0.7 dynamic_slice.3
  43.2 3.4 %copy-done = bf16[4,32,128,256]{3,2,1,0:T(8,128)(2,1)S(1)} copy-done((bf16[4,32,128,256]{3,2,1,0:T(8,128)(2,1)S(1)}, bf16[4,32,128,256]{3,2,1,0:T(8,128)(2,1)}, u32[]{:S(2)}) %copy-start) | copy-done | bytes 8388632
  47.2 8.5 %factors.1 = f32[128,8,128]{2,1,0:T(8,128)} custom-call(s32[5]{0:T(128)S(1)} %pad_add_fusion.info, s32[4,32]{1,0:T(4,128)S(1)} %copy-done.1, bf16[32,32,256]{2,1,0:T(8,128)(2,1)S(1)} %bitcast.16, bf16[4,32,128,256]{3,2,1,0:T(8,128)(2,1)S(1)} %copy-done, bf16[4,32,128,256]{3,2,1,0:T(8,128)(2,1)} %left.1, bf16[4,256,256]{2,1,0:T(8,128)(2,1)S(1)} %all-to-all-done.1.diag), custom_call_target="tpu_custom_call" | custom-call | tf_op jit(solution)/shard_map/factors/pallas_call | solution.py:205
  55.7 9.8 %all-to-all-start.2 = ((f32[128,8,128]{2,1,0:T(8,128)}), f32[128,8,128]{2,1,0:T(8,128)S(1)}, u32[]{:S(2)}, u32[]{:S(2)}) async-start(f32[128,8,128]{2,1,0:T(8,128)} %factors.1), calls=%async_computation.2 | async-start | bytes 1048576 | tf_op jit(solution)/shard_map/member_exchange/all_to_all | solution.py:218
  66.0 1.8 %coefficient_gather.1 = (f32[128,256]{1,0:T(8,128)}, f32[128,256]{1,0:T(8,128)}) custom-call(f32[512,128]{1,0:T(8,128)} %bitcast.18), custom_call_target="tpu_custom_call" | custom-call | tf_op jit(solution)/shard_map/coefficient_gather/pallas_call | solution.py:194
  67.8 11.4 %all-to-all-done.2 = f32[128,8,128]{2,1,0:T(8,128)S(1)} async-done(((f32[128,8,128]{2,1,0:T(8,128)}), f32[128,8,128]{2,1,0:T(8,128)S(1)}, u32[]{:S(2)}, u32[]{:S(2)}) %all-to-all-start.2) | async-done | bytes 524320 | tf_op jit(solution)/shard_map/member_exchange/all_to_all | solution.py:218
  79.2 0.8 copy-done.2
  80.0 3.3 %stencil.1 = f32[32,4,128]{2,1,0:T(4,128)} custom-call(s32[1]{0:T(128)} %bitcast.1.plane, s32[1,128]{1,0:T(1,128)} %add_bitcast_fusion.place, f32[32,4,8,128]{3,2,1,0:T(8,128)} %bitcast.17, f32[128,256]{1,0:T(8,128)} %get-tuple-element.7.cx_ref, f32[128,256]{1,0:T(8,128)} %get-tuple-element.8.cy_ref), custom_call_target="tpu_custom_call" | custom-call | tf_op jit(solution)/shard_map/stencil/pallas_call | solution.py:225
  83.3 4.4 %all-to-all-start.4 = ((f32[32,4,128]{2,1,0:T(4,128)}), f32[32,4,128]{2,1,0:T(4,128)S(1)}, u32[]{:S(2)}, u32[]{:S(2)}) async-start(f32[32,4,128]{2,1,0:T(4,128)} %stencil.1), calls=%async_computation.4 | async-start | bytes 131072 | tf_op jit(solution)/shard_map/block_exchange/all_to_all | solution.py:237
  87.7 7.4 %all-to-all-done.4.got = f32[32,4,128]{2,1,0:T(4,128)S(1)} async-done(((f32[32,4,128]{2,1,0:T(4,128)}), f32[32,4,128]{2,1,0:T(4,128)S(1)}, u32[]{:S(2)}, u32[]{:S(2)}) %all-to-all-start.4) | async-done | bytes 65568 | tf_op jit(solution)/shard_map/block_exchange/all_to_all | solution.py:237
  95.7 1.7 %block.1 = f32[32,4,64]{2,1,0:T(4,128)} custom-call(s32[1]{0:T(128)} %bitcast.parity, f32[32,4,128]{2,1,0:T(4,128)} %copy-done.4), custom_call_target="tpu_custom_call" | custom-call | tf_op jit(solution)/shard_map/block/pallas_call | solution.py:240
  (20 shorter events, 2.4 us)
Async XLA Ops:
  1.8 12.8 %all-to-all-start.1 = ((bf16[4,256,256]{2,1,0:T(8,128)(2,1)}), bf16[4,256,256]{2,1,0:T(8,128)(2,1)S(1)}, u32[]{:S(2)}, u32[]{:S(2)}) async-start(bf16[4,256,256]{2,1,0:T(8,128)(2,1)} %broadcast_in_dim.43), calls=%async_computation.1 | async-start | bytes 1048576 | tf_op jit(solution)/shard_map/diagonal_gather/all_to_all | solution.py:175
  6.6 5.8 %collective-permute-start = (bf16[4,32,256]{2,1,0:T(8,128)(2,1)}, bf16[4,32,256]{2,1,0:T(8,128)(2,1)S(1)}, u32[]{:S(2)}, u32[]{:S(2)}) collective-permute-start(bf16[4,32,256]{2,1,0:T(8,128)(2,1)} %param.10), channel_id=1, source_target_pairs={{0,0},{1,32},{2,64},{3,96},{4,4},{5,36},{6,68},{7,100},{8,8},{9,40... | collective-permute-start | bytes 196616 | tf_op jit(solution)/shard_map/noise_gather/ppermute | solution.py:179
  15.4 17.0 %all-to-all-start = ((bf16[8,4,32,256]{3,2,1,0:T(8,128)(2,1)}), bf16[8,4,32,256]{3,2,1,0:T(8,128)(2,1)S(1)}, u32[]{:S(2)}, u32[]{:S(2)}) async-start(bf16[8,4,32,256]{3,2,1,0:T(8,128)(2,1)} %broadcast_in_dim.40), calls=%async_computation | async-start | bytes 1048576 | tf_op jit(solution)/shard_map/noise_gather/all_to_all | solution.py:180
  33.2 22.5 %all-to-all-start.3 = ((f32[128,4,128]{2,1,0:T(4,128)}), f32[128,4,128]{2,1,0:T(4,128)S(1)}, u32[]{:S(2)}, u32[]{:S(2)}) async-start(f32[128,4,128]{2,1,0:T(4,128)} %broadcast_in_dim.44), calls=%async_computation.3 | async-start | bytes 524288 | tf_op jit(solution)/shard_map/coefficient_gather/all_to_all | solution.py:193
  43.2 3.4 %copy-start = (bf16[4,32,128,256]{3,2,1,0:T(8,128)(2,1)S(1)}, bf16[4,32,128,256]{3,2,1,0:T(8,128)(2,1)}, u32[]{:S(2)}) copy-start(bf16[4,32,128,256]{3,2,1,0:T(8,128)(2,1)} %right.1) | copy-start | bytes 25165828
  46.6 0.7 copy-start.1
  47.2 18.3 %copy-start.5 = (s32[128]{0:T(128)S(1)}, s32[128]{0:T(128)}, u32[]{:S(2)}) copy-start(s32[128]{0:T(128)} %param.15) | copy-start | bytes 1540
  55.7 10.3 %copy-start.3 = (f32[128,4,128]{2,1,0:T(4,128)}, f32[128,4,128]{2,1,0:T(4,128)S(1)}, u32[]{:S(2)}) copy-start(f32[128,4,128]{2,1,0:T(4,128)S(1)} %all-to-all-done.3) | copy-start | bytes 786436
  55.7 23.5 %all-to-all-start.2 = ((f32[128,8,128]{2,1,0:T(8,128)}), f32[128,8,128]{2,1,0:T(8,128)S(1)}, u32[]{:S(2)}, u32[]{:S(2)}) async-start(f32[128,8,128]{2,1,0:T(8,128)} %factors.1), calls=%async_computation.2 | async-start | bytes 1048576 | tf_op jit(solution)/shard_map/member_exchange/all_to_all | solution.py:218
  79.2 0.8 copy-start.2
  83.3 11.8 %all-to-all-start.4 = ((f32[32,4,128]{2,1,0:T(4,128)}), f32[32,4,128]{2,1,0:T(4,128)S(1)}, u32[]{:S(2)}, u32[]{:S(2)}) async-start(f32[32,4,128]{2,1,0:T(4,128)} %stencil.1), calls=%async_computation.4 | async-start | bytes 131072 | tf_op jit(solution)/shard_map/block_exchange/all_to_all | solution.py:237
  95.1 0.6 copy-start.4

commit v2 on v1

v2 whole, which is shorter than its diff:
```python
import functools

import jax
import jax.numpy as jnp
import numpy as np
from jax import lax
from jax.experimental import pallas as pl
from jax.experimental.pallas import tpu as pltpu
from jax.sharding import PartitionSpec as P

ITERS = 4
MIXING = 0.05
BOTH = ("wide", "narrow")
VMEM = pltpu.VMEM
SMEM = pltpu.SMEM
MIB = 1 << 20


def specs(*spaces):
    return [pl.BlockSpec(memory_space=space) for space in spaces]


def near(value):
    return pltpu.with_memory_space_constraint(value, VMEM)


def far(value):
    return pltpu.with_memory_space_constraint(value, pltpu.HBM)


def limit(mib):
    return pltpu.CompilerParams(vmem_limit_bytes=mib * MIB)


def factor_kernel(info, keep, noise, right, left, d0, d1, d2, d3, out, coeff, turned, own):
    rows, cols, rank_max, cells = right.shape
    members = noise.shape[1]
    for j, diag in enumerate((d0, d1, d2, d3)):
        row = info[rows] ^ j
        local = info[row]
        held = jnp.logical_and(local >= 0, local < cols)
        tile = noise[jnp.clip(local, 0, cols - 1)]
        term = lax.dot_general(
            tile, diag[...], (((1,), (1,)), ((), ())), preferred_element_type=jnp.float32
        )
        own[row] = jnp.where(held, term, 0.0)
    for c in range(cols):
        span = slice(c * rank_max, (c + 1) * rank_max)
        block = right[:, c].reshape(rows * rank_max, cells)
        product = lax.dot_general(
            noise[c], block, (((1,), (1,)), ((), ())), preferred_element_type=jnp.float32
        )
        for p in range(rows):
            piece = product[:, p * rank_max : (p + 1) * rank_max]
            piece = jnp.where(keep[p : p + 1, span] > 0, piece, 0.0)
            coeff[p, :, span] = piece.astype(jnp.bfloat16)
    for p in range(rows):
        total = own[p] + jnp.dot(
            coeff[p],
            left[p].reshape(cols * rank_max, cells),
            preferred_element_type=jnp.float32,
        )
        for g in range(members // 8):
            for h in range(2):
                turned[pl.ds(64 * g + 2 * p + h, 8, stride=8), :] = total[
                    8 * g : 8 * g + 8, 128 * h : 128 * h + 128
                ]
    for d in range(out.shape[0]):
        member = d % members
        out[d] = turned[8 * member : 8 * member + 8, :]


def fetch_kernel(right, left, right_out, left_out, done):
    parts = 4
    copies = []
    for i, (source, target) in enumerate(((right, right_out), (left, left_out))):
        for j in range(parts):
            copies.append(pltpu.make_async_copy(source.at[j], target.at[j], done.at[parts * i + j]))
    for copy in copies:
        copy.start()
    for copy in copies:
        copy.wait()


def weight_kernel(parity, low, own, high, out):
    lane = lax.broadcasted_iota(jnp.int32, (8, 128), 1)
    odd = parity[0] == 1
    pieces = [
        jnp.concatenate(
            [low[4 * q + 2 : 4 * q + 4, :], own[4 * q : 4 * q + 4, :], high[4 * q : 4 * q + 2, :]],
            axis=0,
        )
        for q in range(3)
    ]
    turned = [pltpu.roll(piece, 64, 1) for piece in pieces]
    zero = jnp.zeros((8, 128), jnp.float32)
    for h in range(2):
        signed = []
        for first, second in ((pieces, turned), (turned, pieces)):
            if h == 0:
                even_form = jnp.where(lane < 64, zero, second[0])
                odd_form = jnp.where(lane < 64, first[0], second[1])
            else:
                even_form = jnp.where(lane < 64, first[1], second[2])
                odd_form = jnp.where(lane < 64, first[2], zero)
            signed.append(jnp.where(odd, odd_form, even_form))
        cx, cy = signed
        span = slice(128 * h, 128 * h + 128)
        out[0, :, span] = 1.0 - jnp.abs(cx) - jnp.abs(cy) - 4.0 * MIXING
        out[1, :, span] = MIXING + jnp.maximum(cx, 0.0)
        out[2, :, span] = MIXING + jnp.maximum(-cx, 0.0)
        out[3, :, span] = MIXING + jnp.maximum(cy, 0.0)
        out[4, :, span] = MIXING + jnp.maximum(-cy, 0.0)


def place_kernel(place, got, out, summed, window):
    total = got[:, 0] + got[:, 1] + got[:, 2] + got[:, 3]
    summed[...] = total.reshape(256, 128)
    target = lax.broadcasted_iota(jnp.int32, (64, 128), 0)
    one_hot = jnp.where(target == place[...], 1.0, 0.0).astype(jnp.bfloat16)
    one_hot = jnp.concatenate([one_hot] * 3, axis=1)
    for h in range(2):
        rest = summed[pl.ds(h, 128, stride=2), :]
        parts = []
        for _ in range(3):
            part = rest.astype(jnp.bfloat16)
            parts.append(part)
            rest = rest - part.astype(jnp.float32)
        field = jnp.dot(
            one_hot, jnp.concatenate(parts, axis=0), preferred_element_type=jnp.float32
        ).reshape(4, 16, 128)
        window[h, :, 0:8] = field[:, 8:16]
        window[h, :, 8:24] = field
        window[h, :, 24:32] = field[:, 0:8]
    for txl in range(2):
        for k in range(4):
            if k == 0:
                sources = ((1, txl), (0, txl + 1))
            elif k == 3:
                sources = ((1, txl + 1), (0, txl + 2))
            else:
                sources = ((0, txl + 1), (1, txl + 1))
            for nd in range(4):
                for side, (h, tx) in enumerate(sources):
                    out[txl * 16 + k * 4 + nd, :, 128 * side : 128 * side + 128] = window[
                        h, tx, 6 + 4 * nd : 14 + 4 * nd, :
                    ]


def block_kernel(parity, weight, got, out, done):
    members = got.shape[0]
    chunk = 4
    shape = (chunk, 8, 256)
    lane = lax.broadcasted_iota(jnp.int32, shape, 2)
    left, right = lane % 16 == 0, lane % 16 == 15
    centre, w_low_x, w_high_x, w_low_y, w_high_y = [
        jnp.broadcast_to(weight[i][None], shape) for i in range(5)
    ]
    odd = parity[0] == 1
    for start in range(0, members, chunk):
        field = got[start : start + chunk]
        for _ in range(ITERS):
            low_x = pltpu.roll(field, 16, 2)
            high_x = pltpu.roll(field, 240, 2)
            edge = pltpu.roll(pltpu.roll(field, 241, 2), 1, 1)
            low_y = jnp.where(left, edge, pltpu.roll(field, 1, 2))
            edge = pltpu.roll(pltpu.roll(field, 15, 2), 7, 1)
            high_y = jnp.where(right, edge, pltpu.roll(field, 255, 2))
            field = (
                centre * field
                + w_low_x * low_x
                + w_high_x * high_x
                + w_low_y * low_y
                + w_high_y * high_y
            )
        mine = jnp.where(odd, pltpu.roll(field[:, :, :128], 64, 2), field[:, :, 128:])
        done[8 * start : 8 * (start + chunk), :] = mine.reshape(8 * chunk, 128)
    lane = lax.broadcasted_iota(jnp.int32, (members, 128), 1)
    pieces = [done[pl.ds(2 + a, members, stride=8), :] for a in range(4)]
    for i in range(4):
        line = pieces[0]
        for a in range(4):
            shift = (16 * (a - i)) % 128
            moved = pltpu.roll(pieces[a], shift, 1) if shift else pieces[a]
            line = moved if a == 0 else jnp.where(lane // 16 == a, moved, line)
        out[:, i, :] = line[:, :64]


def shared(value, count):
    return jnp.broadcast_to(value[None], (count, *value.shape))


def ring(count):
    forward = [(i, (i + 1) % count) for i in range(count)]
    return forward, [(b, a) for a, b in forward]


def per_device(
    noise,
    diagonal_tile_blocks,
    left_factors,
    right_factors,
    ranks,
    owner,
    courant_x,
    courant_number_second,
    upwind_x,
    upwind_y,
):
    wide, narrow = lax.axis_size("wide"), lax.axis_size("narrow")
    group = wide // narrow
    devices = wide * narrow
    w, n = lax.axis_index("wide"), lax.axis_index("narrow")
    plane = w // group
    rows, cols = ranks.shape
    rank_max = left_factors.shape[2]
    members = noise.shape[1]
    cells = noise.shape[2]
    f32 = jnp.float32

    swap = [
        ((z * group + r) * narrow + b, (b * group + r) * narrow + z)
        for z in range(narrow)
        for r in range(group)
        for b in range(narrow)
    ]
    planes = [[z * group + r for r in range(group)] for z in range(narrow)]
    slabs = [[z * group * narrow + i for i in range(group * narrow)] for z in range(narrow)]

    with jax.named_scope("noise_gather"):
        swapped = lax.ppermute(noise, BOTH, swap)
        swapped, right_factors, left_factors = lax.optimization_barrier(
            (swapped, right_factors, left_factors)
        )
        columns = lax.all_to_all(
            shared(swapped, group), "wide", 0, 0, axis_index_groups=planes, tiled=True
        ).reshape(group * rows, members, cells)

    with jax.named_scope("factor_fetch"):
        right_near, left_near = pl.pallas_call(
            fetch_kernel,
            out_shape=[pltpu.VMEM(right_factors.shape, right_factors.dtype)] * 2,
            in_specs=specs(pltpu.HBM, pltpu.HBM),
            out_specs=specs(VMEM, VMEM),
            scratch_shapes=[pltpu.SemaphoreType.DMA((2 * rows,))],
            compiler_params=limit(1),
            cost_estimate=pl.CostEstimate(
                flops=0, transcendentals=0, bytes_accessed=4 * right_factors.size
            ),
        )(far(right_factors), far(left_factors))

    with jax.named_scope("diagonal_gather"):
        own_diag = jnp.tril(diagonal_tile_blocks[0])
        diags = [own_diag] + [
            lax.ppermute(own_diag, "narrow", [(i, i ^ j) for i in range(narrow)])
            for j in range(1, narrow)
        ]

    with jax.named_scope("coefficient_halo"):
        signed = [
            jnp.where(flag == 1, value, -value)
            .reshape(rows, 4, 16)
            .transpose(1, 0, 2)
            .reshape(4, 64)
            for value, flag in ((courant_x, upwind_x), (courant_number_second, upwind_y))
        ]
        own = jnp.concatenate(signed, axis=1)
        forward, backward = ring(wide)
        own = jnp.concatenate(
            [lax.ppermute(own, "wide", forward), own, lax.ppermute(own, "wide", backward)], axis=0
        )
        forward, backward = ring(narrow)
        parity = (w % 2)[None].astype(jnp.int32)
        weight = pl.pallas_call(
            weight_kernel,
            out_shape=pltpu.VMEM((5, 8, 256), f32),
            in_specs=specs(SMEM, VMEM, VMEM, VMEM),
            out_specs=pl.BlockSpec(memory_space=VMEM),
            compiler_params=limit(2),
        )(
            parity,
            near(lax.ppermute(own, "narrow", forward)),
            near(own),
            near(lax.ppermute(own, "narrow", backward)),
        )

    with jax.named_scope("factors"):
        info = jnp.concatenate(
            [
                lax.dynamic_slice_in_dim(owner, w * rows, rows) - n * cols,
                n[None].astype(jnp.int32),
            ]
        )
        keep = (
            jnp.arange(rank_max, dtype=jnp.int32)[None, None, :] < ranks[:, :, None]
        ).astype(f32).reshape(rows, cols * rank_max)
        partial_sums = pl.pallas_call(
            factor_kernel,
            out_shape=pltpu.VMEM((devices, 8, 128), f32),
            in_specs=specs(SMEM, *[VMEM] * 8),
            out_specs=pl.BlockSpec(memory_space=VMEM),
            scratch_shapes=[
                pltpu.VMEM((rows, members, cols * rank_max), jnp.bfloat16),
                pltpu.VMEM((members * 8, 128), f32),
                pltpu.VMEM((rows, members, cells), f32),
            ],
            compiler_params=limit(8),
        )(
            info,
            near(keep),
            near(columns),
            right_near,
            left_near,
            *[near(d) for d in diags],
        )

    with jax.named_scope("member_exchange"):
        got = lax.all_to_all(partial_sums, BOTH, 0, 0, tiled=True)
        got, weight = lax.optimization_barrier((got, weight))

    with jax.named_scope("place"):
        bits = [(owner >> b) & 1 for b in range(7)]
        tile_y = bits[0] | bits[2] << 1 | bits[4] << 2 | bits[6] << 3
        tile_x = bits[1] | bits[3] << 1 | bits[5] << 2
        place = (tile_x * 16 + tile_y - 32 * plane.astype(jnp.int32) + 16) & 127
        blocks = pl.pallas_call(
            place_kernel,
            out_shape=pltpu.VMEM((members, 8, 256), f32),
            in_specs=specs(VMEM, VMEM),
            out_specs=pl.BlockSpec(memory_space=VMEM),
            scratch_shapes=[pltpu.VMEM((256, 128), f32), pltpu.VMEM((2, 4, 32, 128), f32)],
            compiler_params=limit(4),
        )(near(place[None]), near(got.reshape(wide, narrow, 8, 128)))

    with jax.named_scope("block_exchange"):
        mine = lax.all_to_all(blocks, BOTH, 0, 0, axis_index_groups=slabs, tiled=True)

    with jax.named_scope("stencil"):
        return pl.pallas_call(
            block_kernel,
            out_shape=jax.ShapeDtypeStruct((members, 4, 64), f32),
            in_specs=specs(SMEM, VMEM, VMEM),
            out_specs=pl.BlockSpec(memory_space=VMEM),
            scratch_shapes=[pltpu.VMEM((members * 8, 128), f32)],
            compiler_params=limit(4),
        )(parity, weight, near(mine))


def solution(mesh):
    placed = (
        P("wide", None, None),
        P(("wide", "narrow"), None, None),
        P("wide", "narrow", None, None),
        P("wide", "narrow", None, None),
        P("wide", "narrow"),
        P(),
        P("wide", "narrow"),
        P("wide", "narrow"),
        P("wide", "narrow"),
        P("wide", "narrow"),
    )
    return jax.shard_map(
        per_device, mesh=mesh, in_specs=placed, out_specs=P(None, "wide", "narrow"), check_vma=False
    )
```

time: 98.1 us -> 96.5 us (0.984)
  waiting for transfers between devices: 31.7 us -> 13.6 us
  blocking collectives: 0 us -> 11.7 us
  local copies, waits for them, and re-layouts: 8.99 us -> 14.5 us
  starting transfers between devices: 38.4 us -> 37.1 us
  Pallas kernels: 15.2 us -> 16.4 us
    all_to_all x3 -> x0, starting transfers between devices: 18.4 us -> none  [the longest x1 9.15 us: per_device(): everyone = lax.all_to_all(shared(own, devices), BOTH, 0, 0, tiled=True)]
    ppermute x0 -> x7, starting transfers between devices: none -> 13.2 us  [the longest x1 8.01 us: per_device(): lax.ppermute(own, 'wide', backward)]
    all_to_all x0 -> x1, blocking collectives: none -> 11.7 us  [per_device(): lax.all_to_all(blocks, BOTH, 0, 0, axis_index_groups=slabs, tiled=True)]
    all_to_all x1, waiting for transfers between devices: 11.4 us -> 0.01 us  [per_device(): got = lax.all_to_all(partial_sums, BOTH, 0, 0, tiled=True)]
    ppermute x0 -> x7, waiting for transfers between devices: none -> 11.2 us  [the longest x1 7.42 us: per_device(): lax.ppermute(own, 'wide', forward)]
    all_to_all x3 -> x0, waiting for transfers between devices: 9.62 us -> none  [the longest x1 7.42 us: per_device(): lax.all_to_all(blocks, BOTH, 0, 0, axis_index_groups=slabs, tiled=True)]
    all_to_all x1, waiting for transfers between devices: 8.45 us -> 0.01 us  [per_device(): lax.all_to_all(shared(swapped, group), 'wide', 0, 0, axis_index_groups=pl...]
    unnamed x12 -> x17, local copies, waits for them, and re-layouts: 5.49 us -> 13.3 us
  transfers between devices with their start and end apart: 6 -> 10, of which waited for: 5 -> 5; matrix products, arithmetic and copies ran while one was open for 3% -> 3% of each run, Pallas kernels for 11% -> 6%
where the time goes in v2:
time: 96.5 us; the launch traced here: 96.1 us
  starting transfers between devices  37.1 us (38%)
  Pallas kernels  16.4 us (17%)
  local copies, waits for them, and re-layouts  14.5 us (15%)
  waiting for transfers between devices  13.6 us (14%)
  blocking collectives  11.7 us (12%)
  other arithmetic  2.68 us (3%)
    all_to_all x1, starting transfers between devices, per_device(): got = lax.all_to_all(partial_sums, BOTH, 0, 0, tiled=True)  13.5 us
    unnamed x17, local copies, waits for them, and re-layouts  13.3 us
    all_to_all x1, blocking collectives, per_device(): lax.all_to_all(blocks, BOTH, 0, 0, axis_index_groups=slabs, tiled=True)  11.7 us
    ppermute x1, starting transfers between devices, per_device(): lax.ppermute(own, 'wide', backward)  8.01 us
    ppermute x1, waiting for transfers between devices, per_device(): lax.ppermute(own, 'wide', forward)  7.42 us
    all_to_all x1, starting transfers between devices, per_device(): lax.all_to_all(shared(swapped, group), 'wide', 0, 0, axis_index_groups=pl...  6.71 us
    pallas_call x1, Pallas kernels, per_device(): pl.pallas_call(fetch_kernel, out_shape=[pltpu.VMEM(right_factors.shape, r...  5.92 us
    pallas_call x1, Pallas kernels, per_device(): pl.pallas_call(factor_kernel, out_shape=pltpu.VMEM((devices, 8, 128), f32...  5.64 us
  transfers between devices with their start and end apart: 10, of which 5 were waited for; matrix products, arithmetic and copies ran while one was open for 3% of the time, Pallas kernels for 6%

profile of v2, /device:TPU:1, one launch (start us, length us, event | category | flops | bytes accessed | tf_op | source)
XLA Modules:
  0.0 96.1 jit_solution(15953436875286305587)
XLA Ops:
  0.0 0.9 fusion.d0
  0.9 1.5 %collective-permute-start.1 = (bf16[256,256]{1,0:T(8,128)(2,1)S(1)}, bf16[256,256]{1,0:T(8,128)(2,1)S(1)}, u32[]{:S(2)}, u32[]{:S(2)}) collective-permute-start(bf16[256,256]{1,0:T(8,128)(2,1)S(1)} %fusion.d0), channel_id=1, source_target_pairs={{0,1},{1,0},{2,3},{3,2},{4,5},{5,4},{6,7},{7,6},{8,9},{9,8},{10,11... | collective-permute-start | bytes 393224 | tf_op jit(solution)/shard_map/diagonal_gather/ppermute | solution.py:255
  2.5 1.3 %collective-permute-start.2 = (bf16[256,256]{1,0:T(8,128)(2,1)S(1)}, bf16[256,256]{1,0:T(8,128)(2,1)S(1)}, u32[]{:S(2)}, u32[]{:S(2)}) collective-permute-start(bf16[256,256]{1,0:T(8,128)(2,1)S(1)} %fusion.d0), channel_id=1, source_target_pairs={{0,2},{1,3},{2,0},{3,1},{4,6},{5,7},{6,4},{7,5},{8,10},{9,11},{10,... | collective-permute-start | bytes 393224 | tf_op jit(solution)/shard_map/diagonal_gather/ppermute | solution.py:255
  4.2 3.7 %collective-permute-start = (bf16[4,32,256]{2,1,0:T(8,128)(2,1)}, bf16[4,32,256]{2,1,0:T(8,128)(2,1)S(1)}, u32[]{:S(2)}, u32[]{:S(2)}) collective-permute-start(bf16[4,32,256]{2,1,0:T(8,128)(2,1)} %param.10), channel_id=1, source_target_pairs={{0,0},{1,32},{2,64},{3,96},{4,4},{5,36},{6,68},{7,100},{8,8},{9,40... | collective-permute-start | bytes 196616 | tf_op jit(solution)/shard_map/noise_gather/ppermute | solution.py:231
  7.9 2.3 %collective-permute-done = bf16[4,32,256]{2,1,0:T(8,128)(2,1)S(1)} collective-permute-done((bf16[4,32,256]{2,1,0:T(8,128)(2,1)}, bf16[4,32,256]{2,1,0:T(8,128)(2,1)S(1)}, u32[]{:S(2)}, u32[]{:S(2)}) %collective-permute-start) | collective-permute-done | bytes 65568 | tf_op jit(solution)/shard_map/noise_gather/ppermute | solution.py:231
  10.3 0.9 broadcast_in_dim.23
  11.1 6.7 %all-to-all-start = ((bf16[8,4,32,256]{3,2,1,0:T(8,128)(2,1)}), bf16[8,4,32,256]{3,2,1,0:T(8,128)(2,1)S(1)}, u32[]{:S(2)}, u32[]{:S(2)}) async-start(bf16[8,4,32,256]{3,2,1,0:T(8,128)(2,1)} %broadcast_in_dim.23), calls=%async_computation | async-start | bytes 1048576 | tf_op jit(solution)/shard_map/noise_gather/all_to_all | solution.py:235
  17.9 0.7 negate_select_fusion
  18.6 0.7 dynamic-slice_subtract_fusion
  19.4 5.9 %factor_fetch.1 = (bf16[4,32,128,256]{3,2,1,0:T(8,128)(2,1)S(1)}, bf16[4,32,128,256]{3,2,1,0:T(8,128)(2,1)S(1)}) custom-call(bf16[4,32,128,256]{3,2,1,0:T(8,128)(2,1)} %right, bf16[4,32,128,256]{3,2,1,0:T(8,128)(2,1)} %left), custom_call_target="tpu_custom_call" | custom-call | bytes 16777216 | tf_op jit(solution)/shard_map/factor_fetch/pallas_call | solution.py:240
  25.4 3.2 %copy-done.1 = bf16[4,32,128,256]{3,2,1,0:T(8,128)(2,1)} copy-done((bf16[4,32,128,256]{3,2,1,0:T(8,128)(2,1)}, bf16[4,32,128,256]{3,2,1,0:T(8,128)(2,1)S(1)}, u32[]{:S(2)}) %copy-start.1) | copy-done | bytes 8388632
  28.6 3.2 %copy-done.3 = bf16[4,32,128,256]{3,2,1,0:T(8,128)(2,1)} copy-done((bf16[4,32,128,256]{3,2,1,0:T(8,128)(2,1)}, bf16[4,32,128,256]{3,2,1,0:T(8,128)(2,1)S(1)}, u32[]{:S(2)}) %copy-start.3) | copy-done | bytes 8388632
  31.8 3.4 %copy-done.2 = bf16[4,32,128,256]{3,2,1,0:T(8,128)(2,1)S(1)} copy-done((bf16[4,32,128,256]{3,2,1,0:T(8,128)(2,1)S(1)}, bf16[4,32,128,256]{3,2,1,0:T(8,128)(2,1)}, u32[]{:S(2)}) %copy-start.2) | copy-done | bytes 8388632
  35.2 3.4 %copy-done.4 = bf16[4,32,128,256]{3,2,1,0:T(8,128)(2,1)S(1)} copy-done((bf16[4,32,128,256]{3,2,1,0:T(8,128)(2,1)S(1)}, bf16[4,32,128,256]{3,2,1,0:T(8,128)(2,1)}, u32[]{:S(2)}) %copy-start.4) | copy-done | bytes 8388632
  38.6 5.6 %factors.1 = f32[128,8,128]{2,1,0:T(8,128)} custom-call(s32[5]{0:T(128)S(1)} %pad_add_fusion.info, f32[4,4096]{1,0:T(4,128)S(1)} %fusion.1.keep, bf16[32,32,256]{2,1,0:T(8,128)(2,1)S(1)} %bitcast.22, bf16[4,32,128,256]{3,2,1,0:T(8,128)(2,1)S(1)} %copy-done.2, bf16[4,32,128,256]{3,2,1,0:T(8,128)(2,1)S(1)} %copy-done.4, bf16[256,256]{1,0:T(8,128)(2,1)S(1)} %fusion.d0, ...), custom_call_target="tpu_custom_call" | custom-call | tf_op jit(solution)/shard_map/factors/pallas_call | solution.py:297
  44.2 13.5 %all-to-all-start.1 = ((f32[128,8,128]{2,1,0:T(8,128)}), f32[128,8,128]{2,1,0:T(8,128)S(1)}, u32[]{:S(2)}, u32[]{:S(2)}) async-start(f32[128,8,128]{2,1,0:T(8,128)} %factors.1), calls=%async_computation.1 | async-start | bytes 1048576 | tf_op jit(solution)/shard_map/member_exchange/all_to_all | solution.py:318
  58.2 8.0 %collective-permute-start.5 = (f32[4,128]{1,0:T(4,128)S(1)}, f32[4,128]{1,0:T(4,128)S(1)}, u32[]{:S(2)}, u32[]{:S(2)}) collective-permute-start(f32[4,128]{1,0:T(4,128)S(1)} %pad_maximum_fusion.1), channel_id=1, source_target_pairs={{4,0},{8,4},{12,8},{16,12},{20,16},{24,20},{28,24},{32,28},{36,32}... | collective-permute-start | bytes 6152 | tf_op jit(solution)/shard_map/coefficient_halo/ppermute | solution.py:270
  66.2 0.7 collective-permute-done.5
  67.0 7.4 %collective-permute-done.4 = f32[4,128]{1,0:T(4,128)S(1)} collective-permute-done((f32[4,128]{1,0:T(4,128)S(1)}, f32[4,128]{1,0:T(4,128)S(1)}, u32[]{:S(2)}, u32[]{:S(2)}) %collective-permute-start.4) | collective-permute-done | bytes 2080 | tf_op jit(solution)/shard_map/coefficient_halo/ppermute | solution.py:270
  74.5 2.0 %collective-permute-start.6 = (f32[12,128]{1,0:T(8,128)S(1)}, f32[12,128]{1,0:T(8,128)S(1)}, u32[]{:S(2)}, u32[]{:S(2)}) collective-permute-start(f32[12,128]{1,0:T(8,128)S(1)} %pad_maximum_fusion.own), channel_id=1, source_target_pairs={{0,1},{1,2},{2,3},{3,0},{4,5},{5,6},{6,7},{7,4},{8,9},{9,10},{10,1... | collective-permute-start | bytes 18440 | tf_op jit(solution)/shard_map/coefficient_halo/ppermute | solution.py:282
  76.5 0.8 collective-permute-done.6.low
  77.3 2.3 %collective-permute-done.7.high = f32[12,128]{1,0:T(8,128)S(1)} collective-permute-done((f32[12,128]{1,0:T(8,128)S(1)}, f32[12,128]{1,0:T(8,128)S(1)}, u32[]{:S(2)}, u32[]{:S(2)}) %collective-permute-start.7) | collective-permute-done | bytes 6176 | tf_op jit(solution)/shard_map/coefficient_halo/ppermute | solution.py:284
  79.8 11.7 %all_to_all.15.got = f32[32,8,256]{2,1,0:T(8,128)S(1)} all-to-all(f32[32,8,256]{2,1,0:T(8,128)S(1)} %place.1), channel_id=1, replica_groups={{0,1,2,3,4,5,6,7,8,9,10,11,12,13,14,15,16,17,18,19,20,21,22,23,24,25,26..., dimensions={0} | all-to-all | bytes 524288 | tf_op jit(solution)/shard_map/block_exchange/all_to_all | solution.py:336
  91.5 4.5 %stencil.1 = f32[32,4,64]{2,1,0:T(4,128)} custom-call(s32[1]{0:T(128)} %bitcast.parity, f32[5,8,256]{2,1,0:T(8,128)S(1)} %coefficient_halo.1.weight, f32[32,8,256]{2,1,0:T(8,128)S(1)} %all_to_all.15.got), custom_call_target="tpu_custom_call" | custom-call | tf_op jit(solution)/shard_map/stencil/pallas_call | solution.py:339
  (36 shorter events, 1.5 us)
Async XLA Ops:
  0.0 7.8 %copy-start = (s32[4,32]{1,0:T(4,128)S(1)}, s32[4,32]{1,0:T(4,128)}, u32[]{:S(2)}) copy-start(s32[4,32]{1,0:T(4,128)} %param.14) | copy-start | bytes 1540
  0.9 30.9 %collective-permute-start.1 = (bf16[256,256]{1,0:T(8,128)(2,1)S(1)}, bf16[256,256]{1,0:T(8,128)(2,1)S(1)}, u32[]{:S(2)}, u32[]{:S(2)}) collective-permute-start(bf16[256,256]{1,0:T(8,128)(2,1)S(1)} %fusion.d0), channel_id=1, source_target_pairs={{0,1},{1,0},{2,3},{3,2},{4,5},{5,4},{6,7},{7,6},{8,9},{9,8},{10,11... | collective-permute-start | bytes 393224 | tf_op jit(solution)/shard_map/diagonal_gather/ppermute | solution.py:255
  2.5 29.4 %collective-permute-start.2 = (bf16[256,256]{1,0:T(8,128)(2,1)S(1)}, bf16[256,256]{1,0:T(8,128)(2,1)S(1)}, u32[]{:S(2)}, u32[]{:S(2)}) collective-permute-start(bf16[256,256]{1,0:T(8,128)(2,1)S(1)} %fusion.d0), channel_id=1, source_target_pairs={{0,2},{1,3},{2,0},{3,1},{4,6},{5,7},{6,4},{7,5},{8,10},{9,11},{10,... | collective-permute-start | bytes 393224 | tf_op jit(solution)/shard_map/diagonal_gather/ppermute | solution.py:255
  3.8 28.1 %collective-permute-start.3 = (bf16[256,256]{1,0:T(8,128)(2,1)S(1)}, bf16[256,256]{1,0:T(8,128)(2,1)S(1)}, u32[]{:S(2)}, u32[]{:S(2)}) collective-permute-start(bf16[256,256]{1,0:T(8,128)(2,1)S(1)} %fusion.d0), channel_id=1, source_target_pairs={{0,3},{1,2},{2,1},{3,0},{4,7},{5,6},{6,5},{7,4},{8,11},{9,10},{10,... | collective-permute-start | bytes 393224 | tf_op jit(solution)/shard_map/diagonal_gather/ppermute | solution.py:255
  4.2 6.1 %collective-permute-start = (bf16[4,32,256]{2,1,0:T(8,128)(2,1)}, bf16[4,32,256]{2,1,0:T(8,128)(2,1)S(1)}, u32[]{:S(2)}, u32[]{:S(2)}) collective-permute-start(bf16[4,32,256]{2,1,0:T(8,128)(2,1)} %param.10), channel_id=1, source_target_pairs={{0,0},{1,32},{2,64},{3,96},{4,4},{5,36},{6,68},{7,100},{8,8},{9,40... | collective-permute-start | bytes 196616 | tf_op jit(solution)/shard_map/noise_gather/ppermute | solution.py:231
  11.1 20.7 %all-to-all-start = ((bf16[8,4,32,256]{3,2,1,0:T(8,128)(2,1)}), bf16[8,4,32,256]{3,2,1,0:T(8,128)(2,1)S(1)}, u32[]{:S(2)}, u32[]{:S(2)}) async-start(bf16[8,4,32,256]{3,2,1,0:T(8,128)(2,1)} %broadcast_in_dim.23), calls=%async_computation | async-start | bytes 1048576 | tf_op jit(solution)/shard_map/noise_gather/all_to_all | solution.py:235
  25.4 3.2 %copy-start.1 = (bf16[4,32,128,256]{3,2,1,0:T(8,128)(2,1)}, bf16[4,32,128,256]{3,2,1,0:T(8,128)(2,1)S(1)}, u32[]{:S(2)}) copy-start(bf16[4,32,128,256]{3,2,1,0:T(8,128)(2,1)S(1)} %get-tuple-element.15.right) | copy-start | bytes 25165828
  28.6 3.2 %copy-start.3 = (bf16[4,32,128,256]{3,2,1,0:T(8,128)(2,1)}, bf16[4,32,128,256]{3,2,1,0:T(8,128)(2,1)S(1)}, u32[]{:S(2)}) copy-start(bf16[4,32,128,256]{3,2,1,0:T(8,128)(2,1)S(1)} %get-tuple-element.16.left) | copy-start | bytes 25165828
  31.8 3.4 %copy-start.2 = (bf16[4,32,128,256]{3,2,1,0:T(8,128)(2,1)S(1)}, bf16[4,32,128,256]{3,2,1,0:T(8,128)(2,1)}, u32[]{:S(2)}) copy-start(bf16[4,32,128,256]{3,2,1,0:T(8,128)(2,1)} %copy-done.1) | copy-start | bytes 25165828
  35.2 3.4 %copy-start.4 = (bf16[4,32,128,256]{3,2,1,0:T(8,128)(2,1)S(1)}, bf16[4,32,128,256]{3,2,1,0:T(8,128)(2,1)}, u32[]{:S(2)}) copy-start(bf16[4,32,128,256]{3,2,1,0:T(8,128)(2,1)} %copy-done.3) | copy-start | bytes 25165828
  38.6 19.2 %copy-start.5 = (f32[4,64]{1,0:T(4,128)S(1)}, f32[4,64]{1,0:T(4,128)}, u32[]{:S(2)}) copy-start(f32[4,64]{1,0:T(4,128)} %param.16) | copy-start | bytes 3076
  38.6 19.2 %copy-start.6 = (s32[4,64]{1,0:T(4,128)S(1)}, s32[4,64]{1,0:T(4,128)}, u32[]{:S(2)}) copy-start(s32[4,64]{1,0:T(4,128)} %param.18) | copy-start | bytes 3076
  38.6 37.9 %copy-start.7 = (s32[128]{0:T(128)S(1)}, s32[128]{0:T(128)}, u32[]{:S(2)}) copy-start(s32[128]{0:T(128)} %param.15) | copy-start | bytes 1540
  44.2 35.4 %all-to-all-start.1 = ((f32[128,8,128]{2,1,0:T(8,128)}), f32[128,8,128]{2,1,0:T(8,128)S(1)}, u32[]{:S(2)}, u32[]{:S(2)}) async-start(f32[128,8,128]{2,1,0:T(8,128)} %factors.1), calls=%async_computation.1 | async-start | bytes 1048576 | tf_op jit(solution)/shard_map/member_exchange/all_to_all | solution.py:318
  58.2 8.7 %collective-permute-start.5 = (f32[4,128]{1,0:T(4,128)S(1)}, f32[4,128]{1,0:T(4,128)S(1)}, u32[]{:S(2)}, u32[]{:S(2)}) collective-permute-start(f32[4,128]{1,0:T(4,128)S(1)} %pad_maximum_fusion.1), channel_id=1, source_target_pairs={{4,0},{8,4},{12,8},{16,12},{20,16},{24,20},{28,24},{32,28},{36,32}... | collective-permute-start | bytes 6152 | tf_op jit(solution)/shard_map/coefficient_halo/ppermute | solution.py:270
  66.2 8.2 %collective-permute-start.4 = (f32[4,128]{1,0:T(4,128)S(1)}, f32[4,128]{1,0:T(4,128)S(1)}, u32[]{:S(2)}, u32[]{:S(2)}) collective-permute-start(f32[4,128]{1,0:T(4,128)S(1)} %pad_maximum_fusion.1), channel_id=1, source_target_pairs={{0,4},{4,8},{8,12},{12,16},{16,20},{20,24},{24,28},{28,32},{32,36}... | collective-permute-start | bytes 6152 | tf_op jit(solution)/shard_map/coefficient_halo/ppermute | solution.py:270
  74.5 2.8 %collective-permute-start.6 = (f32[12,128]{1,0:T(8,128)S(1)}, f32[12,128]{1,0:T(8,128)S(1)}, u32[]{:S(2)}, u32[]{:S(2)}) collective-permute-start(f32[12,128]{1,0:T(8,128)S(1)} %pad_maximum_fusion.own), channel_id=1, source_target_pairs={{0,1},{1,2},{2,3},{3,0},{4,5},{5,6},{6,7},{7,4},{8,9},{9,10},{10,1... | collective-permute-start | bytes 18440 | tf_op jit(solution)/shard_map/coefficient_halo/ppermute | solution.py:282
  76.5 3.1 %collective-permute-start.7 = (f32[12,128]{1,0:T(8,128)S(1)}, f32[12,128]{1,0:T(8,128)S(1)}, u32[]{:S(2)}, u32[]{:S(2)}) collective-permute-start(f32[12,128]{1,0:T(8,128)S(1)} %pad_maximum_fusion.own), channel_id=1, source_target_pairs={{1,0},{2,1},{3,2},{0,3},{5,4},{6,5},{7,6},{4,7},{9,8},{10,9},{11,1... | collective-permute-start | bytes 18440 | tf_op jit(solution)/shard_map/coefficient_halo/ppermute | solution.py:284

commit v3 on v2

--- a/solution.py
+++ b/solution.py
@@ -14,6 +14,7 @@
 VMEM = pltpu.VMEM
 SMEM = pltpu.SMEM
 MIB = 1 << 20
+CHUNKS = 8
 
 
 def specs(*spaces):
@@ -32,9 +33,41 @@
     return pltpu.CompilerParams(vmem_limit_bytes=mib * MIB)
 
 
-def factor_kernel(info, keep, noise, right, left, d0, d1, d2, d3, out, coeff, turned, own):
+def factor_kernel(
+    info,
+    keep,
+    noise,
+    right_far,
+    left_far,
+    d0,
+    d1,
+    d2,
+    d3,
+    out,
+    coeff,
+    turned,
+    own,
+    right,
+    left,
+    right_done,
+    left_done,
+):
     rows, cols, rank_max, cells = right.shape
     members = noise.shape[1]
+    each = cols // CHUNKS
+    right_copies = [
+        pltpu.make_async_copy(
+            right_far.at[:, i * each : (i + 1) * each],
+            right.at[:, i * each : (i + 1) * each],
+            right_done.at[i],
+        )
+        for i in range(CHUNKS)
+    ]
+    left_copies = [
+        pltpu.make_async_copy(left_far.at[p], left.at[p], left_done.at[p]) for p in range(rows)
+    ]
+    for copy in right_copies + left_copies:
+        copy.start()
     for j, diag in enumerate((d0, d1, d2, d3)):
         row = info[rows] ^ j
         local = info[row]
@@ -45,6 +78,8 @@
         )
         own[row] = jnp.where(held, term, 0.0)
     for c in range(cols):
+        if c % each == 0:
+            right_copies[c // each].wait()
         span = slice(c * rank_max, (c + 1) * rank_max)
         block = right[:, c].reshape(rows * rank_max, cells)
         product = lax.dot_general(
@@ -55,6 +90,7 @@
             piece = jnp.where(keep[p : p + 1, span] > 0, piece, 0.0)
             coeff[p, :, span] = piece.astype(jnp.bfloat16)
     for p in range(rows):
+        left_copies[p].wait()
         total = own[p] + jnp.dot(
             coeff[p],
             left[p].reshape(cols * rank_max, cells),
@@ -68,18 +104,6 @@
     for d in range(out.shape[0]):
         member = d % members
         out[d] = turned[8 * member : 8 * member + 8, :]
-
-
-def fetch_kernel(right, left, right_out, left_out, done):
-    parts = 4
-    copies = []
-    for i, (source, target) in enumerate(((right, right_out), (left, left_out))):
-        for j in range(parts):
-            copies.append(pltpu.make_async_copy(source.at[j], target.at[j], done.at[parts * i + j]))
-    for copy in copies:
-        copy.start()
-    for copy in copies:
-        copy.wait()
 
 
 def weight_kernel(parity, low, own, high, out):
@@ -147,25 +171,23 @@
                     ]
 
 
-def block_kernel(parity, weight, got, out, done):
+def block_kernel(parity, weight, got, out, ping, pong, done):
     members = got.shape[0]
     chunk = 4
     shape = (chunk, 8, 256)
     lane = lax.broadcasted_iota(jnp.int32, shape, 2)
     left, right = lane % 16 == 0, lane % 16 == 15
-    centre, w_low_x, w_high_x, w_low_y, w_high_y = [
-        jnp.broadcast_to(weight[i][None], shape) for i in range(5)
-    ]
+    centre, w_low_x, w_high_x, w_low_y, w_high_y = [weight[i][None] for i in range(5)]
     odd = parity[0] == 1
-    for start in range(0, members, chunk):
-        field = got[start : start + chunk]
-        for _ in range(ITERS):
+    source = got
+    for step in range(ITERS):
+        target = (ping, pong)[step % 2]
+        for start in range(0, members, chunk):
+            field = source[start : start + chunk]
             low_x = pltpu.roll(field, 16, 2)
             high_x = pltpu.roll(field, 240, 2)
-            edge = pltpu.roll(pltpu.roll(field, 241, 2), 1, 1)
-            low_y = jnp.where(left, edge, pltpu.roll(field, 1, 2))
-            edge = pltpu.roll(pltpu.roll(field, 15, 2), 7, 1)
-            high_y = jnp.where(right, edge, pltpu.roll(field, 255, 2))
+            low_y = pltpu.roll(jnp.where(right, pltpu.roll(high_x, 1, 1), field), 1, 2)
+            high_y = pltpu.roll(jnp.where(left, pltpu.roll(low_x, 7, 1), field), 255, 2)
             field = (
                 centre * field
                 + w_low_x * low_x
@@ -173,8 +195,12 @@
                 + w_low_y * low_y
                 + w_high_y * high_y
             )
-        mine = jnp.where(odd, pltpu.roll(field[:, :, :128], 64, 2), field[:, :, 128:])
-        done[8 * start : 8 * (start + chunk), :] = mine.reshape(8 * chunk, 128)
+            if step < ITERS - 1:
+                target[start : start + chunk] = field
+            else:
+                mine = jnp.where(odd, pltpu.roll(field[:, :, :128], 64, 2), field[:, :, 128:])
+                done[8 * start : 8 * (start + chunk), :] = mine.reshape(8 * chunk, 128)
+        source = target
     lane = lax.broadcasted_iota(jnp.int32, (members, 128), 1)
     pieces = [done[pl.ds(2 + a, members, stride=8), :] for a in range(4)]
     for i in range(4):
@@ -229,28 +255,13 @@
 
     with jax.named_scope("noise_gather"):
         swapped = lax.ppermute(noise, BOTH, swap)
-        swapped, right_factors, left_factors = lax.optimization_barrier(
-            (swapped, right_factors, left_factors)
-        )
+        sending, own_diag = lax.optimization_barrier((shared(swapped, group), diagonal_tile_blocks[0]))
         columns = lax.all_to_all(
-            shared(swapped, group), "wide", 0, 0, axis_index_groups=planes, tiled=True
+            sending, "wide", 0, 0, axis_index_groups=planes, tiled=True
         ).reshape(group * rows, members, cells)
 
-    with jax.named_scope("factor_fetch"):
-        right_near, left_near = pl.pallas_call(
-            fetch_kernel,
-            out_shape=[pltpu.VMEM(right_factors.shape, right_factors.dtype)] * 2,
-            in_specs=specs(pltpu.HBM, pltpu.HBM),
-            out_specs=specs(VMEM, VMEM),
-            scratch_shapes=[pltpu.SemaphoreType.DMA((2 * rows,))],
-            compiler_params=limit(1),
-            cost_estimate=pl.CostEstimate(
-                flops=0, transcendentals=0, bytes_accessed=4 * right_factors.size
-            ),
-        )(far(right_factors), far(left_factors))
-
     with jax.named_scope("diagonal_gather"):
-        own_diag = jnp.tril(diagonal_tile_blocks[0])
+        own_diag = jnp.tril(own_diag)
         diags = [own_diag] + [
             lax.ppermute(own_diag, "narrow", [(i, i ^ j) for i in range(narrow)])
             for j in range(1, narrow)
@@ -297,26 +308,29 @@
         partial_sums = pl.pallas_call(
             factor_kernel,
             out_shape=pltpu.VMEM((devices, 8, 128), f32),
-            in_specs=specs(SMEM, *[VMEM] * 8),
+            in_specs=specs(SMEM, VMEM, VMEM, pltpu.HBM, pltpu.HBM, *[VMEM] * 4),
             out_specs=pl.BlockSpec(memory_space=VMEM),
             scratch_shapes=[
                 pltpu.VMEM((rows, members, cols * rank_max), jnp.bfloat16),
                 pltpu.VMEM((members * 8, 128), f32),
                 pltpu.VMEM((rows, members, cells), f32),
+                pltpu.VMEM(right_factors.shape, right_factors.dtype),
+                pltpu.VMEM(left_factors.shape, left_factors.dtype),
+                pltpu.SemaphoreType.DMA((CHUNKS,)),
+                pltpu.SemaphoreType.DMA((rows,)),
             ],
-            compiler_params=limit(8),
+            compiler_params=limit(24),
         )(
             info,
             near(keep),
             near(columns),
-            right_near,
-            left_near,
+            far(right_factors),
+            far(left_factors),
             *[near(d) for d in diags],
         )
 
     with jax.named_scope("member_exchange"):
         got = lax.all_to_all(partial_sums, BOTH, 0, 0, tiled=True)
-        got, weight = lax.optimization_barrier((got, weight))
 
     with jax.named_scope("place"):
         bits = [(owner >> b) & 1 for b in range(7)]
@@ -341,7 +355,11 @@
             out_shape=jax.ShapeDtypeStruct((members, 4, 64), f32),
             in_specs=specs(SMEM, VMEM, VMEM),
             out_specs=pl.BlockSpec(memory_space=VMEM),
-            scratch_shapes=[pltpu.VMEM((members * 8, 128), f32)],
+            scratch_shapes=[
+                pltpu.VMEM((members, 8, 256), f32),
+                pltpu.VMEM((members, 8, 256), f32),
+                pltpu.VMEM((members * 8, 128), f32),
+            ],
             compiler_params=limit(4),
         )(parity, weight, near(mine))
 

time: 96.5 us -> 87.7 us (0.909)
  waiting for transfers between devices: 13.6 us -> 29.5 us
  local copies, waits for them, and re-layouts: 14.5 us -> 1.31 us
  blocking collectives: 11.7 us -> 0 us
  starting transfers between devices: 37.1 us -> 39.3 us
  Pallas kernels: 16.4 us -> 15.1 us
    all_to_all x1, waiting for transfers between devices: 0.01 us -> 13.7 us  [per_device(): got = lax.all_to_all(partial_sums, BOTH, 0, 0, tiled=True)]
    unnamed x17 -> x13, local copies, waits for them, and re-layouts: 13.3 us -> 0.1 us
    all_to_all x1 -> x0, blocking collectives: 11.7 us -> none  [per_device(): lax.all_to_all(blocks, BOTH, 0, 0, axis_index_groups=slabs, tiled=True)]
    ppermute x3, waiting for transfers between devices: 0.01 us -> 9.62 us  [per_device(): lax.ppermute(own_diag, 'narrow', [(i, i ^ j) for i in range(narrow)])]
    ppermute x1, waiting for transfers between devices: 7.42 us -> 1.05 us  [per_device(): lax.ppermute(own, 'wide', forward)]
    pallas_call x1 -> x0, Pallas kernels: 5.92 us -> none  [per_device(): pl.pallas_call(fetch_kernel, out_shape=[pltpu.VMEM(right_factors.shape, r...]
    all_to_all x1, starting transfers between devices: 13.5 us -> 8.69 us  [per_device(): got = lax.all_to_all(partial_sums, BOTH, 0, 0, tiled=True)]
    all_to_all x1 -> x2, starting transfers between devices: 6.71 us -> 11 us  [the longest x1 6.65 us: per_device(): lax.all_to_all(sending, 'wide', 0, 0, axis_index_groups=planes, tiled=True)]
  transfers between devices with their start and end apart: 10 -> 11, of which waited for: 5 -> 7; matrix products, arithmetic and copies ran while one was open for 3% -> 3% of each run, Pallas kernels for 6% -> 0%
where the time goes in v3:
time: 87.7 us; the launch traced here: 87.3 us
  starting transfers between devices  39.3 us (45%)
  waiting for transfers between devices  29.5 us (34%)
  Pallas kernels  15.1 us (17%)
  other arithmetic  1.97 us (2%)
  local copies, waits for them, and re-layouts  1.31 us (1%)
    all_to_all x1, waiting for transfers between devices, per_device(): got = lax.all_to_all(partial_sums, BOTH, 0, 0, tiled=True)  13.7 us
    pallas_call x1, Pallas kernels, per_device(): pl.pallas_call(factor_kernel, out_shape=pltpu.VMEM((devices, 8, 128), f32...  9.85 us
    ppermute x3, waiting for transfers between devices, per_device(): lax.ppermute(own_diag, 'narrow', [(i, i ^ j) for i in range(narrow)])  9.62 us
    all_to_all x1, starting transfers between devices, per_device(): got = lax.all_to_all(partial_sums, BOTH, 0, 0, tiled=True)  8.69 us
    all_to_all x1, starting transfers between devices, per_device(): lax.all_to_all(sending, 'wide', 0, 0, axis_index_groups=planes, tiled=True)  6.65 us
    ppermute x1, starting transfers between devices, per_device(): swapped = lax.ppermute(noise, BOTH, swap)  5.05 us
    ppermute x3, starting transfers between devices, per_device(): lax.ppermute(own_diag, 'narrow', [(i, i ^ j) for i in range(narrow)])  4.61 us
    all_to_all x1, starting transfers between devices, per_device(): lax.all_to_all(blocks, BOTH, 0, 0, axis_index_groups=slabs, tiled=True)  4.39 us
  transfers between devices with their start and end apart: 11, of which 7 were waited for; matrix products, arithmetic and copies ran while one was open for 3% of the time, Pallas kernels for 0%

profile of v3, /device:TPU:1, one launch (start us, length us, event | category | flops | bytes accessed | tf_op | source)
XLA Modules:
  0.0 87.3 jit_solution(17336787306353030493)
XLA Ops:
  0.0 5.1 %collective-permute-start.4 = (bf16[4,32,256]{2,1,0:T(8,128)(2,1)}, bf16[4,32,256]{2,1,0:T(8,128)(2,1)S(1)}, u32[]{:S(2)}, u32[]{:S(2)}) collective-permute-start(bf16[4,32,256]{2,1,0:T(8,128)(2,1)} %param.10), channel_id=1, source_target_pairs={{0,0},{1,32},{2,64},{3,96},{4,4},{5,36},{6,68},{7,100},{8,8},{9,40... | collective-permute-start | bytes 196616 | tf_op jit(solution)/shard_map/noise_gather/ppermute | solution.py:257
  5.2 2.0 %collective-permute-done.4 = bf16[4,32,256]{2,1,0:T(8,128)(2,1)S(1)} collective-permute-done((bf16[4,32,256]{2,1,0:T(8,128)(2,1)}, bf16[4,32,256]{2,1,0:T(8,128)(2,1)S(1)}, u32[]{:S(2)}, u32[]{:S(2)}) %collective-permute-start.4) | collective-permute-done | bytes 65568 | tf_op jit(solution)/shard_map/noise_gather/ppermute | solution.py:257
  7.2 0.9 broadcast_in_dim.24
  8.1 6.7 %all-to-all-start = ((bf16[8,4,32,256]{3,2,1,0:T(8,128)(2,1)}), bf16[8,4,32,256]{3,2,1,0:T(8,128)(2,1)S(1)}, u32[]{:S(2)}, u32[]{:S(2)}) async-start(bf16[8,4,32,256]{3,2,1,0:T(8,128)(2,1)} %broadcast_in_dim.24), calls=%async_computation | async-start | bytes 1048576 | tf_op jit(solution)/shard_map/noise_gather/all_to_all | solution.py:259
  14.8 0.9 %fusion.d0 = bf16[256,256]{1,0:T(8,128)(2,1)S(1)} fusion(bf16[256,256]{1,0:T(8,128)(2,1)} %bitcast.23), kind=kLoop, calls=%fused_computation.1 | loop fusion | flops 131072 | bytes 262144 | tf_op jit(solution)/shard_map/diagonal_gather/jit(tril)/select_n | solution.py:264
  15.7 0.1 collective-permute-start.5
  15.8 4.5 %collective-permute-start.6 = (bf16[256,256]{1,0:T(8,128)(2,1)S(1)}, bf16[256,256]{1,0:T(8,128)(2,1)S(1)}, u32[]{:S(2)}, u32[]{:S(2)}) collective-permute-start(bf16[256,256]{1,0:T(8,128)(2,1)S(1)} %fusion.d0), channel_id=1, source_target_pairs={{0,2},{1,3},{2,0},{3,1},{4,6},{5,7},{6,4},{7,5},{8,10},{9,11},{10,... | collective-permute-start | bytes 393224 | tf_op jit(solution)/shard_map/diagonal_gather/ppermute | solution.py:266
  20.3 0.7 dynamic-slice_subtract_fusion
  21.2 6.1 %collective-permute-done.6.d2 = bf16[256,256]{1,0:T(8,128)(2,1)S(1)} collective-permute-done((bf16[256,256]{1,0:T(8,128)(2,1)S(1)}, bf16[256,256]{1,0:T(8,128)(2,1)S(1)}, u32[]{:S(2)}, u32[]{:S(2)}) %collective-permute-start.6) | collective-permute-done | bytes 131104 | tf_op jit(solution)/shard_map/diagonal_gather/ppermute | solution.py:266
  27.3 3.5 %collective-permute-done.7.d3 = bf16[256,256]{1,0:T(8,128)(2,1)S(1)} collective-permute-done((bf16[256,256]{1,0:T(8,128)(2,1)S(1)}, bf16[256,256]{1,0:T(8,128)(2,1)S(1)}, u32[]{:S(2)}, u32[]{:S(2)}) %collective-permute-start.7) | collective-permute-done | bytes 131104 | tf_op jit(solution)/shard_map/diagonal_gather/ppermute | solution.py:266
  30.8 9.8 %factors.1 = f32[128,8,128]{2,1,0:T(8,128)} custom-call(s32[5]{0:T(128)S(1)} %pad_add_fusion.info, f32[4,4096]{1,0:T(4,128)S(1)} %fusion.1.keep, bf16[32,32,256]{2,1,0:T(8,128)(2,1)S(1)} %bitcast.21, bf16[4,32,128,256]{3,2,1,0:T(8,128)(2,1)} %right_far.1, bf16[4,32,128,256]{3,2,1,0:T(8,128)(2,1)} %left_far.1, bf16[256,256]{1,0:T(8,128)(2,1)S(1)} %fusion.d0, ...), custom_call_target="tpu_custom_call" | custom-call | tf_op jit(solution)/shard_map/factors/pallas_call | solution.py:308
  40.7 8.7 %all-to-all-start.1 = ((f32[128,8,128]{2,1,0:T(8,128)}), f32[128,8,128]{2,1,0:T(8,128)S(1)}, u32[]{:S(2)}, u32[]{:S(2)}) async-start(f32[128,8,128]{2,1,0:T(8,128)} %factors.1), calls=%async_computation.1 | async-start | bytes 1048576 | tf_op jit(solution)/shard_map/member_exchange/all_to_all | solution.py:333
  49.4 13.7 %all-to-all-done.1 = f32[128,8,128]{2,1,0:T(8,128)S(1)} async-done(((f32[128,8,128]{2,1,0:T(8,128)}), f32[128,8,128]{2,1,0:T(8,128)S(1)}, u32[]{:S(2)}, u32[]{:S(2)}) %all-to-all-start.1) | async-done | bytes 524320 | tf_op jit(solution)/shard_map/member_exchange/all_to_all | solution.py:333
  63.1 0.9 %place.1 = f32[32,8,256]{2,1,0:T(8,128)} custom-call(s32[1,128]{1,0:T(1,128)S(1)} %and_bitcast_fusion.place, f32[32,4,8,128]{3,2,1,0:T(8,128)S(1)} %bitcast.22), custom_call_target="tpu_custom_call" | custom-call | tf_op jit(solution)/shard_map/place/pallas_call | solution.py:340
  64.0 4.4 %all-to-all-start.2 = ((f32[32,8,256]{2,1,0:T(8,128)}), f32[32,8,256]{2,1,0:T(8,128)S(1)}, u32[]{:S(2)}, u32[]{:S(2)}) async-start(f32[32,8,256]{2,1,0:T(8,128)} %place.1), calls=%async_computation.2 | async-start | bytes 524288 | tf_op jit(solution)/shard_map/block_exchange/all_to_all | solution.py:350
  68.5 0.1 reshape.24
  68.7 0.1 reshape.26
  68.9 2.9 %collective-permute-start = (f32[4,128]{1,0:T(4,128)S(1)}, f32[4,128]{1,0:T(4,128)S(1)}, u32[]{:S(2)}, u32[]{:S(2)}) collective-permute-start(f32[4,128]{1,0:T(4,128)S(1)} %pad_maximum_fusion.1), channel_id=1, source_target_pairs={{0,4},{4,8},{8,12},{12,16},{16,20},{20,24},{24,28},{28,32},{32,36}... | collective-permute-start | bytes 6152 | tf_op jit(solution)/shard_map/coefficient_halo/ppermute | solution.py:281
  71.8 4.3 %collective-permute-start.1 = (f32[4,128]{1,0:T(4,128)S(1)}, f32[4,128]{1,0:T(4,128)S(1)}, u32[]{:S(2)}, u32[]{:S(2)}) collective-permute-start(f32[4,128]{1,0:T(4,128)S(1)} %pad_maximum_fusion.1), channel_id=1, source_target_pairs={{4,0},{8,4},{12,8},{16,12},{20,16},{24,20},{28,24},{32,28},{36,32}... | collective-permute-start | bytes 6152 | tf_op jit(solution)/shard_map/coefficient_halo/ppermute | solution.py:281
  76.1 1.1 %collective-permute-done = f32[4,128]{1,0:T(4,128)S(1)} collective-permute-done((f32[4,128]{1,0:T(4,128)S(1)}, f32[4,128]{1,0:T(4,128)S(1)}, u32[]{:S(2)}, u32[]{:S(2)}) %collective-permute-start) | collective-permute-done | bytes 2080 | tf_op jit(solution)/shard_map/coefficient_halo/ppermute | solution.py:281
  77.2 2.7 %collective-permute-start.2 = (f32[12,128]{1,0:T(8,128)S(1)}, f32[12,128]{1,0:T(8,128)S(1)}, u32[]{:S(2)}, u32[]{:S(2)}) collective-permute-start(f32[12,128]{1,0:T(8,128)S(1)} %pad_maximum_fusion.own), channel_id=1, source_target_pairs={{0,1},{1,2},{2,3},{3,0},{4,5},{5,6},{6,7},{7,4},{8,9},{9,10},{10,1... | collective-permute-start | bytes 18440 | tf_op jit(solution)/shard_map/coefficient_halo/ppermute | solution.py:293
  79.9 0.8 collective-permute-done.2.low
  80.7 2.3 %collective-permute-done.3.high = f32[12,128]{1,0:T(8,128)S(1)} collective-permute-done((f32[12,128]{1,0:T(8,128)S(1)}, f32[12,128]{1,0:T(8,128)S(1)}, u32[]{:S(2)}, u32[]{:S(2)}) %collective-permute-start.3) | collective-permute-done | bytes 6176 | tf_op jit(solution)/shard_map/coefficient_halo/ppermute | solution.py:295
  83.1 4.2 %stencil.1 = f32[32,4,64]{2,1,0:T(4,128)} custom-call(s32[1]{0:T(128)} %bitcast.parity, f32[5,8,256]{2,1,0:T(8,128)S(1)} %coefficient_halo.1.weight, f32[32,8,256]{2,1,0:T(8,128)S(1)} %all-to-all-done.2.got), custom_call_target="tpu_custom_call" | custom-call | tf_op jit(solution)/shard_map/stencil/pallas_call | solution.py:353
  (32 shorter events, 0.7 us)
Async XLA Ops:
  0.0 5.1 %copy-start = (s32[4,32]{1,0:T(4,128)S(1)}, s32[4,32]{1,0:T(4,128)}, u32[]{:S(2)}) copy-start(s32[4,32]{1,0:T(4,128)} %param.14) | copy-start | bytes 1540
  0.0 7.2 %collective-permute-start.4 = (bf16[4,32,256]{2,1,0:T(8,128)(2,1)}, bf16[4,32,256]{2,1,0:T(8,128)(2,1)S(1)}, u32[]{:S(2)}, u32[]{:S(2)}) collective-permute-start(bf16[4,32,256]{2,1,0:T(8,128)(2,1)} %param.10), channel_id=1, source_target_pairs={{0,0},{1,32},{2,64},{3,96},{4,4},{5,36},{6,68},{7,100},{8,8},{9,40... | collective-permute-start | bytes 196616 | tf_op jit(solution)/shard_map/noise_gather/ppermute | solution.py:257
  8.1 22.7 %all-to-all-start = ((bf16[8,4,32,256]{3,2,1,0:T(8,128)(2,1)}), bf16[8,4,32,256]{3,2,1,0:T(8,128)(2,1)S(1)}, u32[]{:S(2)}, u32[]{:S(2)}) async-start(bf16[8,4,32,256]{3,2,1,0:T(8,128)(2,1)} %broadcast_in_dim.24), calls=%async_computation | async-start | bytes 1048576 | tf_op jit(solution)/shard_map/noise_gather/all_to_all | solution.py:259
  15.7 5.4 %collective-permute-start.5 = (bf16[256,256]{1,0:T(8,128)(2,1)S(1)}, bf16[256,256]{1,0:T(8,128)(2,1)S(1)}, u32[]{:S(2)}, u32[]{:S(2)}) collective-permute-start(bf16[256,256]{1,0:T(8,128)(2,1)S(1)} %fusion.d0), channel_id=1, source_target_pairs={{0,1},{1,0},{2,3},{3,2},{4,5},{5,4},{6,7},{7,6},{8,9},{9,8},{10,11... | collective-permute-start | bytes 393224 | tf_op jit(solution)/shard_map/diagonal_gather/ppermute | solution.py:266
  15.8 11.4 %collective-permute-start.6 = (bf16[256,256]{1,0:T(8,128)(2,1)S(1)}, bf16[256,256]{1,0:T(8,128)(2,1)S(1)}, u32[]{:S(2)}, u32[]{:S(2)}) collective-permute-start(bf16[256,256]{1,0:T(8,128)(2,1)S(1)} %fusion.d0), channel_id=1, source_target_pairs={{0,2},{1,3},{2,0},{3,1},{4,6},{5,7},{6,4},{7,5},{8,10},{9,11},{10,... | collective-permute-start | bytes 393224 | tf_op jit(solution)/shard_map/diagonal_gather/ppermute | solution.py:266
  20.3 10.5 %collective-permute-start.7 = (bf16[256,256]{1,0:T(8,128)(2,1)S(1)}, bf16[256,256]{1,0:T(8,128)(2,1)S(1)}, u32[]{:S(2)}, u32[]{:S(2)}) collective-permute-start(bf16[256,256]{1,0:T(8,128)(2,1)S(1)} %fusion.d0), channel_id=1, source_target_pairs={{0,3},{1,2},{2,1},{3,0},{4,7},{5,6},{6,5},{7,4},{8,11},{9,10},{10,... | collective-permute-start | bytes 393224 | tf_op jit(solution)/shard_map/diagonal_gather/ppermute | solution.py:266
  30.8 18.6 %copy-start.5 = (s32[128]{0:T(128)S(1)}, s32[128]{0:T(128)}, u32[]{:S(2)}) copy-start(s32[128]{0:T(128)} %param.15) | copy-start | bytes 1540
  30.8 18.6 %copy-start.1 = (f32[4,64]{1,0:T(4,128)S(1)}, f32[4,64]{1,0:T(4,128)}, u32[]{:S(2)}) copy-start(f32[4,64]{1,0:T(4,128)} %param.16) | copy-start | bytes 3076
  30.8 18.6 %copy-start.2 = (s32[4,64]{1,0:T(4,128)S(1)}, s32[4,64]{1,0:T(4,128)}, u32[]{:S(2)}) copy-start(s32[4,64]{1,0:T(4,128)} %param.18) | copy-start | bytes 3076
  30.8 37.6 %copy-start.3 = (f32[4,64]{1,0:T(4,128)S(1)}, f32[4,64]{1,0:T(4,128)}, u32[]{:S(2)}) copy-start(f32[4,64]{1,0:T(4,128)} %param.17) | copy-start | bytes 3076
  30.8 37.6 %copy-start.4 = (s32[4,64]{1,0:T(4,128)S(1)}, s32[4,64]{1,0:T(4,128)}, u32[]{:S(2)}) copy-start(s32[4,64]{1,0:T(4,128)} %param.19) | copy-start | bytes 3076
  40.7 22.4 %all-to-all-start.1 = ((f32[128,8,128]{2,1,0:T(8,128)}), f32[128,8,128]{2,1,0:T(8,128)S(1)}, u32[]{:S(2)}, u32[]{:S(2)}) async-start(f32[128,8,128]{2,1,0:T(8,128)} %factors.1), calls=%async_computation.1 | async-start | bytes 1048576 | tf_op jit(solution)/shard_map/member_exchange/all_to_all | solution.py:333
  64.0 19.1 %all-to-all-start.2 = ((f32[32,8,256]{2,1,0:T(8,128)}), f32[32,8,256]{2,1,0:T(8,128)S(1)}, u32[]{:S(2)}, u32[]{:S(2)}) async-start(f32[32,8,256]{2,1,0:T(8,128)} %place.1), calls=%async_computation.2 | async-start | bytes 524288 | tf_op jit(solution)/shard_map/block_exchange/all_to_all | solution.py:350
  68.9 8.2 %collective-permute-start = (f32[4,128]{1,0:T(4,128)S(1)}, f32[4,128]{1,0:T(4,128)S(1)}, u32[]{:S(2)}, u32[]{:S(2)}) collective-permute-start(f32[4,128]{1,0:T(4,128)S(1)} %pad_maximum_fusion.1), channel_id=1, source_target_pairs={{0,4},{4,8},{8,12},{12,16},{16,20},{20,24},{24,28},{28,32},{32,36}... | collective-permute-start | bytes 6152 | tf_op jit(solution)/shard_map/coefficient_halo/ppermute | solution.py:281
  71.8 5.3 %collective-permute-start.1 = (f32[4,128]{1,0:T(4,128)S(1)}, f32[4,128]{1,0:T(4,128)S(1)}, u32[]{:S(2)}, u32[]{:S(2)}) collective-permute-start(f32[4,128]{1,0:T(4,128)S(1)} %pad_maximum_fusion.1), channel_id=1, source_target_pairs={{4,0},{8,4},{12,8},{16,12},{20,16},{24,20},{28,24},{32,28},{36,32}... | collective-permute-start | bytes 6152 | tf_op jit(solution)/shard_map/coefficient_halo/ppermute | solution.py:281
  77.2 3.5 %collective-permute-start.2 = (f32[12,128]{1,0:T(8,128)S(1)}, f32[12,128]{1,0:T(8,128)S(1)}, u32[]{:S(2)}, u32[]{:S(2)}) collective-permute-start(f32[12,128]{1,0:T(8,128)S(1)} %pad_maximum_fusion.own), channel_id=1, source_target_pairs={{0,1},{1,2},{2,3},{3,0},{4,5},{5,6},{6,7},{7,4},{8,9},{9,10},{10,1... | collective-permute-start | bytes 18440 | tf_op jit(solution)/shard_map/coefficient_halo/ppermute | solution.py:293
  79.9 3.1 %collective-permute-start.3 = (f32[12,128]{1,0:T(8,128)S(1)}, f32[12,128]{1,0:T(8,128)S(1)}, u32[]{:S(2)}, u32[]{:S(2)}) collective-permute-start(f32[12,128]{1,0:T(8,128)S(1)} %pad_maximum_fusion.own), channel_id=1, source_target_pairs={{1,0},{2,1},{3,2},{0,3},{5,4},{6,5},{7,6},{4,7},{9,8},{10,9},{11,1... | collective-permute-start | bytes 18440 | tf_op jit(solution)/shard_map/coefficient_halo/ppermute | solution.py:295

commit v4 on v3

v4 whole, which is shorter than its diff:
```python
import functools

import jax
import jax.numpy as jnp
import numpy as np
from jax import lax
from jax.experimental import pallas as pl
from jax.experimental.pallas import tpu as pltpu
from jax.sharding import PartitionSpec as P

ITERS = 4
MIXING = 0.05
BOTH = ("wide", "narrow")
VMEM = pltpu.VMEM
SMEM = pltpu.SMEM
MIB = 1 << 20


def specs(*spaces):
    return [pl.BlockSpec(memory_space=space) for space in spaces]


def near(value):
    return pltpu.with_memory_space_constraint(value, VMEM)


def far(value):
    return pltpu.with_memory_space_constraint(value, pltpu.HBM)


def limit(mib):
    return pltpu.CompilerParams(vmem_limit_bytes=mib * MIB)


def halves(count):
    return slice(0, count // 2), slice(count // 2, count)


def factor_kernel(
    owner,
    keep,
    right_far,
    left_far,
    diag_far,
    *rest,
):
    pieces, (out, noise, coeff, turned, right, left, diag, done) = rest[:-8], rest[-8:]
    rows, cols, rank_max, cells = right.shape
    members = noise.shape[1]
    each = cols // len(pieces)
    chunks = [slice(i * each, (i + 1) * each) for i in range(len(pieces))]
    pairs = [(right_far.at[:, span], right.at[:, span]) for span in chunks]
    pairs += [(left_far.at[p, span], left.at[p, span]) for p in range(rows) for span in halves(cols)]
    pairs += [(diag_far, diag)]
    copies = [
        pltpu.make_async_copy(source, target, done.at[i])
        for i, (source, target) in enumerate(pairs)
    ]
    ahead = 3
    for copy in copies[:ahead]:
        copy.start()

    def arrived(i):
        copies[i].wait()
        if i + ahead < len(copies):
            copies[i + ahead].start()

    w, n = lax.axis_index("wide"), lax.axis_index("narrow")
    place = w % len(pieces)
    for j, piece in enumerate(pieces):
        noise[pl.ds(each * (place ^ j), each)] = piece[...]
    for c in range(cols):
        if c % each == 0:
            arrived(c // each)
        span = slice(c * rank_max, (c + 1) * rank_max)
        block = right[:, c].reshape(rows * rank_max, cells)
        product = lax.dot_general(
            noise[c], block, (((1,), (1,)), ((), ())), preferred_element_type=jnp.float32
        )
        for p in range(rows):
            part = product[:, p * rank_max : (p + 1) * rank_max]
            part = jnp.where(keep[p : p + 1, span] > 0, part, 0.0)
            coeff[p, :, span] = part.astype(jnp.bfloat16)
    sums = []
    for p in range(rows):
        total = 0.0
        for i, span in enumerate(halves(cols)):
            arrived(len(chunks) + 2 * p + i)
            total = total + jnp.dot(
                coeff[p, :, rank_max * span.start : rank_max * span.stop],
                left[p, span].reshape(cols // 2 * rank_max, cells),
                preferred_element_type=jnp.float32,
            )
        sums.append(total)
    arrived(len(copies) - 1)
    for p, total in enumerate(sums):
        local = owner[rows * w + p] - cols * n
        held = jnp.logical_and(local >= 0, local < cols)
        term = lax.dot_general(
            noise[jnp.clip(local, 0, cols - 1)],
            diag[p].astype(jnp.bfloat16),
            (((1,), (1,)), ((), ())),
            preferred_element_type=jnp.float32,
        )
        total = total + jnp.where(held, term, 0.0)
        for g in range(members // 8):
            for h in range(2):
                turned[pl.ds(64 * g + 2 * p + h, 8, stride=8), :] = total[
                    8 * g : 8 * g + 8, 128 * h : 128 * h + 128
                ]
    for d in range(out.shape[0]):
        member = d % members
        out[d] = turned[8 * member : 8 * member + 8, :]


def weight_kernel(low, own, high, out):
    low, own, high = low[...], own[...], high[...]
    lane = lax.broadcasted_iota(jnp.int32, low.shape, 1)
    cx, cy = [
        jnp.where(
            lane < 16,
            pltpu.roll(low, edge, 1),
            jnp.where(lane < 80, pltpu.roll(own, middle, 1), pltpu.roll(high, edge, 1)),
        )
        for edge, middle in ((80, 16), (16, 80))
    ]
    weights = (
        1.0 - jnp.abs(cx) - jnp.abs(cy) - 4.0 * MIXING,
        MIXING + jnp.maximum(cx, 0.0),
        MIXING + jnp.maximum(-cx, 0.0),
        MIXING + jnp.maximum(cy, 0.0),
        MIXING + jnp.maximum(-cy, 0.0),
    )
    for i, weight in enumerate(weights):
        for row in range(12):
            out[i, row] = jnp.broadcast_to(weight[row : row + 1], (8, 128))


def place_kernel(place, got, out, summed, window):
    total = got[:, 0] + got[:, 1] + got[:, 2] + got[:, 3]
    summed[...] = total.reshape(256, 128)
    target = lax.broadcasted_iota(jnp.int32, (64, 128), 0)
    one_hot = jnp.where(target == place[...], 1.0, 0.0).astype(jnp.bfloat16)
    one_hot = jnp.concatenate([one_hot] * 3, axis=1)
    fields = []
    for h in range(2):
        rest = summed[pl.ds(h, 128, stride=2), :]
        parts = []
        for _ in range(3):
            part = rest.astype(jnp.bfloat16)
            parts.append(part)
            rest = rest - part.astype(jnp.float32)
        fields.append(
            jnp.dot(
                one_hot, jnp.concatenate(parts, axis=0), preferred_element_type=jnp.float32
            ).reshape(4, 16, 128)
        )
    shape = (8, 8, 128)
    sub = lax.broadcasted_iota(jnp.int32, shape, 1)
    group = lax.broadcasted_iota(jnp.int32, shape, 2) // 16
    sides = []
    for h in range(2):
        x = jnp.concatenate([f[:, 8 * h : 8 * h + 8] for f in fields], axis=1).reshape(shape)
        for bit in (1, 2, 4):
            in_sub, in_group = (sub & bit) != 0, (group & bit) != 0
            later = pltpu.roll(pltpu.roll(x, 8 - bit, 1), 16 * bit, 2)
            earlier = pltpu.roll(pltpu.roll(x, bit, 1), 128 - 16 * bit, 2)
            x = jnp.where(in_sub == in_group, x, jnp.where(in_group, later, earlier))
        sides.append(x.reshape(64, 128))
    lane = lax.broadcasted_iota(jnp.int32, (64, 128), 1)
    for nd in range(4):
        shift = 80 if nd % 2 else 16
        first, second = (sides[1], sides[0]) if nd in (0, 3) else (sides[0], sides[1])
        window[nd] = jnp.where(
            lane < shift, pltpu.roll(first, shift, 1), pltpu.roll(second, shift, 1)
        )
    for txl in range(2):
        for k in range(4):
            start = 12 + 16 * txl + 4 * k
            for nd in range(4):
                out[txl * 16 + k * 4 + nd] = window[nd, start : start + 16, :]


def block_kernel(weight, got, out):
    members = out.shape[0]
    for start in range(0, members, 8):
        field = {r: got[pl.ds(16 * start + r, 8, stride=16), :] for r in range(12)}
        for step in range(ITERS):
            field = {
                r: weight[0, r] * field[r]
                + weight[1, r] * field[r - 1]
                + weight[2, r] * field[r + 1]
                + weight[3, r] * pltpu.roll(field[r], 1, 1)
                + weight[4, r] * pltpu.roll(field[r], 127, 1)
                for r in range(1 + step, 11 - step)
            }
        for i in range(4):
            out[start : start + 8, i, :] = pltpu.roll(field[4 + i], 112, 1)[:, :64]


def ring(count):
    forward = [(i, (i + 1) % count) for i in range(count)]
    return forward, [(b, a) for a, b in forward]


def per_device(
    noise,
    diagonal_tile_blocks,
    left_factors,
    right_factors,
    ranks,
    owner,
    courant_x,
    courant_number_second,
    upwind_x,
    upwind_y,
):
    wide, narrow = lax.axis_size("wide"), lax.axis_size("narrow")
    group = wide // narrow
    devices = wide * narrow
    plane = lax.axis_index("wide") // group
    rows, cols = ranks.shape
    rank_max = left_factors.shape[2]
    members = noise.shape[1]
    cells = noise.shape[2]
    f32 = jnp.float32

    slabs = [[z * group * narrow + i for i in range(group * narrow)] for z in range(narrow)]

    with jax.named_scope("noise_gather"):
        pieces = [
            lax.ppermute(
                noise,
                BOTH,
                [
                    ((z * group + r) * narrow + b, (b * group + (r ^ j)) * narrow + z)
                    for z in range(narrow)
                    for r in range(group)
                    for b in range(narrow)
                ],
            )
            for j in range(group)
        ]

    with jax.named_scope("diagonal_gather"):
        diag = lax.all_gather(jnp.tril(diagonal_tile_blocks).astype(f32), "narrow", tiled=True)

    with jax.named_scope("coefficient_halo"):
        own = jnp.concatenate(
            [
                jnp.where(flag == 1, value, -value)
                for value, flag in ((courant_x, upwind_x), (courant_number_second, upwind_y))
            ],
            axis=1,
        )
        forward, backward = ring(wide)
        own = jnp.concatenate(
            [lax.ppermute(own, "wide", forward), own, lax.ppermute(own, "wide", backward)], axis=0
        )

    with jax.named_scope("factors"):
        keep = (
            jnp.arange(rank_max, dtype=jnp.int32)[None, None, :] < ranks[:, :, None]
        ).astype(f32).reshape(rows, cols * rank_max)
        partial_sums = pl.pallas_call(
            factor_kernel,
            out_shape=pltpu.VMEM((devices, 8, 128), f32),
            in_specs=specs(SMEM, VMEM, pltpu.HBM, pltpu.HBM, pltpu.HBM, *[VMEM] * group),
            out_specs=pl.BlockSpec(memory_space=VMEM),
            scratch_shapes=[
                pltpu.VMEM((cols, members, cells), noise.dtype),
                pltpu.VMEM((rows, members, cols * rank_max), jnp.bfloat16),
                pltpu.VMEM((members * 8, 128), f32),
                pltpu.VMEM(right_factors.shape, right_factors.dtype),
                pltpu.VMEM(left_factors.shape, left_factors.dtype),
                pltpu.VMEM(diag.shape, f32),
                pltpu.SemaphoreType.DMA((group + 2 * rows + 1,)),
            ],
            compiler_params=limit(28),
        )(
            owner,
            near(keep),
            far(right_factors),
            far(left_factors),
            far(diag),
            *[near(piece) for piece in pieces],
        )

    with jax.named_scope("member_exchange"):
        got = lax.all_to_all(partial_sums, BOTH, 0, 0, tiled=True)
        got, own = lax.optimization_barrier((got, own))

    with jax.named_scope("weights"):
        forward, backward = ring(narrow)
        weight = pl.pallas_call(
            weight_kernel,
            out_shape=pltpu.VMEM((5, 12, 8, 128), f32),
            in_specs=specs(VMEM, VMEM, VMEM),
            out_specs=pl.BlockSpec(memory_space=VMEM),
            compiler_params=limit(2),
        )(
            near(lax.ppermute(own, "narrow", forward)),
            near(own),
            near(lax.ppermute(own, "narrow", backward)),
        )

    with jax.named_scope("place"):
        bits = [(owner >> b) & 1 for b in range(7)]
        tile_y = bits[0] | bits[2] << 1 | bits[4] << 2 | bits[6] << 3
        tile_x = bits[1] | bits[3] << 1 | bits[5] << 2
        place = (tile_x * 16 + tile_y - 32 * plane.astype(jnp.int32) + 16) & 127
        blocks = pl.pallas_call(
            place_kernel,
            out_shape=pltpu.VMEM((members, 16, 128), f32),
            in_specs=specs(VMEM, VMEM),
            out_specs=pl.BlockSpec(memory_space=VMEM),
            scratch_shapes=[pltpu.VMEM((256, 128), f32), pltpu.VMEM((4, 64, 128), f32)],
            compiler_params=limit(4),
        )(near(place[None]), near(got.reshape(wide, narrow, 8, 128)))

    with jax.named_scope("block_exchange"):
        mine = lax.all_to_all(blocks, BOTH, 0, 0, axis_index_groups=slabs, tiled=True)

    with jax.named_scope("stencil"):
        return pl.pallas_call(
            block_kernel,
            out_shape=jax.ShapeDtypeStruct((members, 4, 64), f32),
            in_specs=specs(VMEM, VMEM),
            out_specs=pl.BlockSpec(memory_space=VMEM),
            compiler_params=limit(4),
        )(weight, near(mine.reshape(members * 16, 128)))


def solution(mesh):
    placed = (
        P("wide", None, None),
        P(("wide", "narrow"), None, None),
        P("wide", "narrow", None, None),
        P("wide", "narrow", None, None),
        P("wide", "narrow"),
        P(),
        P("wide", "narrow"),
        P("wide", "narrow"),
        P("wide", "narrow"),
        P("wide", "narrow"),
    )
    return jax.shard_map(
        per_device, mesh=mesh, in_specs=placed, out_specs=P(None, "wide", "narrow"), check_vma=False
    )
```

time: 87.7 us -> 100 us (1.14)
  between operations: 0.18 us -> 13.5 us
  starting transfers between devices: 39.3 us -> 45.6 us
  waiting for transfers between devices: 29.5 us -> 25 us
  Pallas kernels: 15.1 us -> 13.2 us
    all_to_all x1, waiting for transfers between devices: 13.7 us -> 0.01 us  [per_device(): got = lax.all_to_all(partial_sums, BOTH, 0, 0, tiled=True)]
    ppermute x4 -> x8, starting transfers between devices: 9.66 us -> 21 us  [per_device(): lax.ppermute(noise, BOTH, [((z * group + r) * narrow + b, (b * group + (r...]
    all_to_all x1 -> x0, starting transfers between devices: 6.65 us -> none  [per_device(): lax.all_to_all(sending, 'wide', 0, 0, axis_index_groups=planes, tiled=True)]
    ppermute x1, waiting for transfers between devices: 1.05 us -> 7.42 us  [per_device(): lax.ppermute(own, 'wide', forward)]
    ppermute x1, starting transfers between devices: 4.28 us -> 8.01 us  [per_device(): lax.ppermute(own, 'wide', backward)]
    all_to_all x1, waiting for transfers between devices: 0.01 us -> 3.29 us  [per_device(): lax.all_to_all(blocks, BOTH, 0, 0, axis_index_groups=slabs, tiled=True)]
    pallas_call x1, Pallas kernels: 4.21 us -> 1.09 us  [per_device(): pl.pallas_call(block_kernel, out_shape=jax.ShapeDtypeStruct((members, 4,...]
    ppermute x1, starting transfers between devices: 2.91 us -> 0.01 us  [per_device(): lax.ppermute(own, 'wide', forward)]
  transfers between devices with their start and end apart: 11 -> 15, of which waited for: 7 -> 8; matrix products, arithmetic and copies ran while one was open for 3% -> 0% of each run, Pallas kernels for 0% -> 0%
where the time goes in v4:
time: 100 us
  starting transfers between devices  45.6 us (46%)
  waiting for transfers between devices  25 us (25%)
  between operations  13.5 us (14%)
  Pallas kernels  13.2 us (13%)
  other arithmetic  1.87 us (2%)
    ppermute x8, starting transfers between devices, per_device(): lax.ppermute(noise, BOTH, [((z * group + r) * narrow + b, (b * group + (r...  21 us
    pallas_call x1, Pallas kernels, per_device(): pl.pallas_call(factor_kernel, out_shape=pltpu.VMEM((devices, 8, 128), f32...  10.8 us
    ppermute x8, waiting for transfers between devices, per_device(): lax.ppermute(noise, BOTH, [((z * group + r) * narrow + b, (b * group + (r...  9.59 us
    all_to_all x1, starting transfers between devices, per_device(): got = lax.all_to_all(partial_sums, BOTH, 0, 0, tiled=True)  9.57 us
    ppermute x1, starting transfers between devices, per_device(): lax.ppermute(own, 'wide', backward)  8.01 us
    ppermute x1, waiting for transfers between devices, per_device(): lax.ppermute(own, 'wide', forward)  7.42 us
    all_to_all x1, starting transfers between devices, per_device(): lax.all_to_all(blocks, BOTH, 0, 0, axis_index_groups=slabs, tiled=True)  5.31 us
    all_to_all x1, waiting for transfers between devices, per_device(): lax.all_to_all(blocks, BOTH, 0, 0, axis_index_groups=slabs, tiled=True)  3.29 us
  transfers between devices with their start and end apart: 15, of which 8 were waited for; matrix products, arithmetic and copies ran while one was open for 0% of the time, Pallas kernels for 0%

profile of v4, /device:TPU:1, one launch (start us, length us, event | category | flops | bytes accessed | tf_op | source)
XLA Modules:
  0.0 100.0 jit_solution(13792034134353138398)
XLA Ops:
  6.5 1.6 %fusion.1 = f32[1,256,256]{2,1,0:T(8,128)} fusion(bf16[1,256,256]{2,1,0:T(8,128)(2,1)} %param.11), kind=kLoop, calls=%fused_computation.2 | loop fusion | flops 196608 | bytes 393216 | tf_op jit(solution)/shard_map/diagonal_gather/convert_element_type | solution.py:246
  8.2 4.9 %collective-permute-start = (bf16[4,32,256]{2,1,0:T(8,128)(2,1)}, bf16[4,32,256]{2,1,0:T(8,128)(2,1)S(1)}, u32[]{:S(2)}, u32[]{:S(2)}) collective-permute-start(bf16[4,32,256]{2,1,0:T(8,128)(2,1)} %param.10), channel_id=1, source_target_pairs={{0,0},{1,32},{2,64},{3,96},{4,4},{5,36},{6,68},{7,100},{8,8},{9,40... | collective-permute-start | bytes 196616 | tf_op jit(solution)/shard_map/noise_gather/ppermute | solution.py:232
  13.2 2.6 %collective-permute-start.1 = (bf16[4,32,256]{2,1,0:T(8,128)(2,1)}, bf16[4,32,256]{2,1,0:T(8,128)(2,1)S(1)}, u32[]{:S(2)}, u32[]{:S(2)}) collective-permute-start(bf16[4,32,256]{2,1,0:T(8,128)(2,1)} %param.10), channel_id=1, source_target_pairs={{0,4},{1,36},{2,68},{3,100},{4,0},{5,32},{6,64},{7,96},{8,12},{9,4... | collective-permute-start | bytes 196616 | tf_op jit(solution)/shard_map/noise_gather/ppermute | solution.py:232
  15.7 2.7 %collective-permute-start.2 = (bf16[4,32,256]{2,1,0:T(8,128)(2,1)}, bf16[4,32,256]{2,1,0:T(8,128)(2,1)S(1)}, u32[]{:S(2)}, u32[]{:S(2)}) collective-permute-start(bf16[4,32,256]{2,1,0:T(8,128)(2,1)} %param.10), channel_id=1, source_target_pairs={{0,8},{1,40},{2,72},{3,104},{4,12},{5,44},{6,76},{7,108},{8,0},{9,... | collective-permute-start | bytes 196616 | tf_op jit(solution)/shard_map/noise_gather/ppermute | solution.py:232
  18.5 4.2 %collective-permute-start.4 = (bf16[4,32,256]{2,1,0:T(8,128)(2,1)}, bf16[4,32,256]{2,1,0:T(8,128)(2,1)S(1)}, u32[]{:S(2)}, u32[]{:S(2)}) collective-permute-start(bf16[4,32,256]{2,1,0:T(8,128)(2,1)} %param.10), channel_id=1, source_target_pairs={{0,16},{1,48},{2,80},{3,112},{4,20},{5,52},{6,84},{7,116},{8,24},{... | collective-permute-start | bytes 196616 | tf_op jit(solution)/shard_map/noise_gather/ppermute | solution.py:232
  22.8 2.5 %collective-permute-start.5 = (bf16[4,32,256]{2,1,0:T(8,128)(2,1)}, bf16[4,32,256]{2,1,0:T(8,128)(2,1)S(1)}, u32[]{:S(2)}, u32[]{:S(2)}) collective-permute-start(bf16[4,32,256]{2,1,0:T(8,128)(2,1)} %param.10), channel_id=1, source_target_pairs={{0,20},{1,52},{2,84},{3,116},{4,16},{5,48},{6,80},{7,112},{8,28},{... | collective-permute-start | bytes 196616 | tf_op jit(solution)/shard_map/noise_gather/ppermute | solution.py:232
  25.3 4.0 %collective-permute-start.6 = (bf16[4,32,256]{2,1,0:T(8,128)(2,1)}, bf16[4,32,256]{2,1,0:T(8,128)(2,1)S(1)}, u32[]{:S(2)}, u32[]{:S(2)}) collective-permute-start(bf16[4,32,256]{2,1,0:T(8,128)(2,1)} %param.10), channel_id=1, source_target_pairs={{0,24},{1,56},{2,88},{3,120},{4,28},{5,60},{6,92},{7,124},{8,16},{... | collective-permute-start | bytes 196616 | tf_op jit(solution)/shard_map/noise_gather/ppermute | solution.py:232
  29.4 3.7 %collective-permute-done.5.rest_5_ = bf16[4,32,256]{2,1,0:T(8,128)(2,1)S(1)} collective-permute-done((bf16[4,32,256]{2,1,0:T(8,128)(2,1)}, bf16[4,32,256]{2,1,0:T(8,128)(2,1)S(1)}, u32[]{:S(2)}, u32[]{:S(2)}) %collective-permute-start.5) | collective-permute-done | bytes 65568 | tf_op jit(solution)/shard_map/noise_gather/ppermute | solution.py:232
  33.1 1.2 %collective-permute-done.6.rest_6_ = bf16[4,32,256]{2,1,0:T(8,128)(2,1)S(1)} collective-permute-done((bf16[4,32,256]{2,1,0:T(8,128)(2,1)}, bf16[4,32,256]{2,1,0:T(8,128)(2,1)S(1)}, u32[]{:S(2)}, u32[]{:S(2)}) %collective-permute-start.6) | collective-permute-done | bytes 65568 | tf_op jit(solution)/shard_map/noise_gather/ppermute | solution.py:232
  34.3 4.7 %collective-permute-done.7.rest_7_ = bf16[4,32,256]{2,1,0:T(8,128)(2,1)S(1)} collective-permute-done((bf16[4,32,256]{2,1,0:T(8,128)(2,1)}, bf16[4,32,256]{2,1,0:T(8,128)(2,1)S(1)}, u32[]{:S(2)}, u32[]{:S(2)}) %collective-permute-start.7) | collective-permute-done | bytes 65568 | tf_op jit(solution)/shard_map/noise_gather/ppermute | solution.py:232
  39.0 0.7 copy-done.1
  39.6 10.8 %factors.1 = f32[128,8,128]{2,1,0:T(8,128)} custom-call(s32[128]{0:T(128)S(1)} %copy-done.1, f32[4,4096]{1,0:T(4,128)S(1)} %fusion.2.keep, bf16[4,32,128,256]{3,2,1,0:T(8,128)(2,1)} %right_far.1, bf16[4,32,128,256]{3,2,1,0:T(8,128)(2,1)} %left_far.1, f32[4,256,256]{2,1,0:T(8,128)} %all-gather.2.cloned.1.call-done.diag_far, ...), custom_call_target="tpu_custom_call" | custom-call | tf_op jit(solution)/shard_map/factors/pallas_call | solution.py:265
  50.4 9.6 %all-to-all-start = ((f32[128,8,128]{2,1,0:T(8,128)}), f32[128,8,128]{2,1,0:T(8,128)S(1)}, u32[]{:S(2)}, u32[]{:S(2)}) async-start(f32[128,8,128]{2,1,0:T(8,128)} %factors.1), calls=%async_computation | async-start | bytes 1048576 | tf_op jit(solution)/shard_map/member_exchange/all_to_all | solution.py:290
  60.1 8.0 %collective-permute-start.9 = (f32[4,128]{1,0:T(4,128)S(1)}, f32[4,128]{1,0:T(4,128)S(1)}, u32[]{:S(2)}, u32[]{:S(2)}) collective-permute-start(f32[4,128]{1,0:T(4,128)S(1)} %pad_maximum_fusion.1), channel_id=1, source_target_pairs={{4,0},{8,4},{12,8},{16,12},{20,16},{24,20},{28,24},{32,28},{36,32}... | collective-permute-start | bytes 6152 | tf_op jit(solution)/shard_map/coefficient_halo/ppermute | solution.py:258
  68.2 0.7 collective-permute-done.9
  68.9 7.4 %collective-permute-done.8 = f32[4,128]{1,0:T(4,128)S(1)} collective-permute-done((f32[4,128]{1,0:T(4,128)S(1)}, f32[4,128]{1,0:T(4,128)S(1)}, u32[]{:S(2)}, u32[]{:S(2)}) %collective-permute-start.8) | collective-permute-done | bytes 2080 | tf_op jit(solution)/shard_map/coefficient_halo/ppermute | solution.py:258
  76.4 1.3 %place.1 = f32[32,16,128]{2,1,0:T(8,128)} custom-call(s32[1,128]{1,0:T(1,128)S(1)} %and_bitcast_fusion.place, f32[32,4,8,128]{3,2,1,0:T(8,128)S(1)} %bitcast.12), custom_call_target="tpu_custom_call" | custom-call | tf_op jit(solution)/shard_map/place/pallas_call | solution.py:312
  77.7 5.3 %all-to-all-start.1 = ((f32[32,16,128]{2,1,0:T(8,128)}), f32[32,16,128]{2,1,0:T(8,128)S(1)}, u32[]{:S(2)}, u32[]{:S(2)}) async-start(f32[32,16,128]{2,1,0:T(8,128)} %place.1), calls=%async_computation.1 | async-start | bytes 524288 | tf_op jit(solution)/shard_map/block_exchange/all_to_all | solution.py:322
  83.0 1.7 %collective-permute-start.10 = (f32[12,128]{1,0:T(8,128)S(1)}, f32[12,128]{1,0:T(8,128)S(1)}, u32[]{:S(2)}, u32[]{:S(2)}) collective-permute-start(f32[12,128]{1,0:T(8,128)S(1)} %pad_maximum_fusion.own), channel_id=1, source_target_pairs={{0,1},{1,2},{2,3},{3,0},{4,5},{5,6},{6,7},{7,4},{8,9},{9,10},{10,1... | collective-permute-start | bytes 18440 | tf_op jit(solution)/shard_map/weights/ppermute | solution.py:302
  84.7 1.6 %collective-permute-done.10.low = f32[12,128]{1,0:T(8,128)S(1)} collective-permute-done((f32[12,128]{1,0:T(8,128)S(1)}, f32[12,128]{1,0:T(8,128)S(1)}, u32[]{:S(2)}, u32[]{:S(2)}) %collective-permute-start.10) | collective-permute-done | bytes 6176 | tf_op jit(solution)/shard_map/weights/ppermute | solution.py:302
  86.2 2.4 %collective-permute-done.11.high = f32[12,128]{1,0:T(8,128)S(1)} collective-permute-done((f32[12,128]{1,0:T(8,128)S(1)}, f32[12,128]{1,0:T(8,128)S(1)}, u32[]{:S(2)}, u32[]{:S(2)}) %collective-permute-start.11) | collective-permute-done | bytes 6176 | tf_op jit(solution)/shard_map/weights/ppermute | solution.py:304
  88.7 0.1 weights.1.weight
  88.8 3.3 %all-to-all-done.1 = f32[32,16,128]{2,1,0:T(8,128)S(1)} async-done(((f32[32,16,128]{2,1,0:T(8,128)}), f32[32,16,128]{2,1,0:T(8,128)S(1)}, u32[]{:S(2)}, u32[]{:S(2)}) %all-to-all-start.1) | async-done | bytes 262176 | tf_op jit(solution)/shard_map/block_exchange/all_to_all | solution.py:322
  92.1 1.1 %stencil.1 = f32[32,4,64]{2,1,0:T(4,128)} custom-call(f32[5,12,8,128]{3,2,1,0:T(8,128)S(1)} %weights.1.weight, f32[512,128]{1,0:T(8,128)S(1)} %bitcast.13), custom_call_target="tpu_custom_call" | custom-call | tf_op jit(solution)/shard_map/stencil/pallas_call | solution.py:325
  (33 shorter events, 0.4 us)
Async XLA Ops:
  6.5 16.1 %copy-start = (s32[4,32]{1,0:T(4,128)S(1)}, s32[4,32]{1,0:T(4,128)}, u32[]{:S(2)}) copy-start(s32[4,32]{1,0:T(4,128)} %param.14) | copy-start | bytes 1540
  6.5 32.5 %all-gather.2.cloned.1.call-start = ((), (), s32[]{:S(2)}) async-start(), calls=%async_computation.2 | async-start | bytes 1310720 | tf_op jit(solution)/shard_map/diagonal_gather/all_gather | solution.py:246
  8.2 14.5 %collective-permute-start = (bf16[4,32,256]{2,1,0:T(8,128)(2,1)}, bf16[4,32,256]{2,1,0:T(8,128)(2,1)S(1)}, u32[]{:S(2)}, u32[]{:S(2)}) collective-permute-start(bf16[4,32,256]{2,1,0:T(8,128)(2,1)} %param.10), channel_id=1, source_target_pairs={{0,0},{1,32},{2,64},{3,96},{4,4},{5,36},{6,68},{7,100},{8,8},{9,40... | collective-permute-start | bytes 196616 | tf_op jit(solution)/shard_map/noise_gather/ppermute | solution.py:232
  13.2 12.1 %collective-permute-start.1 = (bf16[4,32,256]{2,1,0:T(8,128)(2,1)}, bf16[4,32,256]{2,1,0:T(8,128)(2,1)S(1)}, u32[]{:S(2)}, u32[]{:S(2)}) collective-permute-start(bf16[4,32,256]{2,1,0:T(8,128)(2,1)} %param.10), channel_id=1, source_target_pairs={{0,4},{1,36},{2,68},{3,100},{4,0},{5,32},{6,64},{7,96},{8,12},{9,4... | collective-permute-start | bytes 196616 | tf_op jit(solution)/shard_map/noise_gather/ppermute | solution.py:232
  15.7 13.6 %collective-permute-start.2 = (bf16[4,32,256]{2,1,0:T(8,128)(2,1)}, bf16[4,32,256]{2,1,0:T(8,128)(2,1)S(1)}, u32[]{:S(2)}, u32[]{:S(2)}) collective-permute-start(bf16[4,32,256]{2,1,0:T(8,128)(2,1)} %param.10), channel_id=1, source_target_pairs={{0,8},{1,40},{2,72},{3,104},{4,12},{5,44},{6,76},{7,108},{8,0},{9,... | collective-permute-start | bytes 196616 | tf_op jit(solution)/shard_map/noise_gather/ppermute | solution.py:232
  18.5 10.9 %collective-permute-start.3 = (bf16[4,32,256]{2,1,0:T(8,128)(2,1)}, bf16[4,32,256]{2,1,0:T(8,128)(2,1)S(1)}, u32[]{:S(2)}, u32[]{:S(2)}) collective-permute-start(bf16[4,32,256]{2,1,0:T(8,128)(2,1)} %param.10), channel_id=1, source_target_pairs={{0,12},{1,44},{2,76},{3,108},{4,8},{5,40},{6,72},{7,104},{8,4},{9,... | collective-permute-start | bytes 196616 | tf_op jit(solution)/shard_map/noise_gather/ppermute | solution.py:232
  18.5 10.9 %collective-permute-start.4 = (bf16[4,32,256]{2,1,0:T(8,128)(2,1)}, bf16[4,32,256]{2,1,0:T(8,128)(2,1)S(1)}, u32[]{:S(2)}, u32[]{:S(2)}) collective-permute-start(bf16[4,32,256]{2,1,0:T(8,128)(2,1)} %param.10), channel_id=1, source_target_pairs={{0,16},{1,48},{2,80},{3,112},{4,20},{5,52},{6,84},{7,116},{8,24},{... | collective-permute-start | bytes 196616 | tf_op jit(solution)/shard_map/noise_gather/ppermute | solution.py:232
  22.8 10.4 %collective-permute-start.5 = (bf16[4,32,256]{2,1,0:T(8,128)(2,1)}, bf16[4,32,256]{2,1,0:T(8,128)(2,1)S(1)}, u32[]{:S(2)}, u32[]{:S(2)}) collective-permute-start(bf16[4,32,256]{2,1,0:T(8,128)(2,1)} %param.10), channel_id=1, source_target_pairs={{0,20},{1,52},{2,84},{3,116},{4,16},{5,48},{6,80},{7,112},{8,28},{... | collective-permute-start | bytes 196616 | tf_op jit(solution)/shard_map/noise_gather/ppermute | solution.py:232
  25.3 9.0 %collective-permute-start.6 = (bf16[4,32,256]{2,1,0:T(8,128)(2,1)}, bf16[4,32,256]{2,1,0:T(8,128)(2,1)S(1)}, u32[]{:S(2)}, u32[]{:S(2)}) collective-permute-start(bf16[4,32,256]{2,1,0:T(8,128)(2,1)} %param.10), channel_id=1, source_target_pairs={{0,24},{1,56},{2,88},{3,120},{4,28},{5,60},{6,92},{7,124},{8,16},{... | collective-permute-start | bytes 196616 | tf_op jit(solution)/shard_map/noise_gather/ppermute | solution.py:232
  29.3 9.7 %collective-permute-start.7 = (bf16[4,32,256]{2,1,0:T(8,128)(2,1)}, bf16[4,32,256]{2,1,0:T(8,128)(2,1)S(1)}, u32[]{:S(2)}, u32[]{:S(2)}) collective-permute-start(bf16[4,32,256]{2,1,0:T(8,128)(2,1)} %param.10), channel_id=1, source_target_pairs={{0,28},{1,60},{2,92},{3,124},{4,24},{5,56},{6,88},{7,120},{8,20},{... | collective-permute-start | bytes 196616 | tf_op jit(solution)/shard_map/noise_gather/ppermute | solution.py:232
  29.3 30.7 %copy-start.3 = (f32[4,64]{1,0:T(4,128)S(1)}, f32[4,64]{1,0:T(4,128)}, u32[]{:S(2)}) copy-start(f32[4,64]{1,0:T(4,128)} %param.17) | copy-start | bytes 3076
  29.3 30.7 %copy-start.4 = (s32[4,64]{1,0:T(4,128)S(1)}, s32[4,64]{1,0:T(4,128)}, u32[]{:S(2)}) copy-start(s32[4,64]{1,0:T(4,128)} %param.19) | copy-start | bytes 3076
  29.3 30.7 %copy-start.5 = (f32[4,64]{1,0:T(4,128)S(1)}, f32[4,64]{1,0:T(4,128)}, u32[]{:S(2)}) copy-start(f32[4,64]{1,0:T(4,128)} %param.16) | copy-start | bytes 3076
  29.3 30.7 %copy-start.6 = (s32[4,64]{1,0:T(4,128)S(1)}, s32[4,64]{1,0:T(4,128)}, u32[]{:S(2)}) copy-start(s32[4,64]{1,0:T(4,128)} %param.18) | copy-start | bytes 3076
  29.3 38.8 %copy-start.2 = (s32[128]{0:T(128)S(1)}, s32[128]{0:T(128)}, u32[]{:S(2)}) copy-start(s32[128]{0:T(128)} %owner.1) | copy-start | bytes 1540
  39.0 0.7 copy-start.1
  50.4 26.0 %all-to-all-start = ((f32[128,8,128]{2,1,0:T(8,128)}), f32[128,8,128]{2,1,0:T(8,128)S(1)}, u32[]{:S(2)}, u32[]{:S(2)}) async-start(f32[128,8,128]{2,1,0:T(8,128)} %factors.1), calls=%async_computation | async-start | bytes 1048576 | tf_op jit(solution)/shard_map/member_exchange/all_to_all | solution.py:290
  60.1 8.7 %collective-permute-start.9 = (f32[4,128]{1,0:T(4,128)S(1)}, f32[4,128]{1,0:T(4,128)S(1)}, u32[]{:S(2)}, u32[]{:S(2)}) collective-permute-start(f32[4,128]{1,0:T(4,128)S(1)} %pad_maximum_fusion.1), channel_id=1, source_target_pairs={{4,0},{8,4},{12,8},{16,12},{20,16},{24,20},{28,24},{32,28},{36,32}... | collective-permute-start | bytes 6152 | tf_op jit(solution)/shard_map/coefficient_halo/ppermute | solution.py:258
  68.1 8.2 %collective-permute-start.8 = (f32[4,128]{1,0:T(4,128)S(1)}, f32[4,128]{1,0:T(4,128)S(1)}, u32[]{:S(2)}, u32[]{:S(2)}) collective-permute-start(f32[4,128]{1,0:T(4,128)S(1)} %pad_maximum_fusion.1), channel_id=1, source_target_pairs={{0,4},{4,8},{8,12},{12,16},{16,20},{20,24},{24,28},{28,32},{32,36}... | collective-permute-start | bytes 6152 | tf_op jit(solution)/shard_map/coefficient_halo/ppermute | solution.py:258
  77.7 14.4 %all-to-all-start.1 = ((f32[32,16,128]{2,1,0:T(8,128)}), f32[32,16,128]{2,1,0:T(8,128)S(1)}, u32[]{:S(2)}, u32[]{:S(2)}) async-start(f32[32,16,128]{2,1,0:T(8,128)} %place.1), calls=%async_computation.1 | async-start | bytes 524288 | tf_op jit(solution)/shard_map/block_exchange/all_to_all | solution.py:322
  83.0 3.3 %collective-permute-start.10 = (f32[12,128]{1,0:T(8,128)S(1)}, f32[12,128]{1,0:T(8,128)S(1)}, u32[]{:S(2)}, u32[]{:S(2)}) collective-permute-start(f32[12,128]{1,0:T(8,128)S(1)} %pad_maximum_fusion.own), channel_id=1, source_target_pairs={{0,1},{1,2},{2,3},{3,0},{4,5},{5,6},{6,7},{7,4},{8,9},{9,10},{10,1... | collective-permute-start | bytes 18440 | tf_op jit(solution)/shard_map/weights/ppermute | solution.py:302
  84.7 4.0 %collective-permute-start.11 = (f32[12,128]{1,0:T(8,128)S(1)}, f32[12,128]{1,0:T(8,128)S(1)}, u32[]{:S(2)}, u32[]{:S(2)}) collective-permute-start(f32[12,128]{1,0:T(8,128)S(1)} %pad_maximum_fusion.own), channel_id=1, source_target_pairs={{1,0},{2,1},{3,2},{0,3},{5,4},{6,5},{7,6},{4,7},{9,8},{10,9},{11,1... | collective-permute-start | bytes 18440 | tf_op jit(solution)/shard_map/weights/ppermute | solution.py:304
Sparse Core Ops, SparseCore 0:
  9.0 26.7 all-gather.1

commit v5 on v4

--- a/solution.py
+++ b/solution.py
@@ -14,6 +14,7 @@
 VMEM = pltpu.VMEM
 SMEM = pltpu.SMEM
 MIB = 1 << 20
+CHUNKS = 8
 
 
 def specs(*spaces):
@@ -39,36 +40,60 @@
 def factor_kernel(
     owner,
     keep,
+    noise,
     right_far,
     left_far,
     diag_far,
-    *rest,
+    d1,
+    d2,
+    d3,
+    out,
+    coeff,
+    turned,
+    own,
+    right,
+    left,
+    d0,
+    kept,
+    done,
 ):
-    pieces, (out, noise, coeff, turned, right, left, diag, done) = rest[:-8], rest[-8:]
     rows, cols, rank_max, cells = right.shape
     members = noise.shape[1]
-    each = cols // len(pieces)
-    chunks = [slice(i * each, (i + 1) * each) for i in range(len(pieces))]
+    each = cols // CHUNKS
+    chunks = [slice(i * each, (i + 1) * each) for i in range(CHUNKS)]
     pairs = [(right_far.at[:, span], right.at[:, span]) for span in chunks]
     pairs += [(left_far.at[p, span], left.at[p, span]) for p in range(rows) for span in halves(cols)]
-    pairs += [(diag_far, diag)]
+    pairs += [(diag_far, d0)]
     copies = [
         pltpu.make_async_copy(source, target, done.at[i])
         for i, (source, target) in enumerate(pairs)
     ]
-    ahead = 3
-    for copy in copies[:ahead]:
+    copies[-1].start()
+    for copy in copies[:CHUNKS]:
         copy.start()
+    copies[-1].wait()
 
     def arrived(i):
         copies[i].wait()
-        if i + ahead < len(copies):
-            copies[i + ahead].start()
+        if i + CHUNKS < len(copies) - 1:
+            copies[i + CHUNKS].start()
 
     w, n = lax.axis_index("wide"), lax.axis_index("narrow")
-    place = w % len(pieces)
-    for j, piece in enumerate(pieces):
-        noise[pl.ds(each * (place ^ j), each)] = piece[...]
+    lower = lax.broadcasted_iota(jnp.int32, (cells, cells), 0) >= lax.broadcasted_iota(
+        jnp.int32, (cells, cells), 1
+    )
+    for j, diag in enumerate((d0, d1, d2, d3)):
+        row = n ^ j
+        local = owner[rows * w + row] - cols * n
+        held = jnp.logical_and(local >= 0, local < cols)
+        kept[...] = jnp.where(lower, diag[...].astype(jnp.float32), 0.0).astype(jnp.bfloat16)
+        term = lax.dot_general(
+            noise[jnp.clip(local, 0, cols - 1)],
+            kept[...],
+            (((1,), (1,)), ((), ())),
+            preferred_element_type=jnp.float32,
+        )
+        own[row] = jnp.where(held, term, 0.0)
     for c in range(cols):
         if c % each == 0:
             arrived(c // each)
@@ -81,28 +106,15 @@
             part = product[:, p * rank_max : (p + 1) * rank_max]
             part = jnp.where(keep[p : p + 1, span] > 0, part, 0.0)
             coeff[p, :, span] = part.astype(jnp.bfloat16)
-    sums = []
     for p in range(rows):
-        total = 0.0
+        total = own[p]
         for i, span in enumerate(halves(cols)):
-            arrived(len(chunks) + 2 * p + i)
+            arrived(CHUNKS + 2 * p + i)
             total = total + jnp.dot(
                 coeff[p, :, rank_max * span.start : rank_max * span.stop],
                 left[p, span].reshape(cols // 2 * rank_max, cells),
                 preferred_element_type=jnp.float32,
             )
-        sums.append(total)
-    arrived(len(copies) - 1)
-    for p, total in enumerate(sums):
-        local = owner[rows * w + p] - cols * n
-        held = jnp.logical_and(local >= 0, local < cols)
-        term = lax.dot_general(
-            noise[jnp.clip(local, 0, cols - 1)],
-            diag[p].astype(jnp.bfloat16),
-            (((1,), (1,)), ((), ())),
-            preferred_element_type=jnp.float32,
-        )
-        total = total + jnp.where(held, term, 0.0)
         for g in range(members // 8):
             for h in range(2):
                 turned[pl.ds(64 * g + 2 * p + h, 8, stride=8), :] = total[
@@ -227,23 +239,27 @@
 
     slabs = [[z * group * narrow + i for i in range(group * narrow)] for z in range(narrow)]
 
+    swap = [
+        ((z * group + r) * narrow + b, (b * group + r) * narrow + z)
+        for z in range(narrow)
+        for r in range(group)
+        for b in range(narrow)
+    ]
+    planes = [[z * group + r for r in range(group)] for z in range(narrow)]
+
+    with jax.named_scope("diagonal_gather"):
+        own_diag = diagonal_tile_blocks[0]
+        diags = [own_diag] + [
+            lax.ppermute(own_diag, "narrow", [(i, i ^ j) for i in range(narrow)])
+            for j in range(1, narrow)
+        ]
+
     with jax.named_scope("noise_gather"):
-        pieces = [
-            lax.ppermute(
-                noise,
-                BOTH,
-                [
-                    ((z * group + r) * narrow + b, (b * group + (r ^ j)) * narrow + z)
-                    for z in range(narrow)
-                    for r in range(group)
-                    for b in range(narrow)
-                ],
-            )
-            for j in range(group)
-        ]
-
-    with jax.named_scope("diagonal_gather"):
-        diag = lax.all_gather(jnp.tril(diagonal_tile_blocks).astype(f32), "narrow", tiled=True)
+        swapped = lax.ppermute(noise, BOTH, swap)
+        sending = jnp.broadcast_to(swapped[None], (group, *swapped.shape))
+        columns = lax.all_to_all(
+            sending, "wide", 0, 0, axis_index_groups=planes, tiled=True
+        ).reshape(cols, members, cells)
 
     with jax.named_scope("coefficient_halo"):
         own = jnp.concatenate(
@@ -253,10 +269,12 @@
             ],
             axis=1,
         )
+        sending, own = lax.optimization_barrier((sending, own))
         forward, backward = ring(wide)
         own = jnp.concatenate(
             [lax.ppermute(own, "wide", forward), own, lax.ppermute(own, "wide", backward)], axis=0
         )
+        columns, own = lax.optimization_barrier((columns, own))
 
     with jax.named_scope("factors"):
         keep = (
@@ -265,25 +283,27 @@
         partial_sums = pl.pallas_call(
             factor_kernel,
             out_shape=pltpu.VMEM((devices, 8, 128), f32),
-            in_specs=specs(SMEM, VMEM, pltpu.HBM, pltpu.HBM, pltpu.HBM, *[VMEM] * group),
+            in_specs=specs(SMEM, VMEM, VMEM, *[pltpu.HBM] * 3, *[VMEM] * (narrow - 1)),
             out_specs=pl.BlockSpec(memory_space=VMEM),
             scratch_shapes=[
-                pltpu.VMEM((cols, members, cells), noise.dtype),
                 pltpu.VMEM((rows, members, cols * rank_max), jnp.bfloat16),
                 pltpu.VMEM((members * 8, 128), f32),
+                pltpu.VMEM((rows, members, cells), f32),
                 pltpu.VMEM(right_factors.shape, right_factors.dtype),
                 pltpu.VMEM(left_factors.shape, left_factors.dtype),
-                pltpu.VMEM(diag.shape, f32),
-                pltpu.SemaphoreType.DMA((group + 2 * rows + 1,)),
+                pltpu.VMEM(own_diag.shape, own_diag.dtype),
+                pltpu.VMEM(own_diag.shape, own_diag.dtype),
+                pltpu.SemaphoreType.DMA((CHUNKS + 2 * rows + 1,)),
             ],
-            compiler_params=limit(28),
+            compiler_params=limit(24),
         )(
-            owner,
+            far(owner),
             near(keep),
+            near(columns),
             far(right_factors),
             far(left_factors),
-            far(diag),
-            *[near(piece) for piece in pieces],
+            far(diags[0]),
+            *[near(d) for d in diags[1:]],
         )
 
     with jax.named_scope("member_exchange"):

time: 100 us -> 80.7 us (0.81)
  between operations: 13.5 us -> 0.13 us
  starting transfers between devices: 45.6 us -> 36 us
  waiting for transfers between devices: 25 us -> 30.7 us
  Pallas kernels: 13.2 us -> 11.5 us
    ppermute x8 -> x4, starting transfers between devices: 21 us -> 6.8 us  [the longest x1 3.74 us: per_device(): swapped = lax.ppermute(noise, BOTH, swap)]
    all_to_all x1, waiting for transfers between devices: 0.01 us -> 13.8 us  [per_device(): got = lax.all_to_all(partial_sums, BOTH, 0, 0, tiled=True)]
    ppermute x8 -> x4, waiting for transfers between devices: 9.59 us -> 1.53 us  [the longest x1 1.52 us: per_device(): swapped = lax.ppermute(noise, BOTH, swap)]
    all_to_all x0 -> x1, starting transfers between devices: none -> 6.7 us  [per_device(): lax.all_to_all(sending, 'wide', 0, 0, axis_index_groups=planes, tiled=True)]
    all_to_all x1, starting transfers between devices: 9.57 us -> 5.9 us  [per_device(): got = lax.all_to_all(partial_sums, BOTH, 0, 0, tiled=True)]
    ppermute x1, starting transfers between devices: 8.01 us -> 10.5 us  [per_device(): lax.ppermute(own, 'wide', backward)]
    pallas_call x1, Pallas kernels: 10.8 us -> 9.09 us  [per_device(): pl.pallas_call(factor_kernel, out_shape=pltpu.VMEM((devices, 8, 128), f32...]
    convert_element_type x1 -> x0, other arithmetic: 1.65 us -> none  [per_device(): jnp.tril(diagonal_tile_blocks).astype(f32)]
  transfers between devices with their start and end apart: 15 -> 11, of which waited for: 8 -> 7; matrix products, arithmetic and copies ran while one was open for 0% -> 2% of each run, Pallas kernels for 0% -> 0%
where the time goes in v5:
time: 80.7 us; the launch traced here: 80.3 us
  starting transfers between devices  36 us (45%)
  waiting for transfers between devices  30.7 us (38%)
  Pallas kernels  11.5 us (14%)
  local copies, waits for them, and re-layouts  0.94 us (1%)
  other arithmetic  0.9 us (1%)
    all_to_all x1, waiting for transfers between devices, per_device(): got = lax.all_to_all(partial_sums, BOTH, 0, 0, tiled=True)  13.8 us
    ppermute x1, starting transfers between devices, per_device(): lax.ppermute(own, 'wide', backward)  10.5 us
    pallas_call x1, Pallas kernels, per_device(): pl.pallas_call(factor_kernel, out_shape=pltpu.VMEM((devices, 8, 128), f32...  9.09 us
    ppermute x1, waiting for transfers between devices, per_device(): lax.ppermute(own, 'wide', forward)  7.42 us
    all_to_all x1, starting transfers between devices, per_device(): lax.all_to_all(sending, 'wide', 0, 0, axis_index_groups=planes, tiled=True)  6.7 us
    all_to_all x1, starting transfers between devices, per_device(): got = lax.all_to_all(partial_sums, BOTH, 0, 0, tiled=True)  5.9 us
    all_to_all x1, starting transfers between devices, per_device(): lax.all_to_all(blocks, BOTH, 0, 0, axis_index_groups=slabs, tiled=True)  4.39 us
    ppermute x1, starting transfers between devices, per_device(): swapped = lax.ppermute(noise, BOTH, swap)  3.74 us
  transfers between devices with their start and end apart: 11, of which 7 were waited for; matrix products, arithmetic and copies ran while one was open for 2% of the time, Pallas kernels for 0%

profile of v5, /device:TPU:1, one launch (start us, length us, event | category | flops | bytes accessed | tf_op | source)
XLA Modules:
  0.0 80.3 jit_solution(7490152373160065103)
XLA Ops:
  0.0 1.4 %collective-permute-start.3 = (bf16[256,256]{1,0:T(8,128)(2,1)}, bf16[256,256]{1,0:T(8,128)(2,1)S(1)}, u32[]{:S(2)}, u32[]{:S(2)}) collective-permute-start(bf16[256,256]{1,0:T(8,128)(2,1)} %bitcast.17), channel_id=1, source_target_pairs={{0,1},{1,0},{2,3},{3,2},{4,5},{5,4},{6,7},{7,6},{8,9},{9,8},{10,11... | collective-permute-start | bytes 393224 | tf_op jit(solution)/shard_map/diagonal_gather/ppermute | solution.py:253
  1.4 1.3 %collective-permute-start.4 = (bf16[256,256]{1,0:T(8,128)(2,1)}, bf16[256,256]{1,0:T(8,128)(2,1)S(1)}, u32[]{:S(2)}, u32[]{:S(2)}) collective-permute-start(bf16[256,256]{1,0:T(8,128)(2,1)} %bitcast.18), channel_id=1, source_target_pairs={{0,2},{1,3},{2,0},{3,1},{4,6},{5,7},{6,4},{7,5},{8,10},{9,11},{10,... | collective-permute-start | bytes 393224 | tf_op jit(solution)/shard_map/diagonal_gather/ppermute | solution.py:253
  2.7 0.3 collective-permute-start.5
  3.1 3.7 %collective-permute-start = (bf16[4,32,256]{2,1,0:T(8,128)(2,1)}, bf16[4,32,256]{2,1,0:T(8,128)(2,1)S(1)}, u32[]{:S(2)}, u32[]{:S(2)}) collective-permute-start(bf16[4,32,256]{2,1,0:T(8,128)(2,1)} %param.10), channel_id=1, source_target_pairs={{0,0},{1,32},{2,64},{3,96},{4,4},{5,36},{6,68},{7,100},{8,8},{9,40... | collective-permute-start | bytes 196616 | tf_op jit(solution)/shard_map/noise_gather/ppermute | solution.py:258
  6.8 0.1 broadcast_bitcast_fusion
  6.9 0.7 negate_select_fusion
  7.7 0.1 pad_maximum_fusion.1
  7.7 1.5 %collective-permute-done = bf16[4,32,256]{2,1,0:T(8,128)(2,1)S(1)} collective-permute-done((bf16[4,32,256]{2,1,0:T(8,128)(2,1)}, bf16[4,32,256]{2,1,0:T(8,128)(2,1)S(1)}, u32[]{:S(2)}, u32[]{:S(2)}) %collective-permute-start) | collective-permute-done | bytes 65568 | tf_op jit(solution)/shard_map/noise_gather/ppermute | solution.py:258
  9.3 0.9 %broadcast_in_dim.4 = bf16[8,4,32,256]{3,2,1,0:T(8,128)(2,1)} broadcast(bf16[4,32,256]{2,1,0:T(8,128)(2,1)S(1)} %collective-permute-done), dimensions={1,2,3} | broadcast | bytes 589824 | tf_op jit(solution)/shard_map/noise_gather/broadcast_in_dim | solution.py:259
  10.1 6.7 %all-to-all-start = ((bf16[8,4,32,256]{3,2,1,0:T(8,128)(2,1)}), bf16[8,4,32,256]{3,2,1,0:T(8,128)(2,1)S(1)}, u32[]{:S(2)}, u32[]{:S(2)}) async-start(bf16[8,4,32,256]{3,2,1,0:T(8,128)(2,1)} %broadcast_in_dim.4), calls=%async_computation | async-start | bytes 1048576 | tf_op jit(solution)/shard_map/noise_gather/all_to_all | solution.py:260
  16.8 10.5 %collective-permute-start.2 = (f32[4,128]{1,0:T(4,128)S(1)}, f32[4,128]{1,0:T(4,128)S(1)}, u32[]{:S(2)}, u32[]{:S(2)}) collective-permute-start(f32[4,128]{1,0:T(4,128)S(1)} %pad_maximum_fusion.1), channel_id=1, source_target_pairs={{4,0},{8,4},{12,8},{16,12},{20,16},{24,20},{28,24},{32,28},{36,32}... | collective-permute-start | bytes 6152 | tf_op jit(solution)/shard_map/coefficient_halo/ppermute | solution.py:275
  27.4 0.7 collective-permute-done.2
  28.1 7.4 %collective-permute-done.1 = f32[4,128]{1,0:T(4,128)S(1)} collective-permute-done((f32[4,128]{1,0:T(4,128)S(1)}, f32[4,128]{1,0:T(4,128)S(1)}, u32[]{:S(2)}, u32[]{:S(2)}) %collective-permute-start.1) | collective-permute-done | bytes 2080 | tf_op jit(solution)/shard_map/coefficient_halo/ppermute | solution.py:275
  35.6 9.1 %factors.1 = f32[128,8,128]{2,1,0:T(8,128)} custom-call(s32[128]{0:T(128)} %owner.1, f32[4,4096]{1,0:T(4,128)S(1)} %fusion.keep, bf16[32,32,256]{2,1,0:T(8,128)(2,1)S(1)} %bitcast.14, bf16[4,32,128,256]{3,2,1,0:T(8,128)(2,1)} %right_far.1, bf16[4,32,128,256]{3,2,1,0:T(8,128)(2,1)} %left_far.1, bf16[256,256]{1,0:T(8,128)(2,1)} %bitcast.20, ...), custom_call_target="tpu_custom_call" | custom-call | tf_op jit(solution)/shard_map/factors/pallas_call | solution.py:283
  44.7 5.9 %all-to-all-start.1 = ((f32[128,8,128]{2,1,0:T(8,128)}), f32[128,8,128]{2,1,0:T(8,128)S(1)}, u32[]{:S(2)}, u32[]{:S(2)}) async-start(f32[128,8,128]{2,1,0:T(8,128)} %factors.1), calls=%async_computation.1 | async-start | bytes 1048576 | tf_op jit(solution)/shard_map/member_exchange/all_to_all | solution.py:310
  50.6 13.8 %all-to-all-done.1 = f32[128,8,128]{2,1,0:T(8,128)S(1)} async-done(((f32[128,8,128]{2,1,0:T(8,128)}), f32[128,8,128]{2,1,0:T(8,128)S(1)}, u32[]{:S(2)}, u32[]{:S(2)}) %all-to-all-start.1) | async-done | bytes 524320 | tf_op jit(solution)/shard_map/member_exchange/all_to_all | solution.py:310
  64.4 1.3 %place.1 = f32[32,16,128]{2,1,0:T(8,128)} custom-call(s32[1,128]{1,0:T(1,128)S(1)} %and_bitcast_fusion.place, f32[32,4,8,128]{3,2,1,0:T(8,128)S(1)} %bitcast.15), custom_call_target="tpu_custom_call" | custom-call | tf_op jit(solution)/shard_map/place/pallas_call | solution.py:332
  65.7 4.4 %all-to-all-start.2 = ((f32[32,16,128]{2,1,0:T(8,128)}), f32[32,16,128]{2,1,0:T(8,128)S(1)}, u32[]{:S(2)}, u32[]{:S(2)}) async-start(f32[32,16,128]{2,1,0:T(8,128)} %place.1), calls=%async_computation.2 | async-start | bytes 524288 | tf_op jit(solution)/shard_map/block_exchange/all_to_all | solution.py:342
  70.1 1.7 %collective-permute-start.6 = (f32[12,128]{1,0:T(8,128)S(1)}, f32[12,128]{1,0:T(8,128)S(1)}, u32[]{:S(2)}, u32[]{:S(2)}) collective-permute-start(f32[12,128]{1,0:T(8,128)S(1)} %pad_maximum_fusion.own), channel_id=1, source_target_pairs={{0,1},{1,2},{2,3},{3,0},{4,5},{5,6},{6,7},{7,4},{8,9},{9,10},{10,1... | collective-permute-start | bytes 18440 | tf_op jit(solution)/shard_map/weights/ppermute | solution.py:322
  71.8 1.6 %collective-permute-done.6.low = f32[12,128]{1,0:T(8,128)S(1)} collective-permute-done((f32[12,128]{1,0:T(8,128)S(1)}, f32[12,128]{1,0:T(8,128)S(1)}, u32[]{:S(2)}, u32[]{:S(2)}) %collective-permute-start.6) | collective-permute-done | bytes 6176 | tf_op jit(solution)/shard_map/weights/ppermute | solution.py:322
  73.4 2.4 %collective-permute-done.7.high = f32[12,128]{1,0:T(8,128)S(1)} collective-permute-done((f32[12,128]{1,0:T(8,128)S(1)}, f32[12,128]{1,0:T(8,128)S(1)}, u32[]{:S(2)}, u32[]{:S(2)}) %collective-permute-start.7) | collective-permute-done | bytes 6176 | tf_op jit(solution)/shard_map/weights/ppermute | solution.py:324
  75.8 0.1 weights.1.weight
  75.9 3.3 %all-to-all-done.2 = f32[32,16,128]{2,1,0:T(8,128)S(1)} async-done(((f32[32,16,128]{2,1,0:T(8,128)}), f32[32,16,128]{2,1,0:T(8,128)S(1)}, u32[]{:S(2)}, u32[]{:S(2)}) %all-to-all-start.2) | async-done | bytes 262176 | tf_op jit(solution)/shard_map/block_exchange/all_to_all | solution.py:342
  79.2 1.1 %stencil.1 = f32[32,4,64]{2,1,0:T(4,128)} custom-call(f32[5,12,8,128]{3,2,1,0:T(8,128)S(1)} %weights.1.weight, f32[512,128]{1,0:T(8,128)S(1)} %bitcast.16), custom_call_target="tpu_custom_call" | custom-call | tf_op jit(solution)/shard_map/stencil/pallas_call | solution.py:345
  (14 shorter events, 0.1 us)
Async XLA Ops:
  0.0 6.8 %copy-start = (s32[4,32]{1,0:T(4,128)S(1)}, s32[4,32]{1,0:T(4,128)}, u32[]{:S(2)}) copy-start(s32[4,32]{1,0:T(4,128)} %param.14) | copy-start | bytes 1540
  0.0 35.5 %collective-permute-start.3 = (bf16[256,256]{1,0:T(8,128)(2,1)}, bf16[256,256]{1,0:T(8,128)(2,1)S(1)}, u32[]{:S(2)}, u32[]{:S(2)}) collective-permute-start(bf16[256,256]{1,0:T(8,128)(2,1)} %bitcast.17), channel_id=1, source_target_pairs={{0,1},{1,0},{2,3},{3,2},{4,5},{5,4},{6,7},{7,6},{8,9},{9,8},{10,11... | collective-permute-start | bytes 393224 | tf_op jit(solution)/shard_map/diagonal_gather/ppermute | solution.py:253
  1.4 34.1 %collective-permute-start.4 = (bf16[256,256]{1,0:T(8,128)(2,1)}, bf16[256,256]{1,0:T(8,128)(2,1)S(1)}, u32[]{:S(2)}, u32[]{:S(2)}) collective-permute-start(bf16[256,256]{1,0:T(8,128)(2,1)} %bitcast.18), channel_id=1, source_target_pairs={{0,2},{1,3},{2,0},{3,1},{4,6},{5,7},{6,4},{7,5},{8,10},{9,11},{10,... | collective-permute-start | bytes 393224 | tf_op jit(solution)/shard_map/diagonal_gather/ppermute | solution.py:253
  2.7 32.8 %collective-permute-start.5 = (bf16[256,256]{1,0:T(8,128)(2,1)}, bf16[256,256]{1,0:T(8,128)(2,1)S(1)}, u32[]{:S(2)}, u32[]{:S(2)}) collective-permute-start(bf16[256,256]{1,0:T(8,128)(2,1)} %bitcast.19), channel_id=1, source_target_pairs={{0,3},{1,2},{2,1},{3,0},{4,7},{5,6},{6,5},{7,4},{8,11},{9,10},{10,... | collective-permute-start | bytes 393224 | tf_op jit(solution)/shard_map/diagonal_gather/ppermute | solution.py:253
  3.1 6.2 %collective-permute-start = (bf16[4,32,256]{2,1,0:T(8,128)(2,1)}, bf16[4,32,256]{2,1,0:T(8,128)(2,1)S(1)}, u32[]{:S(2)}, u32[]{:S(2)}) collective-permute-start(bf16[4,32,256]{2,1,0:T(8,128)(2,1)} %param.10), channel_id=1, source_target_pairs={{0,0},{1,32},{2,64},{3,96},{4,4},{5,36},{6,68},{7,100},{8,8},{9,40... | collective-permute-start | bytes 196616 | tf_op jit(solution)/shard_map/noise_gather/ppermute | solution.py:258
  10.1 25.4 %all-to-all-start = ((bf16[8,4,32,256]{3,2,1,0:T(8,128)(2,1)}), bf16[8,4,32,256]{3,2,1,0:T(8,128)(2,1)S(1)}, u32[]{:S(2)}, u32[]{:S(2)}) async-start(bf16[8,4,32,256]{3,2,1,0:T(8,128)(2,1)} %broadcast_in_dim.4), calls=%async_computation | async-start | bytes 1048576 | tf_op jit(solution)/shard_map/noise_gather/all_to_all | solution.py:260
  16.8 11.3 %collective-permute-start.2 = (f32[4,128]{1,0:T(4,128)S(1)}, f32[4,128]{1,0:T(4,128)S(1)}, u32[]{:S(2)}, u32[]{:S(2)}) collective-permute-start(f32[4,128]{1,0:T(4,128)S(1)} %pad_maximum_fusion.1), channel_id=1, source_target_pairs={{4,0},{8,4},{12,8},{16,12},{20,16},{24,20},{28,24},{32,28},{36,32}... | collective-permute-start | bytes 6152 | tf_op jit(solution)/shard_map/coefficient_halo/ppermute | solution.py:275
  27.3 8.2 %collective-permute-start.1 = (f32[4,128]{1,0:T(4,128)S(1)}, f32[4,128]{1,0:T(4,128)S(1)}, u32[]{:S(2)}, u32[]{:S(2)}) collective-permute-start(f32[4,128]{1,0:T(4,128)S(1)} %pad_maximum_fusion.1), channel_id=1, source_target_pairs={{0,4},{4,8},{8,12},{12,16},{16,20},{20,24},{24,28},{28,32},{32,36}... | collective-permute-start | bytes 6152 | tf_op jit(solution)/shard_map/coefficient_halo/ppermute | solution.py:275
  35.5 15.1 %copy-start.1 = (s32[128]{0:T(128)S(1)}, s32[128]{0:T(128)}, u32[]{:S(2)}) copy-start(s32[128]{0:T(128)} %owner.1) | copy-start | bytes 1540
  44.7 19.8 %all-to-all-start.1 = ((f32[128,8,128]{2,1,0:T(8,128)}), f32[128,8,128]{2,1,0:T(8,128)S(1)}, u32[]{:S(2)}, u32[]{:S(2)}) async-start(f32[128,8,128]{2,1,0:T(8,128)} %factors.1), calls=%async_computation.1 | async-start | bytes 1048576 | tf_op jit(solution)/shard_map/member_exchange/all_to_all | solution.py:310
  65.7 13.5 %all-to-all-start.2 = ((f32[32,16,128]{2,1,0:T(8,128)}), f32[32,16,128]{2,1,0:T(8,128)S(1)}, u32[]{:S(2)}, u32[]{:S(2)}) async-start(f32[32,16,128]{2,1,0:T(8,128)} %place.1), calls=%async_computation.2 | async-start | bytes 524288 | tf_op jit(solution)/shard_map/block_exchange/all_to_all | solution.py:342
  70.1 3.3 %collective-permute-start.6 = (f32[12,128]{1,0:T(8,128)S(1)}, f32[12,128]{1,0:T(8,128)S(1)}, u32[]{:S(2)}, u32[]{:S(2)}) collective-permute-start(f32[12,128]{1,0:T(8,128)S(1)} %pad_maximum_fusion.own), channel_id=1, source_target_pairs={{0,1},{1,2},{2,3},{3,0},{4,5},{5,6},{6,7},{7,4},{8,9},{9,10},{10,1... | collective-permute-start | bytes 18440 | tf_op jit(solution)/shard_map/weights/ppermute | solution.py:322
  71.8 4.0 %collective-permute-start.7 = (f32[12,128]{1,0:T(8,128)S(1)}, f32[12,128]{1,0:T(8,128)S(1)}, u32[]{:S(2)}, u32[]{:S(2)}) collective-permute-start(f32[12,128]{1,0:T(8,128)S(1)} %pad_maximum_fusion.own), channel_id=1, source_target_pairs={{1,0},{2,1},{3,2},{0,3},{5,4},{6,5},{7,6},{4,7},{9,8},{10,9},{11,1... | collective-permute-start | bytes 18440 | tf_op jit(solution)/shard_map/weights/ppermute | solution.py:324

commit v6 on v5

--- a/solution.py
+++ b/solution.py
@@ -37,6 +37,24 @@
     return slice(0, count // 2), slice(count // 2, count)
 
 
+def diagonal_term(owner, noise, block, row, cols, rows):
+    local = owner[rows * lax.axis_index("wide") + row] - cols * lax.axis_index("narrow")
+    held = jnp.logical_and(local >= 0, local < cols)
+    term = lax.dot_general(
+        noise[jnp.clip(local, 0, cols - 1)],
+        block[...],
+        (((1,), (1,)), ((), ())),
+        preferred_element_type=jnp.float32,
+    )
+    return jnp.where(held, term, 0.0)
+
+
+def lower_part(block):
+    shape = block.shape
+    lower = lax.broadcasted_iota(jnp.int32, shape, 0) >= lax.broadcasted_iota(jnp.int32, shape, 1)
+    return jnp.where(lower, block.astype(jnp.float32), 0.0).astype(jnp.bfloat16)
+
+
 def factor_kernel(
     owner,
     keep,
@@ -44,56 +62,32 @@
     right_far,
     left_far,
     diag_far,
-    d1,
-    d2,
-    d3,
     out,
     coeff,
-    turned,
     own,
     right,
     left,
-    d0,
+    diag,
     kept,
     done,
 ):
     rows, cols, rank_max, cells = right.shape
-    members = noise.shape[1]
     each = cols // CHUNKS
     chunks = [slice(i * each, (i + 1) * each) for i in range(CHUNKS)]
     pairs = [(right_far.at[:, span], right.at[:, span]) for span in chunks]
     pairs += [(left_far.at[p, span], left.at[p, span]) for p in range(rows) for span in halves(cols)]
-    pairs += [(diag_far, d0)]
+    pairs += [(diag_far, diag)]
     copies = [
         pltpu.make_async_copy(source, target, done.at[i])
         for i, (source, target) in enumerate(pairs)
     ]
-    copies[-1].start()
     for copy in copies[:CHUNKS]:
         copy.start()
-    copies[-1].wait()
 
     def arrived(i):
         copies[i].wait()
-        if i + CHUNKS < len(copies) - 1:
-            copies[i + CHUNKS].start()
-
-    w, n = lax.axis_index("wide"), lax.axis_index("narrow")
-    lower = lax.broadcasted_iota(jnp.int32, (cells, cells), 0) >= lax.broadcasted_iota(
-        jnp.int32, (cells, cells), 1
-    )
-    for j, diag in enumerate((d0, d1, d2, d3)):
-        row = n ^ j
-        local = owner[rows * w + row] - cols * n
-        held = jnp.logical_and(local >= 0, local < cols)
-        kept[...] = jnp.where(lower, diag[...].astype(jnp.float32), 0.0).astype(jnp.bfloat16)
-        term = lax.dot_general(
-            noise[jnp.clip(local, 0, cols - 1)],
-            kept[...],
-            (((1,), (1,)), ((), ())),
-            preferred_element_type=jnp.float32,
-        )
-        own[row] = jnp.where(held, term, 0.0)
+        copies[i + CHUNKS].start()
+
     for c in range(cols):
         if c % each == 0:
             arrived(c // each)
@@ -106,19 +100,40 @@
             part = product[:, p * rank_max : (p + 1) * rank_max]
             part = jnp.where(keep[p : p + 1, span] > 0, part, 0.0)
             coeff[p, :, span] = part.astype(jnp.bfloat16)
+        if c == cols - 1:
+            copies[CHUNKS + 2 * rows].start()
+            own[...] = jnp.zeros_like(own)
     for p in range(rows):
-        total = own[p]
+        total = 0.0
         for i, span in enumerate(halves(cols)):
-            arrived(CHUNKS + 2 * p + i)
+            copies[CHUNKS + 2 * p + i].wait()
+            if p == 0 and i == 1:
+                copies[CHUNKS + 2 * rows].wait()
+                kept[...] = lower_part(diag[...])
+                row = lax.axis_index("narrow")
+                own[row] = diagonal_term(owner, noise, kept, row, cols, rows)
             total = total + jnp.dot(
                 coeff[p, :, rank_max * span.start : rank_max * span.stop],
                 left[p, span].reshape(cols // 2 * rank_max, cells),
                 preferred_element_type=jnp.float32,
             )
+        out[p] = total + own[p]
+
+
+def finish_kernel(owner, noise, sums, d1, d2, d3, out, turned, own, kept):
+    rows, members, cells = sums.shape
+    cols = noise.shape[0]
+    own[...] = sums[...]
+    for j, diag in enumerate((d1, d2, d3)):
+        kept[j] = lower_part(diag[...])
+    for j in range(rows - 1):
+        row = lax.axis_index("narrow") ^ (j + 1)
+        own[row] = own[row] + diagonal_term(owner, noise, kept.at[j], row, cols, rows)
+    for p in range(rows):
         for g in range(members // 8):
             for h in range(2):
-                turned[pl.ds(64 * g + 2 * p + h, 8, stride=8), :] = total[
-                    8 * g : 8 * g + 8, 128 * h : 128 * h + 128
+                turned[pl.ds(64 * g + 2 * p + h, 8, stride=8), :] = own[
+                    p, 8 * g : 8 * g + 8, 128 * h : 128 * h + 128
                 ]
     for d in range(out.shape[0]):
         member = d % members
@@ -247,13 +262,6 @@
     ]
     planes = [[z * group + r for r in range(group)] for z in range(narrow)]
 
-    with jax.named_scope("diagonal_gather"):
-        own_diag = diagonal_tile_blocks[0]
-        diags = [own_diag] + [
-            lax.ppermute(own_diag, "narrow", [(i, i ^ j) for i in range(narrow)])
-            for j in range(1, narrow)
-        ]
-
     with jax.named_scope("noise_gather"):
         swapped = lax.ppermute(noise, BOTH, swap)
         sending = jnp.broadcast_to(swapped[None], (group, *swapped.shape))
@@ -269,46 +277,65 @@
             ],
             axis=1,
         )
-        sending, own = lax.optimization_barrier((sending, own))
+        columns, own, own_diag = lax.optimization_barrier((columns, own, diagonal_tile_blocks[0]))
         forward, backward = ring(wide)
         own = jnp.concatenate(
             [lax.ppermute(own, "wide", forward), own, lax.ppermute(own, "wide", backward)], axis=0
         )
-        columns, own = lax.optimization_barrier((columns, own))
+
+    with jax.named_scope("diagonal_gather"):
+        diags = [
+            lax.ppermute(own_diag, "narrow", [(i, i ^ j) for i in range(narrow)])
+            for j in range(1, narrow)
+        ]
 
     with jax.named_scope("factors"):
         keep = (
             jnp.arange(rank_max, dtype=jnp.int32)[None, None, :] < ranks[:, :, None]
         ).astype(f32).reshape(rows, cols * rank_max)
-        partial_sums = pl.pallas_call(
+        columns = near(columns)
+        sums = pl.pallas_call(
             factor_kernel,
-            out_shape=pltpu.VMEM((devices, 8, 128), f32),
-            in_specs=specs(SMEM, VMEM, VMEM, *[pltpu.HBM] * 3, *[VMEM] * (narrow - 1)),
+            out_shape=pltpu.VMEM((rows, members, cells), f32),
+            in_specs=specs(SMEM, VMEM, VMEM, *[pltpu.HBM] * 3),
             out_specs=pl.BlockSpec(memory_space=VMEM),
             scratch_shapes=[
                 pltpu.VMEM((rows, members, cols * rank_max), jnp.bfloat16),
-                pltpu.VMEM((members * 8, 128), f32),
                 pltpu.VMEM((rows, members, cells), f32),
                 pltpu.VMEM(right_factors.shape, right_factors.dtype),
                 pltpu.VMEM(left_factors.shape, left_factors.dtype),
-                pltpu.VMEM(own_diag.shape, own_diag.dtype),
-                pltpu.VMEM(own_diag.shape, own_diag.dtype),
+                pltpu.VMEM((cells, cells), own_diag.dtype),
+                pltpu.VMEM((cells, cells), own_diag.dtype),
                 pltpu.SemaphoreType.DMA((CHUNKS + 2 * rows + 1,)),
             ],
             compiler_params=limit(24),
+            cost_estimate=pl.CostEstimate(
+                flops=0, transcendentals=0, bytes_accessed=4 * right_factors.size
+            ),
         )(
             far(owner),
             near(keep),
-            near(columns),
+            columns,
             far(right_factors),
             far(left_factors),
-            far(diags[0]),
-            *[near(d) for d in diags[1:]],
-        )
+            far(diagonal_tile_blocks[0]),
+        )
+        partial_sums = pl.pallas_call(
+            finish_kernel,
+            out_shape=pltpu.VMEM((devices, 8, 128), f32),
+            in_specs=specs(SMEM, *[VMEM] * 5),
+            out_specs=pl.BlockSpec(memory_space=VMEM),
+            scratch_shapes=[
+                pltpu.VMEM((members * 8, 128), f32),
+                pltpu.VMEM((rows, members, cells), f32),
+                pltpu.VMEM((narrow - 1, cells, cells), own_diag.dtype),
+            ],
+            compiler_params=limit(4),
+        )(far(owner), columns, sums, *[near(d) for d in diags])
 
     with jax.named_scope("member_exchange"):
+        partial_sums, own = lax.optimization_barrier((partial_sums, own))
         got = lax.all_to_all(partial_sums, BOTH, 0, 0, tiled=True)
-        got, own = lax.optimization_barrier((got, own))
 
     with jax.named_scope("weights"):
         forward, backward = ring(narrow)

time: 80.7 us -> 86.3 us (1.069)
  starting transfers between devices: 36 us -> 38.7 us
  Pallas kernels: 11.5 us -> 14 us
    all_to_all x1, waiting for transfers between devices: 0.01 us -> 8.15 us  [per_device(): lax.all_to_all(sending, 'wide', 0, 0, axis_index_groups=planes, tiled=True)]
    ppermute x1, waiting for transfers between devices: 7.42 us -> 0.01 us  [per_device(): lax.ppermute(own, 'wide', forward)]
    ppermute x1, starting transfers between devices: 10.5 us -> 4.58 us  [per_device(): lax.ppermute(own, 'wide', backward)]
    ppermute x3, starting transfers between devices: 3.06 us -> 7.15 us  [per_device(): lax.ppermute(own_diag, 'narrow', [(i, i ^ j) for i in range(narrow)])]
    all_to_all x1, starting transfers between devices: 5.9 us -> 9.12 us  [per_device(): got = lax.all_to_all(partial_sums, BOTH, 0, 0, tiled=True)]
    pallas_call x1 -> x2, Pallas kernels: 9.09 us -> 11.6 us  [the longest x1 9.77 us: per_device(): pl.pallas_call(factor_kernel, out_shape=pltpu.VMEM((rows, members, cells)...]
    ppermute x1, starting transfers between devices: 3.74 us -> 5.05 us  [per_device(): swapped = lax.ppermute(noise, BOTH, swap)]
  transfers between devices with their start and end apart: 11 -> 11, of which waited for: 7 -> 6; matrix products, arithmetic and copies ran while one was open for 2% -> 1% of each run, Pallas kernels for 0% -> 11%
where the time goes in v6:
time: 86.3 us; the launch traced here: 85.9 us
  starting transfers between devices  38.7 us (45%)
  waiting for transfers between devices  31.3 us (36%)
  Pallas kernels  14 us (16%)
  local copies, waits for them, and re-layouts  0.94 us (1%)
  other arithmetic  0.89 us (1%)
    all_to_all x1, waiting for transfers between devices, per_device(): got = lax.all_to_all(partial_sums, BOTH, 0, 0, tiled=True)  13.7 us
    pallas_call x1, Pallas kernels, per_device(): pl.pallas_call(factor_kernel, out_shape=pltpu.VMEM((rows, members, cells)...  9.77 us
    all_to_all x1, starting transfers between devices, per_device(): got = lax.all_to_all(partial_sums, BOTH, 0, 0, tiled=True)  9.12 us
    all_to_all x1, waiting for transfers between devices, per_device(): lax.all_to_all(sending, 'wide', 0, 0, axis_index_groups=planes, tiled=True)  8.15 us
    ppermute x3, starting transfers between devices, per_device(): lax.ppermute(own_diag, 'narrow', [(i, i ^ j) for i in range(narrow)])  7.15 us
    all_to_all x1, starting transfers between devices, per_device(): lax.all_to_all(sending, 'wide', 0, 0, axis_index_groups=planes, tiled=True)  6.65 us
    ppermute x1, starting transfers between devices, per_device(): swapped = lax.ppermute(noise, BOTH, swap)  5.05 us
    ppermute x1, starting transfers between devices, per_device(): lax.ppermute(own, 'wide', backward)  4.58 us
  transfers between devices with their start and end apart: 11, of which 6 were waited for; matrix products, arithmetic and copies ran while one was open for 1% of the time, Pallas kernels for 11%

profile of v6, /device:TPU:1, one launch (start us, length us, event | category | flops | bytes accessed | tf_op | source)
XLA Modules:
  0.0 85.9 jit_solution(1724933032977689382)
XLA Ops:
  0.0 5.1 %collective-permute-start = (bf16[4,32,256]{2,1,0:T(8,128)(2,1)}, bf16[4,32,256]{2,1,0:T(8,128)(2,1)S(1)}, u32[]{:S(2)}, u32[]{:S(2)}) collective-permute-start(bf16[4,32,256]{2,1,0:T(8,128)(2,1)} %param.10), channel_id=1, source_target_pairs={{0,0},{1,32},{2,64},{3,96},{4,4},{5,36},{6,68},{7,100},{8,8},{9,40... | collective-permute-start | bytes 196616 | tf_op jit(solution)/shard_map/noise_gather/ppermute | solution.py:266
  5.1 2.1 %collective-permute-done = bf16[4,32,256]{2,1,0:T(8,128)(2,1)S(1)} collective-permute-done((bf16[4,32,256]{2,1,0:T(8,128)(2,1)}, bf16[4,32,256]{2,1,0:T(8,128)(2,1)S(1)}, u32[]{:S(2)}, u32[]{:S(2)}) %collective-permute-start) | collective-permute-done | bytes 65568 | tf_op jit(solution)/shard_map/noise_gather/ppermute | solution.py:266
  7.2 0.9 broadcast_in_dim.4
  8.1 6.7 %all-to-all-start = ((bf16[8,4,32,256]{3,2,1,0:T(8,128)(2,1)}), bf16[8,4,32,256]{3,2,1,0:T(8,128)(2,1)S(1)}, u32[]{:S(2)}, u32[]{:S(2)}) async-start(bf16[8,4,32,256]{3,2,1,0:T(8,128)(2,1)} %broadcast_in_dim.4), calls=%async_computation | async-start | bytes 1048576 | tf_op jit(solution)/shard_map/noise_gather/all_to_all | solution.py:268
  14.7 0.7 negate_select_fusion
  15.5 0.1 pad_maximum_fusion.1
  15.5 0.1 broadcast_bitcast_fusion
  15.6 8.2 %all-to-all-done = bf16[8,4,32,256]{3,2,1,0:T(8,128)(2,1)S(1)} async-done(((bf16[8,4,32,256]{3,2,1,0:T(8,128)(2,1)}), bf16[8,4,32,256]{3,2,1,0:T(8,128)(2,1)S(1)}, u32[]{:S(2)}, u32[]{:S(2)}) %all-to-all-start) | async-done | bytes 524320 | tf_op jit(solution)/shard_map/noise_gather/all_to_all | solution.py:268
  23.8 7.1 %collective-permute-start.2 = (bf16[256,256]{1,0:T(8,128)(2,1)}, bf16[256,256]{1,0:T(8,128)(2,1)S(1)}, u32[]{:S(2)}, u32[]{:S(2)}) collective-permute-start(bf16[256,256]{1,0:T(8,128)(2,1)} %bitcast.19), channel_id=1, source_target_pairs={{0,2},{1,3},{2,0},{3,1},{4,6},{5,7},{6,4},{7,5},{8,10},{9,11},{10,... | collective-permute-start | bytes 393224 | tf_op jit(solution)/shard_map/diagonal_gather/ppermute | solution.py:288
  30.9 4.6 %collective-permute-start.5 = (f32[4,128]{1,0:T(4,128)S(1)}, f32[4,128]{1,0:T(4,128)S(1)}, u32[]{:S(2)}, u32[]{:S(2)}) collective-permute-start(f32[4,128]{1,0:T(4,128)S(1)} %pad_maximum_fusion.1), channel_id=1, source_target_pairs={{4,0},{8,4},{12,8},{16,12},{20,16},{24,20},{28,24},{32,28},{36,32}... | collective-permute-start | bytes 6152 | tf_op jit(solution)/shard_map/coefficient_halo/ppermute | solution.py:283
  35.5 0.1 fusion.keep
  35.6 0.0 copy-start.1
  35.6 9.8 %factors.2.sums = f32[4,32,256]{2,1,0:T(8,128)S(1)} custom-call(s32[128]{0:T(128)} %owner.3, f32[4,4096]{1,0:T(4,128)S(1)} %fusion.keep, bf16[32,32,256]{2,1,0:T(8,128)(2,1)S(1)} %bitcast.14, bf16[4,32,128,256]{3,2,1,0:T(8,128)(2,1)} %right_far.1, bf16[4,32,128,256]{3,2,1,0:T(8,128)(2,1)} %left_far.1, bf16[256,256]{1,0:T(8,128)(2,1)} %bitcast.21), custom_call_target="tpu_custom_call" | custom-call | bytes 16777216 | tf_op jit(solution)/shard_map/factors/pallas_call | solution.py:297
  45.4 1.8 %factors.3 = f32[128,8,128]{2,1,0:T(8,128)} custom-call(s32[128]{0:T(128)} %owner.3, bf16[32,32,256]{2,1,0:T(8,128)(2,1)S(1)} %bitcast.15, f32[4,32,256]{2,1,0:T(8,128)S(1)} %factors.2.sums, bf16[256,256]{1,0:T(8,128)(2,1)S(1)} %collective-permute-done.1.d1, bf16[256,256]{1,0:T(8,128)(2,1)S(1)} %collective-permute-done.2.d2, ...), custom_call_target="tpu_custom_call" | custom-call | tf_op jit(solution)/shard_map/factors/pallas_call | solution.py:323
  47.2 9.1 %all-to-all-start.1 = ((f32[128,8,128]{2,1,0:T(8,128)}), f32[128,8,128]{2,1,0:T(8,128)S(1)}, u32[]{:S(2)}, u32[]{:S(2)}) async-start(f32[128,8,128]{2,1,0:T(8,128)} %factors.3), calls=%async_computation.1 | async-start | bytes 1048576 | tf_op jit(solution)/shard_map/member_exchange/all_to_all | solution.py:338
  56.4 13.7 %all-to-all-done.1 = f32[128,8,128]{2,1,0:T(8,128)S(1)} async-done(((f32[128,8,128]{2,1,0:T(8,128)}), f32[128,8,128]{2,1,0:T(8,128)S(1)}, u32[]{:S(2)}, u32[]{:S(2)}) %all-to-all-start.1) | async-done | bytes 524320 | tf_op jit(solution)/shard_map/member_exchange/all_to_all | solution.py:338
  70.0 1.3 %place.1 = f32[32,16,128]{2,1,0:T(8,128)} custom-call(s32[1,128]{1,0:T(1,128)S(1)} %and_bitcast_fusion.place, f32[32,4,8,128]{3,2,1,0:T(8,128)S(1)} %bitcast.16), custom_call_target="tpu_custom_call" | custom-call | tf_op jit(solution)/shard_map/place/pallas_call | solution.py:359
  71.3 4.4 %all-to-all-start.2 = ((f32[32,16,128]{2,1,0:T(8,128)}), f32[32,16,128]{2,1,0:T(8,128)S(1)}, u32[]{:S(2)}, u32[]{:S(2)}) async-start(f32[32,16,128]{2,1,0:T(8,128)} %place.1), calls=%async_computation.2 | async-start | bytes 524288 | tf_op jit(solution)/shard_map/block_exchange/all_to_all | solution.py:369
  75.7 1.7 %collective-permute-start.6 = (f32[12,128]{1,0:T(8,128)S(1)}, f32[12,128]{1,0:T(8,128)S(1)}, u32[]{:S(2)}, u32[]{:S(2)}) collective-permute-start(f32[12,128]{1,0:T(8,128)S(1)} %pad_maximum_fusion.own), channel_id=1, source_target_pairs={{0,1},{1,2},{2,3},{3,0},{4,5},{5,6},{6,7},{7,4},{8,9},{9,10},{10,1... | collective-permute-start | bytes 18440 | tf_op jit(solution)/shard_map/weights/ppermute | solution.py:349
  77.4 1.6 %collective-permute-done.6.low = f32[12,128]{1,0:T(8,128)S(1)} collective-permute-done((f32[12,128]{1,0:T(8,128)S(1)}, f32[12,128]{1,0:T(8,128)S(1)}, u32[]{:S(2)}, u32[]{:S(2)}) %collective-permute-start.6) | collective-permute-done | bytes 6176 | tf_op jit(solution)/shard_map/weights/ppermute | solution.py:349
  79.0 2.4 %collective-permute-done.7.high = f32[12,128]{1,0:T(8,128)S(1)} collective-permute-done((f32[12,128]{1,0:T(8,128)S(1)}, f32[12,128]{1,0:T(8,128)S(1)}, u32[]{:S(2)}, u32[]{:S(2)}) %collective-permute-start.7) | collective-permute-done | bytes 6176 | tf_op jit(solution)/shard_map/weights/ppermute | solution.py:351
  81.4 0.1 weights.1.weight
  81.5 3.3 %all-to-all-done.2 = f32[32,16,128]{2,1,0:T(8,128)S(1)} async-done(((f32[32,16,128]{2,1,0:T(8,128)}), f32[32,16,128]{2,1,0:T(8,128)S(1)}, u32[]{:S(2)}, u32[]{:S(2)}) %all-to-all-start.2) | async-done | bytes 262176 | tf_op jit(solution)/shard_map/block_exchange/all_to_all | solution.py:369
  84.8 1.1 %stencil.1 = f32[32,4,64]{2,1,0:T(4,128)} custom-call(f32[5,12,8,128]{3,2,1,0:T(8,128)S(1)} %weights.1.weight, f32[512,128]{1,0:T(8,128)S(1)} %bitcast.17), custom_call_target="tpu_custom_call" | custom-call | tf_op jit(solution)/shard_map/stencil/pallas_call | solution.py:372
  (15 shorter events, 0.1 us)
Async XLA Ops:
  0.0 15.5 %copy-start = (s32[4,32]{1,0:T(4,128)S(1)}, s32[4,32]{1,0:T(4,128)}, u32[]{:S(2)}) copy-start(s32[4,32]{1,0:T(4,128)} %param.14) | copy-start | bytes 1540
  0.0 7.2 %collective-permute-start = (bf16[4,32,256]{2,1,0:T(8,128)(2,1)}, bf16[4,32,256]{2,1,0:T(8,128)(2,1)S(1)}, u32[]{:S(2)}, u32[]{:S(2)}) collective-permute-start(bf16[4,32,256]{2,1,0:T(8,128)(2,1)} %param.10), channel_id=1, source_target_pairs={{0,0},{1,32},{2,64},{3,96},{4,4},{5,36},{6,68},{7,100},{8,8},{9,40... | collective-permute-start | bytes 196616 | tf_op jit(solution)/shard_map/noise_gather/ppermute | solution.py:266
  8.1 15.7 %all-to-all-start = ((bf16[8,4,32,256]{3,2,1,0:T(8,128)(2,1)}), bf16[8,4,32,256]{3,2,1,0:T(8,128)(2,1)S(1)}, u32[]{:S(2)}, u32[]{:S(2)}) async-start(bf16[8,4,32,256]{3,2,1,0:T(8,128)(2,1)} %broadcast_in_dim.4), calls=%async_computation | async-start | bytes 1048576 | tf_op jit(solution)/shard_map/noise_gather/all_to_all | solution.py:268
  23.8 21.6 %collective-permute-start.1 = (bf16[256,256]{1,0:T(8,128)(2,1)}, bf16[256,256]{1,0:T(8,128)(2,1)S(1)}, u32[]{:S(2)}, u32[]{:S(2)}) collective-permute-start(bf16[256,256]{1,0:T(8,128)(2,1)} %bitcast.18), channel_id=1, source_target_pairs={{0,1},{1,0},{2,3},{3,2},{4,5},{5,4},{6,7},{7,6},{8,9},{9,8},{10,11... | collective-permute-start | bytes 393224 | tf_op jit(solution)/shard_map/diagonal_gather/ppermute | solution.py:288
  23.8 21.6 %collective-permute-start.2 = (bf16[256,256]{1,0:T(8,128)(2,1)}, bf16[256,256]{1,0:T(8,128)(2,1)S(1)}, u32[]{:S(2)}, u32[]{:S(2)}) collective-permute-start(bf16[256,256]{1,0:T(8,128)(2,1)} %bitcast.19), channel_id=1, source_target_pairs={{0,2},{1,3},{2,0},{3,1},{4,6},{5,7},{6,4},{7,5},{8,10},{9,11},{10,... | collective-permute-start | bytes 393224 | tf_op jit(solution)/shard_map/diagonal_gather/ppermute | solution.py:288
  30.9 14.5 %collective-permute-start.3 = (bf16[256,256]{1,0:T(8,128)(2,1)}, bf16[256,256]{1,0:T(8,128)(2,1)S(1)}, u32[]{:S(2)}, u32[]{:S(2)}) collective-permute-start(bf16[256,256]{1,0:T(8,128)(2,1)} %bitcast.20), channel_id=1, source_target_pairs={{0,3},{1,2},{2,1},{3,0},{4,7},{5,6},{6,5},{7,4},{8,11},{9,10},{10,... | collective-permute-start | bytes 393224 | tf_op jit(solution)/shard_map/diagonal_gather/ppermute | solution.py:288
  30.9 14.4 %collective-permute-start.5 = (f32[4,128]{1,0:T(4,128)S(1)}, f32[4,128]{1,0:T(4,128)S(1)}, u32[]{:S(2)}, u32[]{:S(2)}) collective-permute-start(f32[4,128]{1,0:T(4,128)S(1)} %pad_maximum_fusion.1), channel_id=1, source_target_pairs={{4,0},{8,4},{12,8},{16,12},{20,16},{24,20},{28,24},{32,28},{36,32}... | collective-permute-start | bytes 6152 | tf_op jit(solution)/shard_map/coefficient_halo/ppermute | solution.py:283
  35.5 9.9 %collective-permute-start.4 = (f32[4,128]{1,0:T(4,128)S(1)}, f32[4,128]{1,0:T(4,128)S(1)}, u32[]{:S(2)}, u32[]{:S(2)}) collective-permute-start(f32[4,128]{1,0:T(4,128)S(1)} %pad_maximum_fusion.1), channel_id=1, source_target_pairs={{0,4},{4,8},{8,12},{12,16},{16,20},{20,24},{24,28},{28,32},{32,36}... | collective-permute-start | bytes 6152 | tf_op jit(solution)/shard_map/coefficient_halo/ppermute | solution.py:283
  35.6 20.8 %copy-start.1 = (s32[128]{0:T(128)S(1)}, s32[128]{0:T(128)}, u32[]{:S(2)}) copy-start(s32[128]{0:T(128)} %owner.3) | copy-start | bytes 1540
  47.2 22.9 %all-to-all-start.1 = ((f32[128,8,128]{2,1,0:T(8,128)}), f32[128,8,128]{2,1,0:T(8,128)S(1)}, u32[]{:S(2)}, u32[]{:S(2)}) async-start(f32[128,8,128]{2,1,0:T(8,128)} %factors.3), calls=%async_computation.1 | async-start | bytes 1048576 | tf_op jit(solution)/shard_map/member_exchange/all_to_all | solution.py:338
  71.3 13.5 %all-to-all-start.2 = ((f32[32,16,128]{2,1,0:T(8,128)}), f32[32,16,128]{2,1,0:T(8,128)S(1)}, u32[]{:S(2)}, u32[]{:S(2)}) async-start(f32[32,16,128]{2,1,0:T(8,128)} %place.1), calls=%async_computation.2 | async-start | bytes 524288 | tf_op jit(solution)/shard_map/block_exchange/all_to_all | solution.py:369
  75.7 3.3 %collective-permute-start.6 = (f32[12,128]{1,0:T(8,128)S(1)}, f32[12,128]{1,0:T(8,128)S(1)}, u32[]{:S(2)}, u32[]{:S(2)}) collective-permute-start(f32[12,128]{1,0:T(8,128)S(1)} %pad_maximum_fusion.own), channel_id=1, source_target_pairs={{0,1},{1,2},{2,3},{3,0},{4,5},{5,6},{6,7},{7,4},{8,9},{9,10},{10,1... | collective-permute-start | bytes 18440 | tf_op jit(solution)/shard_map/weights/ppermute | solution.py:349
  77.4 4.0 %collective-permute-start.7 = (f32[12,128]{1,0:T(8,128)S(1)}, f32[12,128]{1,0:T(8,128)S(1)}, u32[]{:S(2)}, u32[]{:S(2)}) collective-permute-start(f32[12,128]{1,0:T(8,128)S(1)} %pad_maximum_fusion.own), channel_id=1, source_target_pairs={{1,0},{2,1},{3,2},{0,3},{5,4},{6,5},{7,6},{4,7},{9,8},{10,9},{11,1... | collective-permute-start | bytes 18440 | tf_op jit(solution)/shard_map/weights/ppermute | solution.py:351

commit v7 on v5

--- a/solution.py
+++ b/solution.py
@@ -239,27 +239,30 @@
 
     slabs = [[z * group * narrow + i for i in range(group * narrow)] for z in range(narrow)]
 
+    def server(plane_to, source):
+        return source ^ (3, 1, 0, 2)[(plane_to - source) % 4]
+
     swap = [
-        ((z * group + r) * narrow + b, (b * group + r) * narrow + z)
+        ((s * group + r) * narrow + server(z, s), (z * group + r) * narrow + s)
+        for s in range(narrow)
+        for r in range(group)
         for z in range(narrow)
-        for r in range(group)
-        for b in range(narrow)
     ]
     planes = [[z * group + r for r in range(group)] for z in range(narrow)]
 
     with jax.named_scope("diagonal_gather"):
         own_diag = diagonal_tile_blocks[0]
-        diags = [own_diag] + [
-            lax.ppermute(own_diag, "narrow", [(i, i ^ j) for i in range(narrow)])
-            for j in range(1, narrow)
+        beside, across = [[(i, i ^ j) for i in range(narrow)] for j in (1, 2)]
+        opposite = lax.ppermute(own_diag, "narrow", across)
+        diags = [
+            own_diag,
+            lax.ppermute(own_diag, "narrow", beside),
+            opposite,
+            lax.ppermute(opposite, "narrow", beside),
         ]
 
     with jax.named_scope("noise_gather"):
         swapped = lax.ppermute(noise, BOTH, swap)
-        sending = jnp.broadcast_to(swapped[None], (group, *swapped.shape))
-        columns = lax.all_to_all(
-            sending, "wide", 0, 0, axis_index_groups=planes, tiled=True
-        ).reshape(cols, members, cells)
 
     with jax.named_scope("coefficient_halo"):
         own = jnp.concatenate(
@@ -269,12 +272,17 @@
             ],
             axis=1,
         )
-        sending, own = lax.optimization_barrier((sending, own))
         forward, backward = ring(wide)
         own = jnp.concatenate(
             [lax.ppermute(own, "wide", forward), own, lax.ppermute(own, "wide", backward)], axis=0
         )
-        columns, own = lax.optimization_barrier((columns, own))
+
+    with jax.named_scope("noise_gather"):
+        sending = jnp.broadcast_to(swapped[None], (group, *swapped.shape))
+        sending, own = lax.optimization_barrier((sending, own))
+        columns = lax.all_to_all(
+            sending, "wide", 0, 0, axis_index_groups=planes, tiled=True
+        ).reshape(cols, members, cells)
 
     with jax.named_scope("factors"):
         keep = (

time: 80.7 us -> 81 us (level)
  waiting for transfers between devices: 30.7 us -> 37.2 us
  starting transfers between devices: 36 us -> 29.7 us
    all_to_all x1, waiting for transfers between devices: 0.01 us -> 8.56 us  [per_device(): lax.all_to_all(sending, 'wide', 0, 0, axis_index_groups=planes, tiled=True)]
    ppermute x1, starting transfers between devices: 3.74 us -> 0.01 us  [per_device(): swapped = lax.ppermute(noise, BOTH, swap)]
    all_to_all x1, starting transfers between devices: 6.7 us -> 4.58 us  [per_device(): lax.all_to_all(sending, 'wide', 0, 0, axis_index_groups=planes, tiled=True)]
    ppermute x1, waiting for transfers between devices: 1.52 us -> 0.01 us  [per_device(): swapped = lax.ppermute(noise, BOTH, swap)]
    all_to_all x1, starting transfers between devices: 5.9 us -> 7.19 us  [per_device(): got = lax.all_to_all(partial_sums, BOTH, 0, 0, tiled=True)]
    ppermute x1, starting transfers between devices: 10.5 us -> 9.5 us  [per_device(): lax.ppermute(own, 'wide', backward)]
    ppermute x3, waiting for transfers between devices: 0.01 us -> 0.92 us  [the longest x1 0.92 us: per_device(): lax.ppermute(opposite, 'narrow', beside)]
  transfers between devices with their start and end apart: 11 -> 11, of which waited for: 7 -> 7; matrix products, arithmetic and copies ran while one was open for 2% -> 1% of each run, Pallas kernels for 0% -> 0%
where the time goes in v7:
time: 81 us; the launch traced here: 80.6 us
  waiting for transfers between devices  37.2 us (46%)
  starting transfers between devices  29.7 us (37%)
  Pallas kernels  11.6 us (14%)
  other arithmetic  0.97 us (1%)
  local copies, waits for them, and re-layouts  0.94 us (1%)
    all_to_all x1, waiting for transfers between devices, per_device(): got = lax.all_to_all(partial_sums, BOTH, 0, 0, tiled=True)  13.7 us
    ppermute x1, starting transfers between devices, per_device(): lax.ppermute(own, 'wide', backward)  9.5 us
    pallas_call x1, Pallas kernels, per_device(): pl.pallas_call(factor_kernel, out_shape=pltpu.VMEM((devices, 8, 128), f32...  9.19 us
    all_to_all x1, waiting for transfers between devices, per_device(): lax.all_to_all(sending, 'wide', 0, 0, axis_index_groups=planes, tiled=True)  8.56 us
    all_to_all x1, starting transfers between devices, per_device(): got = lax.all_to_all(partial_sums, BOTH, 0, 0, tiled=True)  7.19 us
    ppermute x1, waiting for transfers between devices, per_device(): lax.ppermute(own, 'wide', forward)  6.79 us
    all_to_all x1, starting transfers between devices, per_device(): lax.all_to_all(sending, 'wide', 0, 0, axis_index_groups=planes, tiled=True)  4.58 us
    all_to_all x1, starting transfers between devices, per_device(): lax.all_to_all(blocks, BOTH, 0, 0, axis_index_groups=slabs, tiled=True)  4.39 us
  transfers between devices with their start and end apart: 11, of which 7 were waited for; matrix products, arithmetic and copies ran while one was open for 1% of the time, Pallas kernels for 0%

profile of v7, /device:TPU:1, one launch (start us, length us, event | category | flops | bytes accessed | tf_op | source)
XLA Modules:
  0.0 80.6 jit_solution(12335606841099927434)
XLA Ops:
  0.0 0.7 negate_select_fusion
  0.8 0.1 pad_maximum_fusion.1
  0.8 9.5 %collective-permute-start.2 = (f32[4,128]{1,0:T(4,128)S(1)}, f32[4,128]{1,0:T(4,128)S(1)}, u32[]{:S(2)}, u32[]{:S(2)}) collective-permute-start(f32[4,128]{1,0:T(4,128)S(1)} %pad_maximum_fusion.1), channel_id=1, source_target_pairs={{4,0},{8,4},{12,8},{16,12},{20,16},{24,20},{28,24},{32,28},{36,32}... | collective-permute-start | bytes 6152 | tf_op jit(solution)/shard_map/coefficient_halo/ppermute | solution.py:277
  10.3 1.0 %collective-permute-start.3 = (bf16[256,256]{1,0:T(8,128)(2,1)}, bf16[256,256]{1,0:T(8,128)(2,1)S(1)}, u32[]{:S(2)}, u32[]{:S(2)}) collective-permute-start(bf16[256,256]{1,0:T(8,128)(2,1)} %bitcast.17), channel_id=1, source_target_pairs={{0,1},{1,0},{2,3},{3,2},{4,5},{5,4},{6,7},{7,6},{8,9},{9,8},{10,11... | collective-permute-start | bytes 393224 | tf_op jit(solution)/shard_map/diagonal_gather/ppermute | solution.py:259
  11.3 0.3 collective-permute-start.4
  11.6 0.1 broadcast_bitcast_fusion
  11.7 6.8 %collective-permute-done.1 = f32[4,128]{1,0:T(4,128)S(1)} collective-permute-done((f32[4,128]{1,0:T(4,128)S(1)}, f32[4,128]{1,0:T(4,128)S(1)}, u32[]{:S(2)}, u32[]{:S(2)}) %collective-permute-start.1) | collective-permute-done | bytes 2080 | tf_op jit(solution)/shard_map/coefficient_halo/ppermute | solution.py:277
  18.5 0.1 pad_maximum_fusion.own
  18.6 0.9 %broadcast_in_dim.4 = bf16[8,4,32,256]{3,2,1,0:T(8,128)(2,1)} broadcast(bf16[4,32,256]{2,1,0:T(8,128)(2,1)S(1)} %collective-permute-done), dimensions={1,2,3} | broadcast | bytes 589824 | tf_op jit(solution)/shard_map/noise_gather/broadcast_in_dim | solution.py:281
  19.4 4.6 %all-to-all-start = ((bf16[8,4,32,256]{3,2,1,0:T(8,128)(2,1)}), bf16[8,4,32,256]{3,2,1,0:T(8,128)(2,1)S(1)}, u32[]{:S(2)}, u32[]{:S(2)}) async-start(bf16[8,4,32,256]{3,2,1,0:T(8,128)(2,1)} %broadcast_in_dim.4), calls=%async_computation | async-start | bytes 1048576 | tf_op jit(solution)/shard_map/noise_gather/all_to_all | solution.py:283
  24.0 1.1 %collective-permute-start.5 = (bf16[256,256]{1,0:T(8,128)(2,1)S(1)}, bf16[256,256]{1,0:T(8,128)(2,1)S(1)}, u32[]{:S(2)}, u32[]{:S(2)}) collective-permute-start(bf16[256,256]{1,0:T(8,128)(2,1)S(1)} %collective-permute-done.4.d2), channel_id=1, source_target_pairs={{0,1},{1,0},{2,3},{3,2},{4,5},{5,4},{6,7},{7,6},{8,9},{9,8},{10,11... | collective-permute-start | bytes 393224 | tf_op jit(solution)/shard_map/diagonal_gather/ppermute | solution.py:261
  25.2 0.9 %collective-permute-done.5.d3 = bf16[256,256]{1,0:T(8,128)(2,1)S(1)} collective-permute-done((bf16[256,256]{1,0:T(8,128)(2,1)S(1)}, bf16[256,256]{1,0:T(8,128)(2,1)S(1)}, u32[]{:S(2)}, u32[]{:S(2)}) %collective-permute-start.5) | collective-permute-done | bytes 131104 | tf_op jit(solution)/shard_map/diagonal_gather/ppermute | solution.py:261
  26.1 8.6 %all-to-all-done = bf16[8,4,32,256]{3,2,1,0:T(8,128)(2,1)S(1)} async-done(((bf16[8,4,32,256]{3,2,1,0:T(8,128)(2,1)}), bf16[8,4,32,256]{3,2,1,0:T(8,128)(2,1)S(1)}, u32[]{:S(2)}, u32[]{:S(2)}) %all-to-all-start) | async-done | bytes 524320 | tf_op jit(solution)/shard_map/noise_gather/all_to_all | solution.py:283
  34.7 9.2 %factors.1 = f32[128,8,128]{2,1,0:T(8,128)} custom-call(s32[128]{0:T(128)} %owner.1, f32[4,4096]{1,0:T(4,128)S(1)} %fusion.keep, bf16[32,32,256]{2,1,0:T(8,128)(2,1)S(1)} %bitcast.14, bf16[4,32,128,256]{3,2,1,0:T(8,128)(2,1)} %right_far.1, bf16[4,32,128,256]{3,2,1,0:T(8,128)(2,1)} %left_far.1, bf16[256,256]{1,0:T(8,128)(2,1)} %bitcast.19, ...), custom_call_target="tpu_custom_call" | custom-call | tf_op jit(solution)/shard_map/factors/pallas_call | solution.py:291
  43.9 7.2 %all-to-all-start.1 = ((f32[128,8,128]{2,1,0:T(8,128)}), f32[128,8,128]{2,1,0:T(8,128)S(1)}, u32[]{:S(2)}, u32[]{:S(2)}) async-start(f32[128,8,128]{2,1,0:T(8,128)} %factors.1), calls=%async_computation.1 | async-start | bytes 1048576 | tf_op jit(solution)/shard_map/member_exchange/all_to_all | solution.py:318
  51.1 13.7 %all-to-all-done.1 = f32[128,8,128]{2,1,0:T(8,128)S(1)} async-done(((f32[128,8,128]{2,1,0:T(8,128)}), f32[128,8,128]{2,1,0:T(8,128)S(1)}, u32[]{:S(2)}, u32[]{:S(2)}) %all-to-all-start.1) | async-done | bytes 524320 | tf_op jit(solution)/shard_map/member_exchange/all_to_all | solution.py:318
  64.8 1.3 %place.1 = f32[32,16,128]{2,1,0:T(8,128)} custom-call(s32[1,128]{1,0:T(1,128)S(1)} %and_bitcast_fusion.place, f32[32,4,8,128]{3,2,1,0:T(8,128)S(1)} %bitcast.15), custom_call_target="tpu_custom_call" | custom-call | tf_op jit(solution)/shard_map/place/pallas_call | solution.py:340
  66.0 4.4 %all-to-all-start.2 = ((f32[32,16,128]{2,1,0:T(8,128)}), f32[32,16,128]{2,1,0:T(8,128)S(1)}, u32[]{:S(2)}, u32[]{:S(2)}) async-start(f32[32,16,128]{2,1,0:T(8,128)} %place.1), calls=%async_computation.2 | async-start | bytes 524288 | tf_op jit(solution)/shard_map/block_exchange/all_to_all | solution.py:350
  70.5 1.7 %collective-permute-start.6 = (f32[12,128]{1,0:T(8,128)S(1)}, f32[12,128]{1,0:T(8,128)S(1)}, u32[]{:S(2)}, u32[]{:S(2)}) collective-permute-start(f32[12,128]{1,0:T(8,128)S(1)} %pad_maximum_fusion.own), channel_id=1, source_target_pairs={{0,1},{1,2},{2,3},{3,0},{4,5},{5,6},{6,7},{7,4},{8,9},{9,10},{10,1... | collective-permute-start | bytes 18440 | tf_op jit(solution)/shard_map/weights/ppermute | solution.py:330
  72.2 1.6 %collective-permute-done.6.low = f32[12,128]{1,0:T(8,128)S(1)} collective-permute-done((f32[12,128]{1,0:T(8,128)S(1)}, f32[12,128]{1,0:T(8,128)S(1)}, u32[]{:S(2)}, u32[]{:S(2)}) %collective-permute-start.6) | collective-permute-done | bytes 6176 | tf_op jit(solution)/shard_map/weights/ppermute | solution.py:330
  73.7 2.4 %collective-permute-done.7.high = f32[12,128]{1,0:T(8,128)S(1)} collective-permute-done((f32[12,128]{1,0:T(8,128)S(1)}, f32[12,128]{1,0:T(8,128)S(1)}, u32[]{:S(2)}, u32[]{:S(2)}) %collective-permute-start.7) | collective-permute-done | bytes 6176 | tf_op jit(solution)/shard_map/weights/ppermute | solution.py:332
  76.2 0.1 weights.1.weight
  76.3 3.3 %all-to-all-done.2 = f32[32,16,128]{2,1,0:T(8,128)S(1)} async-done(((f32[32,16,128]{2,1,0:T(8,128)}), f32[32,16,128]{2,1,0:T(8,128)S(1)}, u32[]{:S(2)}, u32[]{:S(2)}) %all-to-all-start.2) | async-done | bytes 262176 | tf_op jit(solution)/shard_map/block_exchange/all_to_all | solution.py:350
  79.6 1.1 %stencil.1 = f32[32,4,64]{2,1,0:T(4,128)} custom-call(f32[5,12,8,128]{3,2,1,0:T(8,128)S(1)} %weights.1.weight, f32[512,128]{1,0:T(8,128)S(1)} %bitcast.16), custom_call_target="tpu_custom_call" | custom-call | tf_op jit(solution)/shard_map/stencil/pallas_call | solution.py:353
  (14 shorter events, 0.1 us)
Async XLA Ops:
  0.0 11.6 %copy-start = (s32[4,32]{1,0:T(4,128)S(1)}, s32[4,32]{1,0:T(4,128)}, u32[]{:S(2)}) copy-start(s32[4,32]{1,0:T(4,128)} %param.14) | copy-start | bytes 1540
  0.8 10.9 %collective-permute-start.2 = (f32[4,128]{1,0:T(4,128)S(1)}, f32[4,128]{1,0:T(4,128)S(1)}, u32[]{:S(2)}, u32[]{:S(2)}) collective-permute-start(f32[4,128]{1,0:T(4,128)S(1)} %pad_maximum_fusion.1), channel_id=1, source_target_pairs={{4,0},{8,4},{12,8},{16,12},{20,16},{24,20},{28,24},{32,28},{36,32}... | collective-permute-start | bytes 6152 | tf_op jit(solution)/shard_map/coefficient_halo/ppermute | solution.py:277
  10.3 8.2 %collective-permute-start.1 = (f32[4,128]{1,0:T(4,128)S(1)}, f32[4,128]{1,0:T(4,128)S(1)}, u32[]{:S(2)}, u32[]{:S(2)}) collective-permute-start(f32[4,128]{1,0:T(4,128)S(1)} %pad_maximum_fusion.1), channel_id=1, source_target_pairs={{0,4},{4,8},{8,12},{12,16},{16,20},{20,24},{24,28},{28,32},{32,36}... | collective-permute-start | bytes 6152 | tf_op jit(solution)/shard_map/coefficient_halo/ppermute | solution.py:277
  10.3 14.8 %collective-permute-start.3 = (bf16[256,256]{1,0:T(8,128)(2,1)}, bf16[256,256]{1,0:T(8,128)(2,1)S(1)}, u32[]{:S(2)}, u32[]{:S(2)}) collective-permute-start(bf16[256,256]{1,0:T(8,128)(2,1)} %bitcast.17), channel_id=1, source_target_pairs={{0,1},{1,0},{2,3},{3,2},{4,5},{5,4},{6,7},{7,6},{8,9},{9,8},{10,11... | collective-permute-start | bytes 393224 | tf_op jit(solution)/shard_map/diagonal_gather/ppermute | solution.py:259
  11.3 12.7 %collective-permute-start.4 = (bf16[256,256]{1,0:T(8,128)(2,1)}, bf16[256,256]{1,0:T(8,128)(2,1)S(1)}, u32[]{:S(2)}, u32[]{:S(2)}) collective-permute-start(bf16[256,256]{1,0:T(8,128)(2,1)} %bitcast.18), channel_id=1, source_target_pairs={{0,2},{1,3},{2,0},{3,1},{4,6},{5,7},{6,4},{7,5},{8,10},{9,11},{10,... | collective-permute-start | bytes 393224 | tf_op jit(solution)/shard_map/diagonal_gather/ppermute | solution.py:256
  11.6 7.0 %collective-permute-start = (bf16[4,32,256]{2,1,0:T(8,128)(2,1)}, bf16[4,32,256]{2,1,0:T(8,128)(2,1)S(1)}, u32[]{:S(2)}, u32[]{:S(2)}) collective-permute-start(bf16[4,32,256]{2,1,0:T(8,128)(2,1)} %param.10), channel_id=1, source_target_pairs={{3,0},{1,32},{0,64},{2,96},{7,4},{5,36},{4,68},{6,100},{11,8},{9,4... | collective-permute-start | bytes 196616 | tf_op jit(solution)/shard_map/noise_gather/ppermute | solution.py:265
  19.4 15.2 %all-to-all-start = ((bf16[8,4,32,256]{3,2,1,0:T(8,128)(2,1)}), bf16[8,4,32,256]{3,2,1,0:T(8,128)(2,1)S(1)}, u32[]{:S(2)}, u32[]{:S(2)}) async-start(bf16[8,4,32,256]{3,2,1,0:T(8,128)(2,1)} %broadcast_in_dim.4), calls=%async_computation | async-start | bytes 1048576 | tf_op jit(solution)/shard_map/noise_gather/all_to_all | solution.py:283
  24.0 2.1 %collective-permute-start.5 = (bf16[256,256]{1,0:T(8,128)(2,1)S(1)}, bf16[256,256]{1,0:T(8,128)(2,1)S(1)}, u32[]{:S(2)}, u32[]{:S(2)}) collective-permute-start(bf16[256,256]{1,0:T(8,128)(2,1)S(1)} %collective-permute-done.4.d2), channel_id=1, source_target_pairs={{0,1},{1,0},{2,3},{3,2},{4,5},{5,4},{6,7},{7,6},{8,9},{9,8},{10,11... | collective-permute-start | bytes 393224 | tf_op jit(solution)/shard_map/diagonal_gather/ppermute | solution.py:261
  34.7 16.4 %copy-start.1 = (s32[128]{0:T(128)S(1)}, s32[128]{0:T(128)}, u32[]{:S(2)}) copy-start(s32[128]{0:T(128)} %owner.1) | copy-start | bytes 1540
  43.9 20.9 %all-to-all-start.1 = ((f32[128,8,128]{2,1,0:T(8,128)}), f32[128,8,128]{2,1,0:T(8,128)S(1)}, u32[]{:S(2)}, u32[]{:S(2)}) async-start(f32[128,8,128]{2,1,0:T(8,128)} %factors.1), calls=%async_computation.1 | async-start | bytes 1048576 | tf_op jit(solution)/shard_map/member_exchange/all_to_all | solution.py:318
  66.0 13.5 %all-to-all-start.2 = ((f32[32,16,128]{2,1,0:T(8,128)}), f32[32,16,128]{2,1,0:T(8,128)S(1)}, u32[]{:S(2)}, u32[]{:S(2)}) async-start(f32[32,16,128]{2,1,0:T(8,128)} %place.1), calls=%async_computation.2 | async-start | bytes 524288 | tf_op jit(solution)/shard_map/block_exchange/all_to_all | solution.py:350
  70.5 3.3 %collective-permute-start.6 = (f32[12,128]{1,0:T(8,128)S(1)}, f32[12,128]{1,0:T(8,128)S(1)}, u32[]{:S(2)}, u32[]{:S(2)}) collective-permute-start(f32[12,128]{1,0:T(8,128)S(1)} %pad_maximum_fusion.own), channel_id=1, source_target_pairs={{0,1},{1,2},{2,3},{3,0},{4,5},{5,6},{6,7},{7,4},{8,9},{9,10},{10,1... | collective-permute-start | bytes 18440 | tf_op jit(solution)/shard_map/weights/ppermute | solution.py:330
  72.2 4.0 %collective-permute-start.7 = (f32[12,128]{1,0:T(8,128)S(1)}, f32[12,128]{1,0:T(8,128)S(1)}, u32[]{:S(2)}, u32[]{:S(2)}) collective-permute-start(f32[12,128]{1,0:T(8,128)S(1)} %pad_maximum_fusion.own), channel_id=1, source_target_pairs={{1,0},{2,1},{3,2},{0,3},{5,4},{6,5},{7,6},{4,7},{9,8},{10,9},{11,1... | collective-permute-start | bytes 18440 | tf_op jit(solution)/shard_map/weights/ppermute | solution.py:332

commit v8 on v7

--- a/solution.py
+++ b/solution.py
@@ -125,8 +125,7 @@
         out[d] = turned[8 * member : 8 * member + 8, :]
 
 
-def weight_kernel(low, own, high, out):
-    low, own, high = low[...], own[...], high[...]
+def set_weights(low, own, high, weight):
     lane = lax.broadcasted_iota(jnp.int32, low.shape, 1)
     cx, cy = [
         jnp.where(
@@ -143,12 +142,12 @@
         MIXING + jnp.maximum(cy, 0.0),
         MIXING + jnp.maximum(-cy, 0.0),
     )
-    for i, weight in enumerate(weights):
-        for row in range(12):
-            out[i, row] = jnp.broadcast_to(weight[row : row + 1], (8, 128))
-
-
-def place_kernel(place, got, out, summed, window):
+    for i, value in enumerate(weights):
+        for row in range(1, 11):
+            weight[i, row] = jnp.broadcast_to(value[row : row + 1], (8, 128))
+
+
+def place_kernel(place, got, own, forwarded, out, summed, window):
     total = got[:, 0] + got[:, 1] + got[:, 2] + got[:, 3]
     summed[...] = total.reshape(256, 128)
     target = lax.broadcasted_iota(jnp.int32, (64, 128), 0)
@@ -186,15 +185,44 @@
         window[nd] = jnp.where(
             lane < shift, pltpu.roll(first, shift, 1), pltpu.roll(second, shift, 1)
         )
+    first = lax.axis_index("wide") % 8 == 0
+    edge = jnp.where(first, forwarded[0:3], forwarded[1:4])
+    edge = jnp.concatenate([pltpu.roll(edge, 96 - 32 * q, 1) for q in range(4)], axis=0)
+    free = lax.broadcasted_iota(jnp.int32, (12, 128), 1) >= 96
     for txl in range(2):
         for k in range(4):
             start = 12 + 16 * txl + 4 * k
             for nd in range(4):
-                out[txl * 16 + k * 4 + nd] = window[nd, start : start + 16, :]
-
-
-def block_kernel(weight, got, out):
+                d = txl * 16 + k * 4 + nd
+                out[d, 0:12] = jnp.where(free, edge, window[nd, start : start + 12, :])
+                out[d, 12:16] = own[...]
+
+
+def block_kernel(slots, got, out, weight):
     members = out.shape[0]
+    r = lax.axis_index("wide") % 8
+    n = lax.axis_index("narrow")
+    lane = lax.broadcasted_iota(jnp.int32, (3, 128), 1)
+
+    def across(slot):
+        edge = jnp.zeros((3, 128), jnp.float32)
+        for q in range(4):
+            moved = pltpu.roll(slots[slot, 3 * q : 3 * q + 3, :], (32 * q + 32) % 128, 1)
+            edge = jnp.where(lane // 32 == q, moved, edge)
+        return edge
+
+    zero = jnp.zeros((1, 128), jnp.float32)
+    around = []
+    for step in (3, 0, 1):
+        column = (n + step) % 4
+        below = slots[jnp.maximum(r - 1, 0) * 4 + column, 13:16, :]
+        above = slots[jnp.minimum(r + 1, 7) * 4 + column, 12:15, :]
+        below = jnp.where(r == 0, across(28 + column), below)
+        above = jnp.where(r == 7, across(column), above)
+        around.append(
+            jnp.concatenate([zero, below, slots[r * 4 + column, 12:16, :], above, zero], axis=0)
+        )
+    set_weights(*around, weight)
     for start in range(0, members, 8):
         field = {r: got[pl.ds(16 * start + r, 8, stride=16), :] for r in range(12)}
         for step in range(ITERS):
@@ -208,11 +236,6 @@
             }
         for i in range(4):
             out[start : start + 8, i, :] = pltpu.roll(field[4 + i], 112, 1)[:, :64]
-
-
-def ring(count):
-    forward = [(i, (i + 1) % count) for i in range(count)]
-    return forward, [(b, a) for a, b in forward]
 
 
 def per_device(
@@ -272,14 +295,21 @@
             ],
             axis=1,
         )
-        forward, backward = ring(wide)
-        own = jnp.concatenate(
-            [lax.ppermute(own, "wide", forward), own, lax.ppermute(own, "wide", backward)], axis=0
+        last = group - 1
+        forwarded = lax.ppermute(
+            own,
+            BOTH,
+            [
+                ((z * group + r) * narrow + b, ((z + step) % narrow * group + r) * narrow + b)
+                for z in range(narrow)
+                for r, step in ((0, -1), (last, 1))
+                for b in range(narrow)
+            ],
         )
 
     with jax.named_scope("noise_gather"):
         sending = jnp.broadcast_to(swapped[None], (group, *swapped.shape))
-        sending, own = lax.optimization_barrier((sending, own))
+        sending, forwarded = lax.optimization_barrier((sending, forwarded))
         columns = lax.all_to_all(
             sending, "wide", 0, 0, axis_index_groups=planes, tiled=True
         ).reshape(cols, members, cells)
@@ -316,21 +346,6 @@
 
     with jax.named_scope("member_exchange"):
         got = lax.all_to_all(partial_sums, BOTH, 0, 0, tiled=True)
-        got, own = lax.optimization_barrier((got, own))
-
-    with jax.named_scope("weights"):
-        forward, backward = ring(narrow)
-        weight = pl.pallas_call(
-            weight_kernel,
-            out_shape=pltpu.VMEM((5, 12, 8, 128), f32),
-            in_specs=specs(VMEM, VMEM, VMEM),
-            out_specs=pl.BlockSpec(memory_space=VMEM),
-            compiler_params=limit(2),
-        )(
-            near(lax.ppermute(own, "narrow", forward)),
-            near(own),
-            near(lax.ppermute(own, "narrow", backward)),
-        )
 
     with jax.named_scope("place"):
         bits = [(owner >> b) & 1 for b in range(7)]
@@ -340,11 +355,11 @@
         blocks = pl.pallas_call(
             place_kernel,
             out_shape=pltpu.VMEM((members, 16, 128), f32),
-            in_specs=specs(VMEM, VMEM),
+            in_specs=specs(*[VMEM] * 4),
             out_specs=pl.BlockSpec(memory_space=VMEM),
             scratch_shapes=[pltpu.VMEM((256, 128), f32), pltpu.VMEM((4, 64, 128), f32)],
             compiler_params=limit(4),
-        )(near(place[None]), near(got.reshape(wide, narrow, 8, 128)))
+        )(near(place[None]), near(got.reshape(wide, narrow, 8, 128)), near(own), near(forwarded))
 
     with jax.named_scope("block_exchange"):
         mine = lax.all_to_all(blocks, BOTH, 0, 0, axis_index_groups=slabs, tiled=True)
@@ -355,8 +370,9 @@
             out_shape=jax.ShapeDtypeStruct((members, 4, 64), f32),
             in_specs=specs(VMEM, VMEM),
             out_specs=pl.BlockSpec(memory_space=VMEM),
+            scratch_shapes=[pltpu.VMEM((5, 12, 8, 128), f32)],
             compiler_params=limit(4),
-        )(weight, near(mine.reshape(members * 16, 128)))
+        )(near(mine), near(mine.reshape(members * 16, 128)))
 
 
 def solution(mesh):

time: 81 us -> 74.5 us (0.920)
  blocking collectives: 0 us -> 13 us
  waiting for transfers between devices: 37.2 us -> 25 us
  starting transfers between devices: 29.7 us -> 23.4 us
    all_to_all x0 -> x1, blocking collectives: none -> 13 us  [per_device(): lax.all_to_all(blocks, BOTH, 0, 0, axis_index_groups=slabs, tiled=True)]
    ppermute x4 -> x1, waiting for transfers between devices: 10.8 us -> 0.53 us  [per_device(): lax.ppermute(own, BOTH, [((z * group + r) * narrow + b, ((z + step) % nar...]
    ppermute x4 -> x1, starting transfers between devices: 11.2 us -> 5.65 us  [per_device(): lax.ppermute(own, BOTH, [((z * group + r) * narrow + b, ((z + step) % nar...]
    all_to_all x1 -> x0, starting transfers between devices: 4.39 us -> none  [per_device(): lax.all_to_all(blocks, BOTH, 0, 0, axis_index_groups=slabs, tiled=True)]
    ppermute x1, waiting for transfers between devices: 0.01 us -> 3.59 us  [per_device(): swapped = lax.ppermute(noise, BOTH, swap)]
    all_to_all x1 -> x0, waiting for transfers between devices: 3.29 us -> none  [per_device(): lax.all_to_all(blocks, BOTH, 0, 0, axis_index_groups=slabs, tiled=True)]
    all_to_all x1, waiting for transfers between devices: 8.56 us -> 6.25 us  [per_device(): lax.all_to_all(sending, 'wide', 0, 0, axis_index_groups=planes, tiled=True)]
    ppermute x1, starting transfers between devices: 0.31 us -> 2.04 us  [per_device(): opposite = lax.ppermute(own_diag, 'narrow', across)]
  transfers between devices with their start and end apart: 11 -> 7, of which waited for: 7 -> 5; matrix products, arithmetic and copies ran while one was open for 1% -> 2% of each run, Pallas kernels for 0% -> 0%
where the time goes in v8:
time: 74.5 us; the launch traced here: 74.2 us
  waiting for transfers between devices  25 us (34%)
  starting transfers between devices  23.4 us (31%)
  blocking collectives  13 us (17%)
  Pallas kernels  10.9 us (15%)
  local copies, waits for them, and re-layouts  0.93 us (1%)
  other arithmetic  0.88 us (1%)
    all_to_all x1, waiting for transfers between devices, per_device(): got = lax.all_to_all(partial_sums, BOTH, 0, 0, tiled=True)  13.7 us
    all_to_all x1, blocking collectives, per_device(): lax.all_to_all(blocks, BOTH, 0, 0, axis_index_groups=slabs, tiled=True)  13 us
    pallas_call x1, Pallas kernels, per_device(): pl.pallas_call(factor_kernel, out_shape=pltpu.VMEM((devices, 8, 128), f32...  9.18 us
    all_to_all x1, starting transfers between devices, per_device(): got = lax.all_to_all(partial_sums, BOTH, 0, 0, tiled=True)  8.39 us
    all_to_all x1, waiting for transfers between devices, per_device(): lax.all_to_all(sending, 'wide', 0, 0, axis_index_groups=planes, tiled=True)  6.25 us
    ppermute x1, starting transfers between devices, per_device(): lax.ppermute(own, BOTH, [((z * group + r) * narrow + b, ((z + step) % nar...  5.65 us
    all_to_all x1, starting transfers between devices, per_device(): lax.all_to_all(sending, 'wide', 0, 0, axis_index_groups=planes, tiled=True)  4.09 us
    ppermute x1, waiting for transfers between devices, per_device(): swapped = lax.ppermute(noise, BOTH, swap)  3.59 us
  transfers between devices with their start and end apart: 7, of which 5 were waited for; matrix products, arithmetic and copies ran while one was open for 2% of the time, Pallas kernels for 0%

profile of v8, /device:TPU:1, one launch (start us, length us, event | category | flops | bytes accessed | tf_op | source)
XLA Modules:
  0.0 74.2 jit_solution(8016914797659701999)
XLA Ops:
  0.0 2.0 %collective-permute-start.3 = (bf16[256,256]{1,0:T(8,128)(2,1)}, bf16[256,256]{1,0:T(8,128)(2,1)S(1)}, u32[]{:S(2)}, u32[]{:S(2)}) collective-permute-start(bf16[256,256]{1,0:T(8,128)(2,1)} %bitcast.17), channel_id=1, source_target_pairs={{0,2},{1,3},{2,0},{3,1},{4,6},{5,7},{6,4},{7,5},{8,10},{9,11},{10,... | collective-permute-start | bytes 393224 | tf_op jit(solution)/shard_map/diagonal_gather/ppermute | solution.py:279
  2.0 1.0 %collective-permute-start.2 = (bf16[256,256]{1,0:T(8,128)(2,1)}, bf16[256,256]{1,0:T(8,128)(2,1)S(1)}, u32[]{:S(2)}, u32[]{:S(2)}) collective-permute-start(bf16[256,256]{1,0:T(8,128)(2,1)} %bitcast.18), channel_id=1, source_target_pairs={{0,1},{1,0},{2,3},{3,2},{4,5},{5,4},{6,7},{7,6},{8,9},{9,8},{10,11... | collective-permute-start | bytes 393224 | tf_op jit(solution)/shard_map/diagonal_gather/ppermute | solution.py:282
  3.0 0.7 negate_select_fusion
  3.7 0.1 pad_maximum_fusion.own
  3.8 5.7 %collective-permute-start.1 = (f32[4,128]{1,0:T(4,128)S(1)}, f32[4,128]{1,0:T(4,128)S(1)}, u32[]{:S(2)}, u32[]{:S(2)}) collective-permute-start(f32[4,128]{1,0:T(4,128)S(1)} %pad_maximum_fusion.own), channel_id=1, source_target_pairs={{0,96},{1,97},{2,98},{3,99},{28,60},{29,61},{30,62},{31,63},{32,0}... | collective-permute-start | bytes 6152 | tf_op jit(solution)/shard_map/coefficient_halo/ppermute | solution.py:299
  9.5 0.1 collective-permute-start
  9.6 0.0 copy-done
  9.6 0.1 broadcast_bitcast_fusion
  9.7 0.5 collective-permute-done.1.forwarded
  10.2 3.6 %collective-permute-done = bf16[4,32,256]{2,1,0:T(8,128)(2,1)S(1)} collective-permute-done((bf16[4,32,256]{2,1,0:T(8,128)(2,1)}, bf16[4,32,256]{2,1,0:T(8,128)(2,1)S(1)}, u32[]{:S(2)}, u32[]{:S(2)}) %collective-permute-start) | collective-permute-done | bytes 65568 | tf_op jit(solution)/shard_map/noise_gather/ppermute | solution.py:288
  13.8 0.8 %broadcast_in_dim.5 = bf16[8,4,32,256]{3,2,1,0:T(8,128)(2,1)} broadcast(bf16[4,32,256]{2,1,0:T(8,128)(2,1)S(1)} %collective-permute-done), dimensions={1,2,3} | broadcast | bytes 589824 | tf_op jit(solution)/shard_map/noise_gather/broadcast_in_dim | solution.py:311
  14.6 4.1 %all-to-all-start = ((bf16[8,4,32,256]{3,2,1,0:T(8,128)(2,1)}), bf16[8,4,32,256]{3,2,1,0:T(8,128)(2,1)S(1)}, u32[]{:S(2)}, u32[]{:S(2)}) async-start(bf16[8,4,32,256]{3,2,1,0:T(8,128)(2,1)} %broadcast_in_dim.5), calls=%async_computation | async-start | bytes 1048576 | tf_op jit(solution)/shard_map/noise_gather/all_to_all | solution.py:313
  18.7 0.0 collective-permute-done.3.d2
  18.7 2.2 %collective-permute-start.4 = (bf16[256,256]{1,0:T(8,128)(2,1)S(1)}, bf16[256,256]{1,0:T(8,128)(2,1)S(1)}, u32[]{:S(2)}, u32[]{:S(2)}) collective-permute-start(bf16[256,256]{1,0:T(8,128)(2,1)S(1)} %collective-permute-done.3.d2), channel_id=1, source_target_pairs={{0,1},{1,0},{2,3},{3,2},{4,5},{5,4},{6,7},{7,6},{8,9},{9,8},{10,11... | collective-permute-start | bytes 393224 | tf_op jit(solution)/shard_map/diagonal_gather/ppermute | solution.py:284
  20.9 0.1 fusion.keep
  21.0 0.0 collective-permute-done.2.d1
  21.0 0.9 %collective-permute-done.4.d3 = bf16[256,256]{1,0:T(8,128)(2,1)S(1)} collective-permute-done((bf16[256,256]{1,0:T(8,128)(2,1)S(1)}, bf16[256,256]{1,0:T(8,128)(2,1)S(1)}, u32[]{:S(2)}, u32[]{:S(2)}) %collective-permute-start.4) | collective-permute-done | bytes 131104 | tf_op jit(solution)/shard_map/diagonal_gather/ppermute | solution.py:284
  21.9 6.3 %all-to-all-done = bf16[8,4,32,256]{3,2,1,0:T(8,128)(2,1)S(1)} async-done(((bf16[8,4,32,256]{3,2,1,0:T(8,128)(2,1)}), bf16[8,4,32,256]{3,2,1,0:T(8,128)(2,1)S(1)}, u32[]{:S(2)}, u32[]{:S(2)}) %all-to-all-start) | async-done | bytes 524320 | tf_op jit(solution)/shard_map/noise_gather/all_to_all | solution.py:313
  28.1 9.2 %factors.1 = f32[128,8,128]{2,1,0:T(8,128)} custom-call(s32[128]{0:T(128)} %owner.1, f32[4,4096]{1,0:T(4,128)S(1)} %fusion.keep, bf16[32,32,256]{2,1,0:T(8,128)(2,1)S(1)} %bitcast.15, bf16[4,32,128,256]{3,2,1,0:T(8,128)(2,1)} %right_far.1, bf16[4,32,128,256]{3,2,1,0:T(8,128)(2,1)} %left_far.1, bf16[256,256]{1,0:T(8,128)(2,1)} %bitcast.19, ...), custom_call_target="tpu_custom_call" | custom-call | tf_op jit(solution)/shard_map/factors/pallas_call | solution.py:321
  37.3 8.4 %all-to-all-start.1 = ((f32[128,8,128]{2,1,0:T(8,128)}), f32[128,8,128]{2,1,0:T(8,128)S(1)}, u32[]{:S(2)}, u32[]{:S(2)}) async-start(f32[128,8,128]{2,1,0:T(8,128)} %factors.1), calls=%async_computation.1 | async-start | bytes 1048576 | tf_op jit(solution)/shard_map/member_exchange/all_to_all | solution.py:348
  45.8 13.7 %all-to-all-done.1 = f32[128,8,128]{2,1,0:T(8,128)S(1)} async-done(((f32[128,8,128]{2,1,0:T(8,128)}), f32[128,8,128]{2,1,0:T(8,128)S(1)}, u32[]{:S(2)}, u32[]{:S(2)}) %all-to-all-start.1) | async-done | bytes 524320 | tf_op jit(solution)/shard_map/member_exchange/all_to_all | solution.py:348
  59.5 0.6 place.1
  60.0 13.0 %all_to_all.15.slots = f32[32,16,128]{2,1,0:T(8,128)S(1)} all-to-all(f32[32,16,128]{2,1,0:T(8,128)S(1)} %place.1), channel_id=1, replica_groups={{0,1,2,3,4,5,6,7,8,9,10,11,12,13,14,15,16,17,18,19,20,21,22,23,24,25,26..., dimensions={0} | all-to-all | bytes 524288 | tf_op jit(solution)/shard_map/block_exchange/all_to_all | solution.py:365
  73.0 1.2 %stencil.1 = f32[32,4,64]{2,1,0:T(4,128)} custom-call(f32[32,16,128]{2,1,0:T(8,128)S(1)} %all_to_all.15.slots, f32[512,128]{1,0:T(8,128)S(1)} %bitcast.14), custom_call_target="tpu_custom_call" | custom-call | tf_op jit(solution)/shard_map/stencil/pallas_call | solution.py:368
  (5 shorter events, 0.0 us)
Async XLA Ops:
  0.0 9.6 %copy-start = (s32[4,32]{1,0:T(4,128)S(1)}, s32[4,32]{1,0:T(4,128)}, u32[]{:S(2)}) copy-start(s32[4,32]{1,0:T(4,128)} %param.14) | copy-start | bytes 1540
  0.0 18.7 %collective-permute-start.3 = (bf16[256,256]{1,0:T(8,128)(2,1)}, bf16[256,256]{1,0:T(8,128)(2,1)S(1)}, u32[]{:S(2)}, u32[]{:S(2)}) collective-permute-start(bf16[256,256]{1,0:T(8,128)(2,1)} %bitcast.17), channel_id=1, source_target_pairs={{0,2},{1,3},{2,0},{3,1},{4,6},{5,7},{6,4},{7,5},{8,10},{9,11},{10,... | collective-permute-start | bytes 393224 | tf_op jit(solution)/shard_map/diagonal_gather/ppermute | solution.py:279
  2.0 18.9 %collective-permute-start.2 = (bf16[256,256]{1,0:T(8,128)(2,1)}, bf16[256,256]{1,0:T(8,128)(2,1)S(1)}, u32[]{:S(2)}, u32[]{:S(2)}) collective-permute-start(bf16[256,256]{1,0:T(8,128)(2,1)} %bitcast.18), channel_id=1, source_target_pairs={{0,1},{1,0},{2,3},{3,2},{4,5},{5,4},{6,7},{7,6},{8,9},{9,8},{10,11... | collective-permute-start | bytes 393224 | tf_op jit(solution)/shard_map/diagonal_gather/ppermute | solution.py:282
  3.8 6.4 %collective-permute-start.1 = (f32[4,128]{1,0:T(4,128)S(1)}, f32[4,128]{1,0:T(4,128)S(1)}, u32[]{:S(2)}, u32[]{:S(2)}) collective-permute-start(f32[4,128]{1,0:T(4,128)S(1)} %pad_maximum_fusion.own), channel_id=1, source_target_pairs={{0,96},{1,97},{2,98},{3,99},{28,60},{29,61},{30,62},{31,63},{32,0}... | collective-permute-start | bytes 6152 | tf_op jit(solution)/shard_map/coefficient_halo/ppermute | solution.py:299
  9.5 4.3 %collective-permute-start = (bf16[4,32,256]{2,1,0:T(8,128)(2,1)}, bf16[4,32,256]{2,1,0:T(8,128)(2,1)S(1)}, u32[]{:S(2)}, u32[]{:S(2)}) collective-permute-start(bf16[4,32,256]{2,1,0:T(8,128)(2,1)} %param.10), channel_id=1, source_target_pairs={{3,0},{1,32},{0,64},{2,96},{7,4},{5,36},{4,68},{6,100},{11,8},{9,4... | collective-permute-start | bytes 196616 | tf_op jit(solution)/shard_map/noise_gather/ppermute | solution.py:288
  14.6 13.5 %all-to-all-start = ((bf16[8,4,32,256]{3,2,1,0:T(8,128)(2,1)}), bf16[8,4,32,256]{3,2,1,0:T(8,128)(2,1)S(1)}, u32[]{:S(2)}, u32[]{:S(2)}) async-start(bf16[8,4,32,256]{3,2,1,0:T(8,128)(2,1)} %broadcast_in_dim.5), calls=%async_computation | async-start | bytes 1048576 | tf_op jit(solution)/shard_map/noise_gather/all_to_all | solution.py:313
  18.7 3.2 %collective-permute-start.4 = (bf16[256,256]{1,0:T(8,128)(2,1)S(1)}, bf16[256,256]{1,0:T(8,128)(2,1)S(1)}, u32[]{:S(2)}, u32[]{:S(2)}) collective-permute-start(bf16[256,256]{1,0:T(8,128)(2,1)S(1)} %collective-permute-done.3.d2), channel_id=1, source_target_pairs={{0,1},{1,0},{2,3},{3,2},{4,5},{5,4},{6,7},{7,6},{8,9},{9,8},{10,11... | collective-permute-start | bytes 393224 | tf_op jit(solution)/shard_map/diagonal_gather/ppermute | solution.py:284
  28.1 17.6 %copy-start.1 = (s32[128]{0:T(128)S(1)}, s32[128]{0:T(128)}, u32[]{:S(2)}) copy-start(s32[128]{0:T(128)} %owner.1) | copy-start | bytes 1540
  37.3 22.1 %all-to-all-start.1 = ((f32[128,8,128]{2,1,0:T(8,128)}), f32[128,8,128]{2,1,0:T(8,128)S(1)}, u32[]{:S(2)}, u32[]{:S(2)}) async-start(f32[128,8,128]{2,1,0:T(8,128)} %factors.1), calls=%async_computation.1 | async-start | bytes 1048576 | tf_op jit(solution)/shard_map/member_exchange/all_to_all | solution.py:348

commit v9 on v8

--- a/solution.py
+++ b/solution.py
@@ -309,7 +309,6 @@
 
     with jax.named_scope("noise_gather"):
         sending = jnp.broadcast_to(swapped[None], (group, *swapped.shape))
-        sending, forwarded = lax.optimization_barrier((sending, forwarded))
         columns = lax.all_to_all(
             sending, "wide", 0, 0, axis_index_groups=planes, tiled=True
         ).reshape(cols, members, cells)

time: 74.5 us -> 71.4 us (0.958)
  waiting for transfers between devices: 25 us -> 20.7 us
  starting transfers between devices: 23.4 us -> 25.2 us
    all_to_all x1, waiting for transfers between devices: 13.7 us -> 7.72 us  [per_device(): got = lax.all_to_all(partial_sums, BOTH, 0, 0, tiled=True)]
    all_to_all x1, starting transfers between devices: 4.09 us -> 6.6 us  [per_device(): lax.all_to_all(sending, 'wide', 0, 0, axis_index_groups=planes, tiled=True)]
    all_to_all x1, waiting for transfers between devices: 6.25 us -> 8.11 us  [per_device(): lax.all_to_all(sending, 'wide', 0, 0, axis_index_groups=planes, tiled=True)]
    ppermute x1, starting transfers between devices: 0.08 us -> 1.53 us  [per_device(): swapped = lax.ppermute(noise, BOTH, swap)]
    ppermute x1, starting transfers between devices: 2.19 us -> 1.29 us  [per_device(): lax.ppermute(opposite, 'narrow', beside)]
    all_to_all x1, starting transfers between devices: 8.39 us -> 7.64 us  [per_device(): got = lax.all_to_all(partial_sums, BOTH, 0, 0, tiled=True)]
where the time goes in v9:
time: 71.4 us; the launch traced here: 71.1 us
  starting transfers between devices  25.2 us (35%)
  waiting for transfers between devices  20.7 us (29%)
  blocking collectives  13 us (18%)
  Pallas kernels  10.9 us (15%)
  local copies, waits for them, and re-layouts  0.95 us (1%)
    all_to_all x1, blocking collectives, per_device(): lax.all_to_all(blocks, BOTH, 0, 0, axis_index_groups=slabs, tiled=True)  13 us
    pallas_call x1, Pallas kernels, per_device(): pl.pallas_call(factor_kernel, out_shape=pltpu.VMEM((devices, 8, 128), f32...  9.19 us
    all_to_all x1, waiting for transfers between devices, per_device(): lax.all_to_all(sending, 'wide', 0, 0, axis_index_groups=planes, tiled=True)  8.11 us
    all_to_all x1, waiting for transfers between devices, per_device(): got = lax.all_to_all(partial_sums, BOTH, 0, 0, tiled=True)  7.72 us
    all_to_all x1, starting transfers between devices, per_device(): got = lax.all_to_all(partial_sums, BOTH, 0, 0, tiled=True)  7.64 us
    all_to_all x1, starting transfers between devices, per_device(): lax.all_to_all(sending, 'wide', 0, 0, axis_index_groups=planes, tiled=True)  6.6 us
    ppermute x1, starting transfers between devices, per_device(): lax.ppermute(own, BOTH, [((z * group + r) * narrow + b, ((z + step) % nar...  5.15 us
    ppermute x1, waiting for transfers between devices, per_device(): swapped = lax.ppermute(noise, BOTH, swap)  3.31 us
  transfers between devices with their start and end apart: 7, of which 5 were waited for; matrix products, arithmetic and copies ran while one was open for 2% of the time, Pallas kernels for 0%

profile of v9, /device:TPU:1, one launch (start us, length us, event | category | flops | bytes accessed | tf_op | source)
XLA Modules:
  0.0 71.1 jit_solution(6031301236655313783)
XLA Ops:
  0.0 2.0 %collective-permute-start.2 = (bf16[256,256]{1,0:T(8,128)(2,1)}, bf16[256,256]{1,0:T(8,128)(2,1)S(1)}, u32[]{:S(2)}, u32[]{:S(2)}) collective-permute-start(bf16[256,256]{1,0:T(8,128)(2,1)} %bitcast.17), channel_id=1, source_target_pairs={{0,2},{1,3},{2,0},{3,1},{4,6},{5,7},{6,4},{7,5},{8,10},{9,11},{10,... | collective-permute-start | bytes 393224 | tf_op jit(solution)/shard_map/diagonal_gather/ppermute | solution.py:279
  2.0 1.0 %collective-permute-start.1 = (bf16[256,256]{1,0:T(8,128)(2,1)}, bf16[256,256]{1,0:T(8,128)(2,1)S(1)}, u32[]{:S(2)}, u32[]{:S(2)}) collective-permute-start(bf16[256,256]{1,0:T(8,128)(2,1)} %bitcast.18), channel_id=1, source_target_pairs={{0,1},{1,0},{2,3},{3,2},{4,5},{5,4},{6,7},{7,6},{8,9},{9,8},{10,11... | collective-permute-start | bytes 393224 | tf_op jit(solution)/shard_map/diagonal_gather/ppermute | solution.py:282
  3.0 1.5 %collective-permute-start = (bf16[4,32,256]{2,1,0:T(8,128)(2,1)}, bf16[4,32,256]{2,1,0:T(8,128)(2,1)S(1)}, u32[]{:S(2)}, u32[]{:S(2)}) collective-permute-start(bf16[4,32,256]{2,1,0:T(8,128)(2,1)} %param.10), channel_id=1, source_target_pairs={{3,0},{1,32},{0,64},{2,96},{7,4},{5,36},{4,68},{6,100},{11,8},{9,4... | collective-permute-start | bytes 196616 | tf_op jit(solution)/shard_map/noise_gather/ppermute | solution.py:288
  4.5 0.0 copy-done
  4.5 0.1 broadcast_bitcast_fusion
  4.6 3.3 %collective-permute-done = bf16[4,32,256]{2,1,0:T(8,128)(2,1)S(1)} collective-permute-done((bf16[4,32,256]{2,1,0:T(8,128)(2,1)}, bf16[4,32,256]{2,1,0:T(8,128)(2,1)S(1)}, u32[]{:S(2)}, u32[]{:S(2)}) %collective-permute-start) | collective-permute-done | bytes 65568 | tf_op jit(solution)/shard_map/noise_gather/ppermute | solution.py:288
  7.9 0.8 %broadcast_in_dim.5 = bf16[8,4,32,256]{3,2,1,0:T(8,128)(2,1)} broadcast(bf16[4,32,256]{2,1,0:T(8,128)(2,1)S(1)} %collective-permute-done), dimensions={1,2,3} | broadcast | bytes 589824 | tf_op jit(solution)/shard_map/noise_gather/broadcast_in_dim | solution.py:311
  8.8 6.6 %all-to-all-start = ((bf16[8,4,32,256]{3,2,1,0:T(8,128)(2,1)}), bf16[8,4,32,256]{3,2,1,0:T(8,128)(2,1)S(1)}, u32[]{:S(2)}, u32[]{:S(2)}) async-start(bf16[8,4,32,256]{3,2,1,0:T(8,128)(2,1)} %broadcast_in_dim.5), calls=%async_computation | async-start | bytes 1048576 | tf_op jit(solution)/shard_map/noise_gather/all_to_all | solution.py:312
  15.4 0.0 collective-permute-done.2.d2
  15.4 1.3 %collective-permute-start.3 = (bf16[256,256]{1,0:T(8,128)(2,1)S(1)}, bf16[256,256]{1,0:T(8,128)(2,1)S(1)}, u32[]{:S(2)}, u32[]{:S(2)}) collective-permute-start(bf16[256,256]{1,0:T(8,128)(2,1)S(1)} %collective-permute-done.2.d2), channel_id=1, source_target_pairs={{0,1},{1,0},{2,3},{3,2},{4,5},{5,4},{6,7},{7,6},{8,9},{9,8},{10,11... | collective-permute-start | bytes 393224 | tf_op jit(solution)/shard_map/diagonal_gather/ppermute | solution.py:284
  16.7 0.1 fusion.keep
  16.7 0.0 collective-permute-done.1.d1
  16.7 0.9 %collective-permute-done.3.d3 = bf16[256,256]{1,0:T(8,128)(2,1)S(1)} collective-permute-done((bf16[256,256]{1,0:T(8,128)(2,1)S(1)}, bf16[256,256]{1,0:T(8,128)(2,1)S(1)}, u32[]{:S(2)}, u32[]{:S(2)}) %collective-permute-start.3) | collective-permute-done | bytes 131104 | tf_op jit(solution)/shard_map/diagonal_gather/ppermute | solution.py:284
  17.7 8.1 %all-to-all-done = bf16[8,4,32,256]{3,2,1,0:T(8,128)(2,1)S(1)} async-done(((bf16[8,4,32,256]{3,2,1,0:T(8,128)(2,1)}), bf16[8,4,32,256]{3,2,1,0:T(8,128)(2,1)S(1)}, u32[]{:S(2)}, u32[]{:S(2)}) %all-to-all-start) | async-done | bytes 524320 | tf_op jit(solution)/shard_map/noise_gather/all_to_all | solution.py:312
  25.8 0.0 copy-start.5
  25.8 9.2 %factors.1 = f32[128,8,128]{2,1,0:T(8,128)} custom-call(s32[128]{0:T(128)} %owner.1, f32[4,4096]{1,0:T(4,128)S(1)} %fusion.keep, bf16[32,32,256]{2,1,0:T(8,128)(2,1)S(1)} %bitcast.15, bf16[4,32,128,256]{3,2,1,0:T(8,128)(2,1)} %right_far.1, bf16[4,32,128,256]{3,2,1,0:T(8,128)(2,1)} %left_far.1, bf16[256,256]{1,0:T(8,128)(2,1)} %bitcast.19, ...), custom_call_target="tpu_custom_call" | custom-call | tf_op jit(solution)/shard_map/factors/pallas_call | solution.py:320
  35.0 7.6 %all-to-all-start.1 = ((f32[128,8,128]{2,1,0:T(8,128)}), f32[128,8,128]{2,1,0:T(8,128)S(1)}, u32[]{:S(2)}, u32[]{:S(2)}) async-start(f32[128,8,128]{2,1,0:T(8,128)} %factors.1), calls=%async_computation.1 | async-start | bytes 1048576 | tf_op jit(solution)/shard_map/member_exchange/all_to_all | solution.py:347
  42.7 0.1 pad_maximum_fusion.own
  42.8 5.2 %collective-permute-start.4 = (f32[4,128]{1,0:T(4,128)S(1)}, f32[4,128]{1,0:T(4,128)S(1)}, u32[]{:S(2)}, u32[]{:S(2)}) collective-permute-start(f32[4,128]{1,0:T(4,128)S(1)} %pad_maximum_fusion.own), channel_id=1, source_target_pairs={{0,96},{1,97},{2,98},{3,99},{28,60},{29,61},{30,62},{31,63},{32,0}... | collective-permute-start | bytes 6152 | tf_op jit(solution)/shard_map/coefficient_halo/ppermute | solution.py:299
  48.0 0.7 collective-permute-done.4.forwarded
  48.6 7.7 %all-to-all-done.1 = f32[128,8,128]{2,1,0:T(8,128)S(1)} async-done(((f32[128,8,128]{2,1,0:T(8,128)}), f32[128,8,128]{2,1,0:T(8,128)S(1)}, u32[]{:S(2)}, u32[]{:S(2)}) %all-to-all-start.1) | async-done | bytes 524320 | tf_op jit(solution)/shard_map/member_exchange/all_to_all | solution.py:347
  56.4 0.6 place.1
  56.9 13.0 %all_to_all.15.slots = f32[32,16,128]{2,1,0:T(8,128)S(1)} all-to-all(f32[32,16,128]{2,1,0:T(8,128)S(1)} %place.1), channel_id=1, replica_groups={{0,1,2,3,4,5,6,7,8,9,10,11,12,13,14,15,16,17,18,19,20,21,22,23,24,25,26..., dimensions={0} | all-to-all | bytes 524288 | tf_op jit(solution)/shard_map/block_exchange/all_to_all | solution.py:364
  69.9 1.2 %stencil.1 = f32[32,4,64]{2,1,0:T(4,128)} custom-call(f32[32,16,128]{2,1,0:T(8,128)S(1)} %all_to_all.15.slots, f32[512,128]{1,0:T(8,128)S(1)} %bitcast.14), custom_call_target="tpu_custom_call" | custom-call | tf_op jit(solution)/shard_map/stencil/pallas_call | solution.py:367
  (13 shorter events, 0.0 us)
Async XLA Ops:
  0.0 4.5 %copy-start = (s32[4,32]{1,0:T(4,128)S(1)}, s32[4,32]{1,0:T(4,128)}, u32[]{:S(2)}) copy-start(s32[4,32]{1,0:T(4,128)} %param.14) | copy-start | bytes 1540
  0.0 15.4 %collective-permute-start.2 = (bf16[256,256]{1,0:T(8,128)(2,1)}, bf16[256,256]{1,0:T(8,128)(2,1)S(1)}, u32[]{:S(2)}, u32[]{:S(2)}) collective-permute-start(bf16[256,256]{1,0:T(8,128)(2,1)} %bitcast.17), channel_id=1, source_target_pairs={{0,2},{1,3},{2,0},{3,1},{4,6},{5,7},{6,4},{7,5},{8,10},{9,11},{10,... | collective-permute-start | bytes 393224 | tf_op jit(solution)/shard_map/diagonal_gather/ppermute | solution.py:279
  2.0 14.7 %collective-permute-start.1 = (bf16[256,256]{1,0:T(8,128)(2,1)}, bf16[256,256]{1,0:T(8,128)(2,1)S(1)}, u32[]{:S(2)}, u32[]{:S(2)}) collective-permute-start(bf16[256,256]{1,0:T(8,128)(2,1)} %bitcast.18), channel_id=1, source_target_pairs={{0,1},{1,0},{2,3},{3,2},{4,5},{5,4},{6,7},{7,6},{8,9},{9,8},{10,11... | collective-permute-start | bytes 393224 | tf_op jit(solution)/shard_map/diagonal_gather/ppermute | solution.py:282
  3.0 4.9 %collective-permute-start = (bf16[4,32,256]{2,1,0:T(8,128)(2,1)}, bf16[4,32,256]{2,1,0:T(8,128)(2,1)S(1)}, u32[]{:S(2)}, u32[]{:S(2)}) collective-permute-start(bf16[4,32,256]{2,1,0:T(8,128)(2,1)} %param.10), channel_id=1, source_target_pairs={{3,0},{1,32},{0,64},{2,96},{7,4},{5,36},{4,68},{6,100},{11,8},{9,4... | collective-permute-start | bytes 196616 | tf_op jit(solution)/shard_map/noise_gather/ppermute | solution.py:288
  8.8 17.0 %all-to-all-start = ((bf16[8,4,32,256]{3,2,1,0:T(8,128)(2,1)}), bf16[8,4,32,256]{3,2,1,0:T(8,128)(2,1)S(1)}, u32[]{:S(2)}, u32[]{:S(2)}) async-start(bf16[8,4,32,256]{3,2,1,0:T(8,128)(2,1)} %broadcast_in_dim.5), calls=%async_computation | async-start | bytes 1048576 | tf_op jit(solution)/shard_map/noise_gather/all_to_all | solution.py:312
  15.4 2.3 %collective-permute-start.3 = (bf16[256,256]{1,0:T(8,128)(2,1)S(1)}, bf16[256,256]{1,0:T(8,128)(2,1)S(1)}, u32[]{:S(2)}, u32[]{:S(2)}) collective-permute-start(bf16[256,256]{1,0:T(8,128)(2,1)S(1)} %collective-permute-done.2.d2), channel_id=1, source_target_pairs={{0,1},{1,0},{2,3},{3,2},{4,5},{5,4},{6,7},{7,6},{8,9},{9,8},{10,11... | collective-permute-start | bytes 393224 | tf_op jit(solution)/shard_map/diagonal_gather/ppermute | solution.py:284
  25.8 16.9 %copy-start.1 = (f32[4,64]{1,0:T(4,128)S(1)}, f32[4,64]{1,0:T(4,128)}, u32[]{:S(2)}) copy-start(f32[4,64]{1,0:T(4,128)} %param.17) | copy-start | bytes 3076
  25.8 16.9 %copy-start.2 = (s32[4,64]{1,0:T(4,128)S(1)}, s32[4,64]{1,0:T(4,128)}, u32[]{:S(2)}) copy-start(s32[4,64]{1,0:T(4,128)} %param.19) | copy-start | bytes 3076
  25.8 16.9 %copy-start.3 = (f32[4,64]{1,0:T(4,128)S(1)}, f32[4,64]{1,0:T(4,128)}, u32[]{:S(2)}) copy-start(f32[4,64]{1,0:T(4,128)} %param.16) | copy-start | bytes 3076
  25.8 16.9 %copy-start.4 = (s32[4,64]{1,0:T(4,128)S(1)}, s32[4,64]{1,0:T(4,128)}, u32[]{:S(2)}) copy-start(s32[4,64]{1,0:T(4,128)} %param.18) | copy-start | bytes 3076
  25.8 22.2 %copy-start.5 = (s32[128]{0:T(128)S(1)}, s32[128]{0:T(128)}, u32[]{:S(2)}) copy-start(s32[128]{0:T(128)} %owner.1) | copy-start | bytes 1540
  35.0 21.4 %all-to-all-start.1 = ((f32[128,8,128]{2,1,0:T(8,128)}), f32[128,8,128]{2,1,0:T(8,128)S(1)}, u32[]{:S(2)}, u32[]{:S(2)}) async-start(f32[128,8,128]{2,1,0:T(8,128)} %factors.1), calls=%async_computation.1 | async-start | bytes 1048576 | tf_op jit(solution)/shard_map/member_exchange/all_to_all | solution.py:347
  42.8 5.9 %collective-permute-start.4 = (f32[4,128]{1,0:T(4,128)S(1)}, f32[4,128]{1,0:T(4,128)S(1)}, u32[]{:S(2)}, u32[]{:S(2)}) collective-permute-start(f32[4,128]{1,0:T(4,128)S(1)} %pad_maximum_fusion.own), channel_id=1, source_target_pairs={{0,96},{1,97},{2,98},{3,99},{28,60},{29,61},{30,62},{31,63},{32,0}... | collective-permute-start | bytes 6152 | tf_op jit(solution)/shard_map/coefficient_halo/ppermute | solution.py:299

commit v10 on v9

--- a/solution.py
+++ b/solution.py
@@ -265,13 +265,16 @@
     def server(plane_to, source):
         return source ^ (3, 1, 0, 2)[(plane_to - source) % 4]
 
-    swap = [
-        ((s * group + r) * narrow + server(z, s), (z * group + r) * narrow + s)
-        for s in range(narrow)
-        for r in range(group)
-        for z in range(narrow)
+    swaps = [
+        [
+            ((s * group + r) * narrow + server(z, s), (z * group + (r ^ flip)) * narrow + s)
+            for s in range(narrow)
+            for r in range(group)
+            for z in range(narrow)
+        ]
+        for flip in (0, 1)
     ]
-    planes = [[z * group + r for r in range(group)] for z in range(narrow)]
+    lines = [[z * group + 2 * y + x for y in range(group // 2)] for z in range(narrow) for x in (0, 1)]
 
     with jax.named_scope("diagonal_gather"):
         own_diag = diagonal_tile_blocks[0]
@@ -285,7 +288,7 @@
         ]
 
     with jax.named_scope("noise_gather"):
-        swapped = lax.ppermute(noise, BOTH, swap)
+        swapped, partner = [lax.ppermute(noise, BOTH, swap) for swap in swaps]
 
     with jax.named_scope("coefficient_halo"):
         own = jnp.concatenate(
@@ -308,9 +311,13 @@
         )
 
     with jax.named_scope("noise_gather"):
-        sending = jnp.broadcast_to(swapped[None], (group, *swapped.shape))
+        odd = lax.axis_index("wide") % 2 == 1
+        both = jnp.stack(
+            [jnp.where(odd, partner, swapped), jnp.where(odd, swapped, partner)]
+        )
+        sending = jnp.broadcast_to(both[None], (group // 2, *both.shape))
         columns = lax.all_to_all(
-            sending, "wide", 0, 0, axis_index_groups=planes, tiled=True
+            sending, "wide", 0, 0, axis_index_groups=lines, tiled=True
         ).reshape(cols, members, cells)
 
     with jax.named_scope("factors"):

time: 71.4 us -> 70.3 us (0.985)
  waiting for transfers between devices: 20.7 us -> 13.9 us
  starting transfers between devices: 25.2 us -> 30.8 us
    ppermute x1 -> x2, starting transfers between devices: 1.53 us -> 6.84 us  [per_device(): swapped, partner = [lax.ppermute(noise, BOTH, swap) for swap in swaps]]
    all_to_all x1, waiting for transfers between devices: 8.11 us -> 3.58 us  [per_device(): lax.all_to_all(sending, 'wide', 0, 0, axis_index_groups=lines, tiled=True)]
    all_to_all x1, starting transfers between devices: 6.6 us -> 4.18 us  [per_device(): lax.all_to_all(sending, 'wide', 0, 0, axis_index_groups=lines, tiled=True)]
    all_to_all x1, starting transfers between devices: 7.64 us -> 9.92 us  [per_device(): got = lax.all_to_all(partial_sums, BOTH, 0, 0, tiled=True)]
    ppermute x1 -> x2, waiting for transfers between devices: 3.31 us -> 1.04 us  [per_device(): swapped, partner = [lax.ppermute(noise, BOTH, swap) for swap in swaps]]
    ppermute x1, starting transfers between devices: 1.29 us -> 2.39 us  [per_device(): lax.ppermute(opposite, 'narrow', beside)]
  transfers between devices with their start and end apart: 7 -> 8, of which waited for: 5 -> 5; matrix products, arithmetic and copies ran while one was open for 2% -> 2% of each run, Pallas kernels for 0% -> 0%
where the time goes in v10:
time: 70.3 us; the launch traced here: 70 us
  starting transfers between devices  30.8 us (44%)
  waiting for transfers between devices  13.9 us (20%)
  blocking collectives  13 us (18%)
  Pallas kernels  10.9 us (16%)
  local copies, waits for them, and re-layouts  0.95 us (1%)
    all_to_all x1, blocking collectives, per_device(): lax.all_to_all(blocks, BOTH, 0, 0, axis_index_groups=slabs, tiled=True)  13 us
    all_to_all x1, starting transfers between devices, per_device(): got = lax.all_to_all(partial_sums, BOTH, 0, 0, tiled=True)  9.92 us
    pallas_call x1, Pallas kernels, per_device(): pl.pallas_call(factor_kernel, out_shape=pltpu.VMEM((devices, 8, 128), f32...  9.19 us
    all_to_all x1, waiting for transfers between devices, per_device(): got = lax.all_to_all(partial_sums, BOTH, 0, 0, tiled=True)  7.72 us
    ppermute x2, starting transfers between devices, per_device(): swapped, partner = [lax.ppermute(noise, BOTH, swap) for swap in swaps]  6.84 us
    ppermute x1, starting transfers between devices, per_device(): lax.ppermute(own, BOTH, [((z * group + r) * narrow + b, ((z + step) % nar...  5.15 us
    all_to_all x1, starting transfers between devices, per_device(): lax.all_to_all(sending, 'wide', 0, 0, axis_index_groups=lines, tiled=True)  4.18 us
    all_to_all x1, waiting for transfers between devices, per_device(): lax.all_to_all(sending, 'wide', 0, 0, axis_index_groups=lines, tiled=True)  3.58 us
  transfers between devices with their start and end apart: 8, of which 5 were waited for; matrix products, arithmetic and copies ran while one was open for 2% of the time, Pallas kernels for 0%

profile of v10, /device:TPU:1, one launch (start us, length us, event | category | flops | bytes accessed | tf_op | source)
XLA Modules:
  0.0 70.0 jit_solution(15387855214045631874)
XLA Ops:
  0.0 5.5 %collective-permute-start = (bf16[4,32,256]{2,1,0:T(8,128)(2,1)}, bf16[4,32,256]{2,1,0:T(8,128)(2,1)S(1)}, u32[]{:S(2)}, u32[]{:S(2)}) collective-permute-start(bf16[4,32,256]{2,1,0:T(8,128)(2,1)} %param.10), channel_id=1, source_target_pairs={{3,4},{1,36},{0,68},{2,100},{7,0},{5,32},{4,64},{6,96},{11,12},{9,... | collective-permute-start | bytes 196616 | tf_op jit(solution)/shard_map/noise_gather/ppermute | solution.py:291
  5.5 1.4 %collective-permute-start.1 = (bf16[4,32,256]{2,1,0:T(8,128)(2,1)}, bf16[4,32,256]{2,1,0:T(8,128)(2,1)S(1)}, u32[]{:S(2)}, u32[]{:S(2)}) collective-permute-start(bf16[4,32,256]{2,1,0:T(8,128)(2,1)} %param.10), channel_id=1, source_target_pairs={{3,0},{1,32},{0,64},{2,96},{7,4},{5,36},{4,68},{6,100},{11,8},{9,4... | collective-permute-start | bytes 196616 | tf_op jit(solution)/shard_map/noise_gather/ppermute | solution.py:291
  6.8 1.0 %collective-permute-start.2 = (bf16[256,256]{1,0:T(8,128)(2,1)}, bf16[256,256]{1,0:T(8,128)(2,1)S(1)}, u32[]{:S(2)}, u32[]{:S(2)}) collective-permute-start(bf16[256,256]{1,0:T(8,128)(2,1)} %bitcast.21), channel_id=1, source_target_pairs={{0,1},{1,0},{2,3},{3,2},{4,5},{5,4},{6,7},{7,6},{8,9},{9,8},{10,11... | collective-permute-start | bytes 393224 | tf_op jit(solution)/shard_map/diagonal_gather/ppermute | solution.py:285
  7.8 1.4 %collective-permute-start.3 = (bf16[256,256]{1,0:T(8,128)(2,1)}, bf16[256,256]{1,0:T(8,128)(2,1)S(1)}, u32[]{:S(2)}, u32[]{:S(2)}) collective-permute-start(bf16[256,256]{1,0:T(8,128)(2,1)} %bitcast.22), channel_id=1, source_target_pairs={{0,2},{1,3},{2,0},{3,1},{4,6},{5,7},{6,4},{7,5},{8,10},{9,11},{10,... | collective-permute-start | bytes 393224 | tf_op jit(solution)/shard_map/diagonal_gather/ppermute | solution.py:282
  9.2 0.1 broadcast_bitcast_fusion
  9.3 0.0 collective-permute-done
  9.3 1.0 %collective-permute-done.1 = bf16[4,32,256]{2,1,0:T(8,128)(2,1)S(1)} collective-permute-done((bf16[4,32,256]{2,1,0:T(8,128)(2,1)}, bf16[4,32,256]{2,1,0:T(8,128)(2,1)S(1)}, u32[]{:S(2)}, u32[]{:S(2)}) %collective-permute-start.1) | collective-permute-done | bytes 65568 | tf_op jit(solution)/shard_map/noise_gather/ppermute | solution.py:291
  10.4 0.9 %broadcast_in_dim.5 = bf16[4,2,4,32,256]{4,3,2,1,0:T(8,128)(2,1)} broadcast(bf16[2,4,32,256]{3,2,1,0:T(8,128)(2,1)S(1)} %pad_maximum_fusion), dimensions={1,2,3,4} | broadcast | bytes 655360 | tf_op jit(solution)/shard_map/noise_gather/broadcast_in_dim | solution.py:318
  11.2 4.2 %all-to-all-start = ((bf16[4,2,4,32,256]{4,3,2,1,0:T(8,128)(2,1)}), bf16[4,2,4,32,256]{4,3,2,1,0:T(8,128)(2,1)S(1)}, u32[]{:S(2)}, u32[]{:S(2)}) async-start(bf16[4,2,4,32,256]{4,3,2,1,0:T(8,128)(2,1)} %broadcast_in_dim.5), calls=%async_computation | async-start | bytes 1048576 | tf_op jit(solution)/shard_map/noise_gather/all_to_all | solution.py:319
  15.4 2.4 %collective-permute-start.4 = (bf16[256,256]{1,0:T(8,128)(2,1)S(1)}, bf16[256,256]{1,0:T(8,128)(2,1)S(1)}, u32[]{:S(2)}, u32[]{:S(2)}) collective-permute-start(bf16[256,256]{1,0:T(8,128)(2,1)S(1)} %collective-permute-done.3.d2), channel_id=1, source_target_pairs={{0,1},{1,0},{2,3},{3,2},{4,5},{5,4},{6,7},{7,6},{8,9},{9,8},{10,11... | collective-permute-start | bytes 393224 | tf_op jit(solution)/shard_map/diagonal_gather/ppermute | solution.py:287
  17.8 0.1 fusion.keep
  17.9 0.0 collective-permute-done.2.d1
  17.9 0.9 %collective-permute-done.4.d3 = bf16[256,256]{1,0:T(8,128)(2,1)S(1)} collective-permute-done((bf16[256,256]{1,0:T(8,128)(2,1)S(1)}, bf16[256,256]{1,0:T(8,128)(2,1)S(1)}, u32[]{:S(2)}, u32[]{:S(2)}) %collective-permute-start.4) | collective-permute-done | bytes 131104 | tf_op jit(solution)/shard_map/diagonal_gather/ppermute | solution.py:287
  18.8 3.6 %all-to-all-done = bf16[4,2,4,32,256]{4,3,2,1,0:T(8,128)(2,1)S(1)} async-done(((bf16[4,2,4,32,256]{4,3,2,1,0:T(8,128)(2,1)}), bf16[4,2,4,32,256]{4,3,2,1,0:T(8,128)(2,1)S(1)}, u32[]{:S(2)}, u32[]{:S(2)}) %all-to-all-start) | async-done | bytes 524320 | tf_op jit(solution)/shard_map/noise_gather/all_to_all | solution.py:319
  22.4 0.0 copy-start.5
  22.4 9.2 %factors.1 = f32[128,8,128]{2,1,0:T(8,128)} custom-call(s32[128]{0:T(128)} %owner.1, f32[4,4096]{1,0:T(4,128)S(1)} %fusion.keep, bf16[32,32,256]{2,1,0:T(8,128)(2,1)S(1)} %bitcast.19, bf16[4,32,128,256]{3,2,1,0:T(8,128)(2,1)} %right_far.1, bf16[4,32,128,256]{3,2,1,0:T(8,128)(2,1)} %left_far.1, bf16[256,256]{1,0:T(8,128)(2,1)} %bitcast.23, ...), custom_call_target="tpu_custom_call" | custom-call | tf_op jit(solution)/shard_map/factors/pallas_call | solution.py:327
  31.6 9.9 %all-to-all-start.1 = ((f32[128,8,128]{2,1,0:T(8,128)}), f32[128,8,128]{2,1,0:T(8,128)S(1)}, u32[]{:S(2)}, u32[]{:S(2)}) async-start(f32[128,8,128]{2,1,0:T(8,128)} %factors.1), calls=%async_computation.1 | async-start | bytes 1048576 | tf_op jit(solution)/shard_map/member_exchange/all_to_all | solution.py:354
  41.6 0.1 pad_maximum_fusion.1.own
  41.7 5.2 %collective-permute-start.5 = (f32[4,128]{1,0:T(4,128)S(1)}, f32[4,128]{1,0:T(4,128)S(1)}, u32[]{:S(2)}, u32[]{:S(2)}) collective-permute-start(f32[4,128]{1,0:T(4,128)S(1)} %pad_maximum_fusion.1.own), channel_id=1, source_target_pairs={{0,96},{1,97},{2,98},{3,99},{28,60},{29,61},{30,62},{31,63},{32,0}... | collective-permute-start | bytes 6152 | tf_op jit(solution)/shard_map/coefficient_halo/ppermute | solution.py:302
  46.9 0.7 collective-permute-done.5.forwarded
  47.5 7.7 %all-to-all-done.1 = f32[128,8,128]{2,1,0:T(8,128)S(1)} async-done(((f32[128,8,128]{2,1,0:T(8,128)}), f32[128,8,128]{2,1,0:T(8,128)S(1)}, u32[]{:S(2)}, u32[]{:S(2)}) %all-to-all-start.1) | async-done | bytes 524320 | tf_op jit(solution)/shard_map/member_exchange/all_to_all | solution.py:354
  55.2 0.6 place.1
  55.8 13.0 %all_to_all.15.slots = f32[32,16,128]{2,1,0:T(8,128)S(1)} all-to-all(f32[32,16,128]{2,1,0:T(8,128)S(1)} %place.1), channel_id=1, replica_groups={{0,1,2,3,4,5,6,7,8,9,10,11,12,13,14,15,16,17,18,19,20,21,22,23,24,25,26..., dimensions={0} | all-to-all | bytes 524288 | tf_op jit(solution)/shard_map/block_exchange/all_to_all | solution.py:371
  68.8 1.2 %stencil.1 = f32[32,4,64]{2,1,0:T(4,128)} custom-call(f32[32,16,128]{2,1,0:T(8,128)S(1)} %all_to_all.15.slots, f32[512,128]{1,0:T(8,128)S(1)} %bitcast.18), custom_call_target="tpu_custom_call" | custom-call | tf_op jit(solution)/shard_map/stencil/pallas_call | solution.py:374
  (17 shorter events, 0.1 us)
Async XLA Ops:
  0.0 9.2 %copy-start = (s32[4,32]{1,0:T(4,128)S(1)}, s32[4,32]{1,0:T(4,128)}, u32[]{:S(2)}) copy-start(s32[4,32]{1,0:T(4,128)} %param.14) | copy-start | bytes 1540
  0.0 9.3 %collective-permute-start = (bf16[4,32,256]{2,1,0:T(8,128)(2,1)}, bf16[4,32,256]{2,1,0:T(8,128)(2,1)S(1)}, u32[]{:S(2)}, u32[]{:S(2)}) collective-permute-start(bf16[4,32,256]{2,1,0:T(8,128)(2,1)} %param.10), channel_id=1, source_target_pairs={{3,4},{1,36},{0,68},{2,100},{7,0},{5,32},{4,64},{6,96},{11,12},{9,... | collective-permute-start | bytes 196616 | tf_op jit(solution)/shard_map/noise_gather/ppermute | solution.py:291
  5.5 4.8 %collective-permute-start.1 = (bf16[4,32,256]{2,1,0:T(8,128)(2,1)}, bf16[4,32,256]{2,1,0:T(8,128)(2,1)S(1)}, u32[]{:S(2)}, u32[]{:S(2)}) collective-permute-start(bf16[4,32,256]{2,1,0:T(8,128)(2,1)} %param.10), channel_id=1, source_target_pairs={{3,0},{1,32},{0,64},{2,96},{7,4},{5,36},{4,68},{6,100},{11,8},{9,4... | collective-permute-start | bytes 196616 | tf_op jit(solution)/shard_map/noise_gather/ppermute | solution.py:291
  6.8 11.0 %collective-permute-start.2 = (bf16[256,256]{1,0:T(8,128)(2,1)}, bf16[256,256]{1,0:T(8,128)(2,1)S(1)}, u32[]{:S(2)}, u32[]{:S(2)}) collective-permute-start(bf16[256,256]{1,0:T(8,128)(2,1)} %bitcast.21), channel_id=1, source_target_pairs={{0,1},{1,0},{2,3},{3,2},{4,5},{5,4},{6,7},{7,6},{8,9},{9,8},{10,11... | collective-permute-start | bytes 393224 | tf_op jit(solution)/shard_map/diagonal_gather/ppermute | solution.py:285
  7.8 7.6 %collective-permute-start.3 = (bf16[256,256]{1,0:T(8,128)(2,1)}, bf16[256,256]{1,0:T(8,128)(2,1)S(1)}, u32[]{:S(2)}, u32[]{:S(2)}) collective-permute-start(bf16[256,256]{1,0:T(8,128)(2,1)} %bitcast.22), channel_id=1, source_target_pairs={{0,2},{1,3},{2,0},{3,1},{4,6},{5,7},{6,4},{7,5},{8,10},{9,11},{10,... | collective-permute-start | bytes 393224 | tf_op jit(solution)/shard_map/diagonal_gather/ppermute | solution.py:282
  11.2 11.1 %all-to-all-start = ((bf16[4,2,4,32,256]{4,3,2,1,0:T(8,128)(2,1)}), bf16[4,2,4,32,256]{4,3,2,1,0:T(8,128)(2,1)S(1)}, u32[]{:S(2)}, u32[]{:S(2)}) async-start(bf16[4,2,4,32,256]{4,3,2,1,0:T(8,128)(2,1)} %broadcast_in_dim.5), calls=%async_computation | async-start | bytes 1048576 | tf_op jit(solution)/shard_map/noise_gather/all_to_all | solution.py:319
  15.4 3.4 %collective-permute-start.4 = (bf16[256,256]{1,0:T(8,128)(2,1)S(1)}, bf16[256,256]{1,0:T(8,128)(2,1)S(1)}, u32[]{:S(2)}, u32[]{:S(2)}) collective-permute-start(bf16[256,256]{1,0:T(8,128)(2,1)S(1)} %collective-permute-done.3.d2), channel_id=1, source_target_pairs={{0,1},{1,0},{2,3},{3,2},{4,5},{5,4},{6,7},{7,6},{8,9},{9,8},{10,11... | collective-permute-start | bytes 393224 | tf_op jit(solution)/shard_map/diagonal_gather/ppermute | solution.py:287
  22.4 19.1 %copy-start.1 = (f32[4,64]{1,0:T(4,128)S(1)}, f32[4,64]{1,0:T(4,128)}, u32[]{:S(2)}) copy-start(f32[4,64]{1,0:T(4,128)} %param.17) | copy-start | bytes 3076
  22.4 19.2 %copy-start.2 = (s32[4,64]{1,0:T(4,128)S(1)}, s32[4,64]{1,0:T(4,128)}, u32[]{:S(2)}) copy-start(s32[4,64]{1,0:T(4,128)} %param.19) | copy-start | bytes 3076
  22.4 19.2 %copy-start.3 = (f32[4,64]{1,0:T(4,128)S(1)}, f32[4,64]{1,0:T(4,128)}, u32[]{:S(2)}) copy-start(f32[4,64]{1,0:T(4,128)} %param.16) | copy-start | bytes 3076
  22.4 19.2 %copy-start.4 = (s32[4,64]{1,0:T(4,128)S(1)}, s32[4,64]{1,0:T(4,128)}, u32[]{:S(2)}) copy-start(s32[4,64]{1,0:T(4,128)} %param.18) | copy-start | bytes 3076
  22.4 24.4 %copy-start.5 = (s32[128]{0:T(128)S(1)}, s32[128]{0:T(128)}, u32[]{:S(2)}) copy-start(s32[128]{0:T(128)} %owner.1) | copy-start | bytes 1540
  31.6 23.7 %all-to-all-start.1 = ((f32[128,8,128]{2,1,0:T(8,128)}), f32[128,8,128]{2,1,0:T(8,128)S(1)}, u32[]{:S(2)}, u32[]{:S(2)}) async-start(f32[128,8,128]{2,1,0:T(8,128)} %factors.1), calls=%async_computation.1 | async-start | bytes 1048576 | tf_op jit(solution)/shard_map/member_exchange/all_to_all | solution.py:354
  41.7 5.9 %collective-permute-start.5 = (f32[4,128]{1,0:T(4,128)S(1)}, f32[4,128]{1,0:T(4,128)S(1)}, u32[]{:S(2)}, u32[]{:S(2)}) collective-permute-start(f32[4,128]{1,0:T(4,128)S(1)} %pad_maximum_fusion.1.own), channel_id=1, source_target_pairs={{0,96},{1,97},{2,98},{3,99},{28,60},{29,61},{30,62},{31,63},{32,0}... | collective-permute-start | bytes 6152 | tf_op jit(solution)/shard_map/coefficient_halo/ppermute | solution.py:302

commit v11 on v10

--- a/solution.py
+++ b/solution.py
@@ -15,6 +15,7 @@
 SMEM = pltpu.SMEM
 MIB = 1 << 20
 CHUNKS = 8
+EARLY = 8
 
 
 def specs(*spaces):
@@ -35,15 +36,28 @@
 
 def halves(count):
     return slice(0, count // 2), slice(count // 2, count)
+
+
+def fetch_kernel(right_far, diag_far, right, diag, done):
+    rows, count = right.shape[:2]
+    copies = [
+        pltpu.make_async_copy(right_far.at[p, 0:count], right.at[p], done.at[p]) for p in range(rows)
+    ]
+    copies.append(pltpu.make_async_copy(diag_far, diag, done.at[rows]))
+    for copy in copies:
+        copy.start()
+    for copy in copies:
+        copy.wait()
 
 
 def factor_kernel(
     owner,
     keep,
     noise,
+    early,
+    d0,
     right_far,
     left_far,
-    diag_far,
     d1,
     d2,
     d3,
@@ -53,29 +67,29 @@
     own,
     right,
     left,
-    d0,
     kept,
     done,
 ):
-    rows, cols, rank_max, cells = right.shape
+    rows, cols, rank_max, cells = left.shape
     members = noise.shape[1]
     each = cols // CHUNKS
-    chunks = [slice(i * each, (i + 1) * each) for i in range(CHUNKS)]
-    pairs = [(right_far.at[:, span], right.at[:, span]) for span in chunks]
+    ahead = EARLY // each
+    chunks = [slice(i * each, (i + 1) * each) for i in range(ahead, CHUNKS)]
+    pairs = [
+        (right_far.at[:, span], right.at[:, span.start - EARLY : span.stop - EARLY])
+        for span in chunks
+    ]
     pairs += [(left_far.at[p, span], left.at[p, span]) for p in range(rows) for span in halves(cols)]
-    pairs += [(diag_far, d0)]
     copies = [
         pltpu.make_async_copy(source, target, done.at[i])
         for i, (source, target) in enumerate(pairs)
     ]
-    copies[-1].start()
     for copy in copies[:CHUNKS]:
         copy.start()
-    copies[-1].wait()
 
     def arrived(i):
         copies[i].wait()
-        if i + CHUNKS < len(copies) - 1:
+        if i + CHUNKS < len(copies):
             copies[i + CHUNKS].start()
 
     w, n = lax.axis_index("wide"), lax.axis_index("narrow")
@@ -95,10 +109,10 @@
         )
         own[row] = jnp.where(held, term, 0.0)
     for c in range(cols):
-        if c % each == 0:
-            arrived(c // each)
+        if c >= EARLY and c % each == 0:
+            arrived(c // each - ahead)
         span = slice(c * rank_max, (c + 1) * rank_max)
-        block = right[:, c].reshape(rows * rank_max, cells)
+        block = (early[:, c] if c < EARLY else right[:, c - EARLY]).reshape(rows * rank_max, cells)
         product = lax.dot_general(
             noise[c], block, (((1,), (1,)), ((), ())), preferred_element_type=jnp.float32
         )
@@ -109,7 +123,7 @@
     for p in range(rows):
         total = own[p]
         for i, span in enumerate(halves(cols)):
-            arrived(CHUNKS + 2 * p + i)
+            arrived(len(chunks) + 2 * p + i)
             total = total + jnp.dot(
                 coeff[p, :, rank_max * span.start : rank_max * span.stop],
                 left[p, span].reshape(cols // 2 * rank_max, cells),
@@ -316,6 +330,23 @@
             [jnp.where(odd, partner, swapped), jnp.where(odd, swapped, partner)]
         )
         sending = jnp.broadcast_to(both[None], (group // 2, *both.shape))
+        sending, right_factors, own_diag = lax.optimization_barrier(
+            (sending, right_factors, own_diag)
+        )
+        early, first_diag = pl.pallas_call(
+            fetch_kernel,
+            out_shape=[
+                pltpu.VMEM((rows, EARLY, rank_max, cells), right_factors.dtype),
+                pltpu.VMEM(own_diag.shape, own_diag.dtype),
+            ],
+            in_specs=specs(pltpu.HBM, pltpu.HBM),
+            out_specs=specs(VMEM, VMEM),
+            scratch_shapes=[pltpu.SemaphoreType.DMA((rows + 1,))],
+            compiler_params=limit(1),
+            cost_estimate=pl.CostEstimate(
+                flops=0, transcendentals=0, bytes_accessed=rows * EARLY * rank_max * cells * 4
+            ),
+        )(far(right_factors), far(own_diag))
         columns = lax.all_to_all(
             sending, "wide", 0, 0, axis_index_groups=lines, tiled=True
         ).reshape(cols, members, cells)
@@ -327,26 +358,26 @@
         partial_sums = pl.pallas_call(
             factor_kernel,
             out_shape=pltpu.VMEM((devices, 8, 128), f32),
-            in_specs=specs(SMEM, VMEM, VMEM, *[pltpu.HBM] * 3, *[VMEM] * (narrow - 1)),
+            in_specs=specs(SMEM, *[VMEM] * 4, *[pltpu.HBM] * 2, *[VMEM] * (narrow - 1)),
             out_specs=pl.BlockSpec(memory_space=VMEM),
             scratch_shapes=[
                 pltpu.VMEM((rows, members, cols * rank_max), jnp.bfloat16),
                 pltpu.VMEM((members * 8, 128), f32),
                 pltpu.VMEM((rows, members, cells), f32),
-                pltpu.VMEM(right_factors.shape, right_factors.dtype),
+                pltpu.VMEM((rows, cols - EARLY, rank_max, cells), right_factors.dtype),
                 pltpu.VMEM(left_factors.shape, left_factors.dtype),
                 pltpu.VMEM(own_diag.shape, own_diag.dtype),
-                pltpu.VMEM(own_diag.shape, own_diag.dtype),
-                pltpu.SemaphoreType.DMA((CHUNKS + 2 * rows + 1,)),
+                pltpu.SemaphoreType.DMA((CHUNKS + 2 * rows,)),
             ],
             compiler_params=limit(24),
         )(
             far(owner),
             near(keep),
             near(columns),
+            early,
+            first_diag,
             far(right_factors),
             far(left_factors),
-            far(diags[0]),
             *[near(d) for d in diags[1:]],
         )
 

time: 70.3 us -> 69.7 us (level)
  waiting for transfers between devices: 13.9 us -> 12.3 us
  Pallas kernels: 10.9 us -> 11.9 us
    pallas_call x0 -> x1, Pallas kernels: none -> 1.58 us  [per_device(): pl.pallas_call(fetch_kernel, out_shape=[pltpu.VMEM((rows, EARLY, rank_max...]
    ppermute x1, waiting for transfers between devices: 0.92 us -> 0.01 us  [per_device(): lax.ppermute(opposite, 'narrow', beside)]
  transfers between devices with their start and end apart: 8 -> 8, of which waited for: 5 -> 4; matrix products, arithmetic and copies ran while one was open for 2% -> 2% of each run, Pallas kernels for 0% -> 2%
where the time goes in v11:
time: 69.7 us; the launch traced here: 69.4 us
  starting transfers between devices  30.8 us (44%)
  blocking collectives  13 us (19%)
  waiting for transfers between devices  12.3 us (18%)
  Pallas kernels  11.9 us (17%)
  local copies, waits for them, and re-layouts  0.97 us (1%)
    all_to_all x1, blocking collectives, per_device(): lax.all_to_all(blocks, BOTH, 0, 0, axis_index_groups=slabs, tiled=True)  13 us
    all_to_all x1, starting transfers between devices, per_device(): got = lax.all_to_all(partial_sums, BOTH, 0, 0, tiled=True)  9.92 us
    pallas_call x1, Pallas kernels, per_device(): pl.pallas_call(factor_kernel, out_shape=pltpu.VMEM((devices, 8, 128), f32...  8.54 us
    all_to_all x1, waiting for transfers between devices, per_device(): got = lax.all_to_all(partial_sums, BOTH, 0, 0, tiled=True)  7.72 us
    ppermute x2, starting transfers between devices, per_device(): swapped, partner = [lax.ppermute(noise, BOTH, swap) for swap in swaps]  6.84 us
    ppermute x1, starting transfers between devices, per_device(): lax.ppermute(own, BOTH, [((z * group + r) * narrow + b, ((z + step) % nar...  5.15 us
    all_to_all x1, starting transfers between devices, per_device(): lax.all_to_all(sending, 'wide', 0, 0, axis_index_groups=lines, tiled=True)  4.18 us
    all_to_all x1, waiting for transfers between devices, per_device(): lax.all_to_all(sending, 'wide', 0, 0, axis_index_groups=lines, tiled=True)  2.9 us
  transfers between devices with their start and end apart: 8, of which 4 were waited for; matrix products, arithmetic and copies ran while one was open for 2% of the time, Pallas kernels for 2%

profile of v11, /device:TPU:1, one launch (start us, length us, event | category | flops | bytes accessed | tf_op | source)
XLA Modules:
  0.0 69.4 jit_solution(14766727232423831072)
XLA Ops:
  0.0 5.5 %collective-permute-start = (bf16[4,32,256]{2,1,0:T(8,128)(2,1)}, bf16[4,32,256]{2,1,0:T(8,128)(2,1)S(1)}, u32[]{:S(2)}, u32[]{:S(2)}) collective-permute-start(bf16[4,32,256]{2,1,0:T(8,128)(2,1)} %param.10), channel_id=1, source_target_pairs={{3,4},{1,36},{0,68},{2,100},{7,0},{5,32},{4,64},{6,96},{11,12},{9,... | collective-permute-start | bytes 196616 | tf_op jit(solution)/shard_map/noise_gather/ppermute | solution.py:305
  5.5 1.4 %collective-permute-start.1 = (bf16[4,32,256]{2,1,0:T(8,128)(2,1)}, bf16[4,32,256]{2,1,0:T(8,128)(2,1)S(1)}, u32[]{:S(2)}, u32[]{:S(2)}) collective-permute-start(bf16[4,32,256]{2,1,0:T(8,128)(2,1)} %param.10), channel_id=1, source_target_pairs={{3,0},{1,32},{0,64},{2,96},{7,4},{5,36},{4,68},{6,100},{11,8},{9,4... | collective-permute-start | bytes 196616 | tf_op jit(solution)/shard_map/noise_gather/ppermute | solution.py:305
  6.8 1.0 %collective-permute-start.2 = (bf16[256,256]{1,0:T(8,128)(2,1)}, bf16[256,256]{1,0:T(8,128)(2,1)S(1)}, u32[]{:S(2)}, u32[]{:S(2)}) collective-permute-start(bf16[256,256]{1,0:T(8,128)(2,1)} %bitcast.21), channel_id=1, source_target_pairs={{0,1},{1,0},{2,3},{3,2},{4,5},{5,4},{6,7},{7,6},{8,9},{9,8},{10,11... | collective-permute-start | bytes 393224 | tf_op jit(solution)/shard_map/diagonal_gather/ppermute | solution.py:299
  7.8 1.4 %collective-permute-start.3 = (bf16[256,256]{1,0:T(8,128)(2,1)}, bf16[256,256]{1,0:T(8,128)(2,1)S(1)}, u32[]{:S(2)}, u32[]{:S(2)}) collective-permute-start(bf16[256,256]{1,0:T(8,128)(2,1)} %bitcast.22), channel_id=1, source_target_pairs={{0,2},{1,3},{2,0},{3,1},{4,6},{5,7},{6,4},{7,5},{8,10},{9,11},{10,... | collective-permute-start | bytes 393224 | tf_op jit(solution)/shard_map/diagonal_gather/ppermute | solution.py:296
  9.2 0.1 broadcast_bitcast_fusion
  9.3 1.0 %collective-permute-done.1 = bf16[4,32,256]{2,1,0:T(8,128)(2,1)S(1)} collective-permute-done((bf16[4,32,256]{2,1,0:T(8,128)(2,1)}, bf16[4,32,256]{2,1,0:T(8,128)(2,1)S(1)}, u32[]{:S(2)}, u32[]{:S(2)}) %collective-permute-start.1) | collective-permute-done | bytes 65568 | tf_op jit(solution)/shard_map/noise_gather/ppermute | solution.py:305
  10.4 0.9 %broadcast_in_dim.5 = bf16[4,2,4,32,256]{4,3,2,1,0:T(8,128)(2,1)} broadcast(bf16[2,4,32,256]{3,2,1,0:T(8,128)(2,1)S(1)} %pad_maximum_fusion), dimensions={1,2,3,4} | broadcast | bytes 655360 | tf_op jit(solution)/shard_map/noise_gather/broadcast_in_dim | solution.py:332
  11.2 4.2 %all-to-all-start = ((bf16[4,2,4,32,256]{4,3,2,1,0:T(8,128)(2,1)}), bf16[4,2,4,32,256]{4,3,2,1,0:T(8,128)(2,1)S(1)}, u32[]{:S(2)}, u32[]{:S(2)}) async-start(bf16[4,2,4,32,256]{4,3,2,1,0:T(8,128)(2,1)} %broadcast_in_dim.5), calls=%async_computation | async-start | bytes 1048576 | tf_op jit(solution)/shard_map/noise_gather/all_to_all | solution.py:350
  15.4 0.0 collective-permute-done.3.d2
  15.4 2.4 %collective-permute-start.4 = (bf16[256,256]{1,0:T(8,128)(2,1)S(1)}, bf16[256,256]{1,0:T(8,128)(2,1)S(1)}, u32[]{:S(2)}, u32[]{:S(2)}) collective-permute-start(bf16[256,256]{1,0:T(8,128)(2,1)S(1)} %collective-permute-done.3.d2), channel_id=1, source_target_pairs={{0,1},{1,0},{2,3},{3,2},{4,5},{5,4},{6,7},{7,6},{8,9},{9,8},{10,11... | collective-permute-start | bytes 393224 | tf_op jit(solution)/shard_map/diagonal_gather/ppermute | solution.py:301
  17.8 0.1 fusion.keep
  17.9 1.6 %noise_gather.1 = (bf16[4,8,128,256]{3,2,1,0:T(8,128)(2,1)S(1)}, bf16[256,256]{1,0:T(8,128)(2,1)S(1)}) custom-call(bf16[4,32,128,256]{3,2,1,0:T(8,128)(2,1)} %right_far.1, bf16[256,256]{1,0:T(8,128)(2,1)} %bitcast.23), custom_call_target="tpu_custom_call" | custom-call | bytes 4194304 | tf_op jit(solution)/shard_map/noise_gather/pallas_call | solution.py:336
  19.5 0.0 collective-permute-done.2.d1
  19.5 2.9 %all-to-all-done = bf16[4,2,4,32,256]{4,3,2,1,0:T(8,128)(2,1)S(1)} async-done(((bf16[4,2,4,32,256]{4,3,2,1,0:T(8,128)(2,1)}), bf16[4,2,4,32,256]{4,3,2,1,0:T(8,128)(2,1)S(1)}, u32[]{:S(2)}, u32[]{:S(2)}) %all-to-all-start) | async-done | bytes 524320 | tf_op jit(solution)/shard_map/noise_gather/all_to_all | solution.py:350
  22.4 0.0 copy-start.5
  22.4 8.5 %factors.1 = f32[128,8,128]{2,1,0:T(8,128)} custom-call(s32[128]{0:T(128)} %owner.1, f32[4,4096]{1,0:T(4,128)S(1)} %fusion.keep, bf16[32,32,256]{2,1,0:T(8,128)(2,1)S(1)} %bitcast.19, bf16[4,8,128,256]{3,2,1,0:T(8,128)(2,1)S(1)} %get-tuple-element.13.early, bf16[256,256]{1,0:T(8,128)(2,1)S(1)} %get-tuple-element.14.d0, bf16[4,32,128,256]{3,2,1,0:T(8,128)(2,1)} %right_far.1, ...), custom_call_target="tpu_custom_call" | custom-call | tf_op jit(solution)/shard_map/factors/pallas_call | solution.py:358
  31.0 9.9 %all-to-all-start.1 = ((f32[128,8,128]{2,1,0:T(8,128)}), f32[128,8,128]{2,1,0:T(8,128)S(1)}, u32[]{:S(2)}, u32[]{:S(2)}) async-start(f32[128,8,128]{2,1,0:T(8,128)} %factors.1), calls=%async_computation.1 | async-start | bytes 1048576 | tf_op jit(solution)/shard_map/member_exchange/all_to_all | solution.py:385
  40.9 0.1 pad_maximum_fusion.1.own
  41.0 5.2 %collective-permute-start.5 = (f32[4,128]{1,0:T(4,128)S(1)}, f32[4,128]{1,0:T(4,128)S(1)}, u32[]{:S(2)}, u32[]{:S(2)}) collective-permute-start(f32[4,128]{1,0:T(4,128)S(1)} %pad_maximum_fusion.1.own), channel_id=1, source_target_pairs={{0,96},{1,97},{2,98},{3,99},{28,60},{29,61},{30,62},{31,63},{32,0}... | collective-permute-start | bytes 6152 | tf_op jit(solution)/shard_map/coefficient_halo/ppermute | solution.py:316
  46.2 0.7 collective-permute-done.5.forwarded
  46.9 7.7 %all-to-all-done.1 = f32[128,8,128]{2,1,0:T(8,128)S(1)} async-done(((f32[128,8,128]{2,1,0:T(8,128)}), f32[128,8,128]{2,1,0:T(8,128)S(1)}, u32[]{:S(2)}, u32[]{:S(2)}) %all-to-all-start.1) | async-done | bytes 524320 | tf_op jit(solution)/shard_map/member_exchange/all_to_all | solution.py:385
  54.6 0.6 place.1
  55.2 13.0 %all_to_all.15.slots = f32[32,16,128]{2,1,0:T(8,128)S(1)} all-to-all(f32[32,16,128]{2,1,0:T(8,128)S(1)} %place.1), channel_id=1, replica_groups={{0,1,2,3,4,5,6,7,8,9,10,11,12,13,14,15,16,17,18,19,20,21,22,23,24,25,26..., dimensions={0} | all-to-all | bytes 524288 | tf_op jit(solution)/shard_map/block_exchange/all_to_all | solution.py:402
  68.2 1.2 %stencil.1 = f32[32,4,64]{2,1,0:T(4,128)} custom-call(f32[32,16,128]{2,1,0:T(8,128)S(1)} %all_to_all.15.slots, f32[512,128]{1,0:T(8,128)S(1)} %bitcast.18), custom_call_target="tpu_custom_call" | custom-call | tf_op jit(solution)/shard_map/stencil/pallas_call | solution.py:405
  (18 shorter events, 0.1 us)
Async XLA Ops:
  0.0 9.2 %copy-start = (s32[4,32]{1,0:T(4,128)S(1)}, s32[4,32]{1,0:T(4,128)}, u32[]{:S(2)}) copy-start(s32[4,32]{1,0:T(4,128)} %param.14) | copy-start | bytes 1540
  0.0 9.3 %collective-permute-start = (bf16[4,32,256]{2,1,0:T(8,128)(2,1)}, bf16[4,32,256]{2,1,0:T(8,128)(2,1)S(1)}, u32[]{:S(2)}, u32[]{:S(2)}) collective-permute-start(bf16[4,32,256]{2,1,0:T(8,128)(2,1)} %param.10), channel_id=1, source_target_pairs={{3,4},{1,36},{0,68},{2,100},{7,0},{5,32},{4,64},{6,96},{11,12},{9,... | collective-permute-start | bytes 196616 | tf_op jit(solution)/shard_map/noise_gather/ppermute | solution.py:305
  5.5 4.8 %collective-permute-start.1 = (bf16[4,32,256]{2,1,0:T(8,128)(2,1)}, bf16[4,32,256]{2,1,0:T(8,128)(2,1)S(1)}, u32[]{:S(2)}, u32[]{:S(2)}) collective-permute-start(bf16[4,32,256]{2,1,0:T(8,128)(2,1)} %param.10), channel_id=1, source_target_pairs={{3,0},{1,32},{0,64},{2,96},{7,4},{5,36},{4,68},{6,100},{11,8},{9,4... | collective-permute-start | bytes 196616 | tf_op jit(solution)/shard_map/noise_gather/ppermute | solution.py:305
  6.8 12.6 %collective-permute-start.2 = (bf16[256,256]{1,0:T(8,128)(2,1)}, bf16[256,256]{1,0:T(8,128)(2,1)S(1)}, u32[]{:S(2)}, u32[]{:S(2)}) collective-permute-start(bf16[256,256]{1,0:T(8,128)(2,1)} %bitcast.21), channel_id=1, source_target_pairs={{0,1},{1,0},{2,3},{3,2},{4,5},{5,4},{6,7},{7,6},{8,9},{9,8},{10,11... | collective-permute-start | bytes 393224 | tf_op jit(solution)/shard_map/diagonal_gather/ppermute | solution.py:299
  7.8 7.6 %collective-permute-start.3 = (bf16[256,256]{1,0:T(8,128)(2,1)}, bf16[256,256]{1,0:T(8,128)(2,1)S(1)}, u32[]{:S(2)}, u32[]{:S(2)}) collective-permute-start(bf16[256,256]{1,0:T(8,128)(2,1)} %bitcast.22), channel_id=1, source_target_pairs={{0,2},{1,3},{2,0},{3,1},{4,6},{5,7},{6,4},{7,5},{8,10},{9,11},{10,... | collective-permute-start | bytes 393224 | tf_op jit(solution)/shard_map/diagonal_gather/ppermute | solution.py:296
  11.2 11.1 %all-to-all-start = ((bf16[4,2,4,32,256]{4,3,2,1,0:T(8,128)(2,1)}), bf16[4,2,4,32,256]{4,3,2,1,0:T(8,128)(2,1)S(1)}, u32[]{:S(2)}, u32[]{:S(2)}) async-start(bf16[4,2,4,32,256]{4,3,2,1,0:T(8,128)(2,1)} %broadcast_in_dim.5), calls=%async_computation | async-start | bytes 1048576 | tf_op jit(solution)/shard_map/noise_gather/all_to_all | solution.py:350
  15.4 4.0 %collective-permute-start.4 = (bf16[256,256]{1,0:T(8,128)(2,1)S(1)}, bf16[256,256]{1,0:T(8,128)(2,1)S(1)}, u32[]{:S(2)}, u32[]{:S(2)}) collective-permute-start(bf16[256,256]{1,0:T(8,128)(2,1)S(1)} %collective-permute-done.3.d2), channel_id=1, source_target_pairs={{0,1},{1,0},{2,3},{3,2},{4,5},{5,4},{6,7},{7,6},{8,9},{9,8},{10,11... | collective-permute-start | bytes 393224 | tf_op jit(solution)/shard_map/diagonal_gather/ppermute | solution.py:301
  22.4 18.5 %copy-start.1 = (f32[4,64]{1,0:T(4,128)S(1)}, f32[4,64]{1,0:T(4,128)}, u32[]{:S(2)}) copy-start(f32[4,64]{1,0:T(4,128)} %param.17) | copy-start | bytes 3076
  22.4 18.5 %copy-start.2 = (s32[4,64]{1,0:T(4,128)S(1)}, s32[4,64]{1,0:T(4,128)}, u32[]{:S(2)}) copy-start(s32[4,64]{1,0:T(4,128)} %param.19) | copy-start | bytes 3076
  22.4 18.5 %copy-start.3 = (f32[4,64]{1,0:T(4,128)S(1)}, f32[4,64]{1,0:T(4,128)}, u32[]{:S(2)}) copy-start(f32[4,64]{1,0:T(4,128)} %param.16) | copy-start | bytes 3076
  22.4 18.5 %copy-start.4 = (s32[4,64]{1,0:T(4,128)S(1)}, s32[4,64]{1,0:T(4,128)}, u32[]{:S(2)}) copy-start(s32[4,64]{1,0:T(4,128)} %param.18) | copy-start | bytes 3076
  22.4 23.8 %copy-start.5 = (s32[128]{0:T(128)S(1)}, s32[128]{0:T(128)}, u32[]{:S(2)}) copy-start(s32[128]{0:T(128)} %owner.1) | copy-start | bytes 1540
  31.0 23.7 %all-to-all-start.1 = ((f32[128,8,128]{2,1,0:T(8,128)}), f32[128,8,128]{2,1,0:T(8,128)S(1)}, u32[]{:S(2)}, u32[]{:S(2)}) async-start(f32[128,8,128]{2,1,0:T(8,128)} %factors.1), calls=%async_computation.1 | async-start | bytes 1048576 | tf_op jit(solution)/shard_map/member_exchange/all_to_all | solution.py:385
  41.0 5.9 %collective-permute-start.5 = (f32[4,128]{1,0:T(4,128)S(1)}, f32[4,128]{1,0:T(4,128)S(1)}, u32[]{:S(2)}, u32[]{:S(2)}) collective-permute-start(f32[4,128]{1,0:T(4,128)S(1)} %pad_maximum_fusion.1.own), channel_id=1, source_target_pairs={{0,96},{1,97},{2,98},{3,99},{28,60},{29,61},{30,62},{31,63},{32,0}... | collective-permute-start | bytes 6152 | tf_op jit(solution)/shard_map/coefficient_halo/ppermute | solution.py:316

commit v12 on v11

--- a/solution.py
+++ b/solution.py
@@ -69,6 +69,7 @@
     left,
     kept,
     done,
+    sent,
 ):
     rows, cols, rank_max, cells = left.shape
     members = noise.shape[1]
@@ -100,10 +101,10 @@
         row = n ^ j
         local = owner[rows * w + row] - cols * n
         held = jnp.logical_and(local >= 0, local < cols)
-        kept[...] = jnp.where(lower, diag[...].astype(jnp.float32), 0.0).astype(jnp.bfloat16)
+        kept[j] = jnp.where(lower, diag[...].astype(jnp.float32), 0.0).astype(jnp.bfloat16)
         term = lax.dot_general(
             noise[jnp.clip(local, 0, cols - 1)],
-            kept[...],
+            kept[j],
             (((1,), (1,)), ((), ())),
             preferred_element_type=jnp.float32,
         )
@@ -134,9 +135,13 @@
                 turned[pl.ds(64 * g + 2 * p + h, 8, stride=8), :] = total[
                     8 * g : 8 * g + 8, 128 * h : 128 * h + 128
                 ]
-    for d in range(out.shape[0]):
-        member = d % members
-        out[d] = turned[8 * member : 8 * member + 8, :]
+    sends = [
+        pltpu.make_async_copy(turned, out.at[i], sent.at[i]) for i in range(out.shape[0])
+    ]
+    for send in sends:
+        send.start()
+    for send in sends:
+        send.wait()
 
 
 def set_weights(low, own, high, weight):
@@ -357,17 +362,18 @@
         ).astype(f32).reshape(rows, cols * rank_max)
         partial_sums = pl.pallas_call(
             factor_kernel,
-            out_shape=pltpu.VMEM((devices, 8, 128), f32),
+            out_shape=pltpu.HBM((devices // members, members * 8, 128), f32),
             in_specs=specs(SMEM, *[VMEM] * 4, *[pltpu.HBM] * 2, *[VMEM] * (narrow - 1)),
-            out_specs=pl.BlockSpec(memory_space=VMEM),
+            out_specs=pl.BlockSpec(memory_space=pltpu.HBM),
             scratch_shapes=[
                 pltpu.VMEM((rows, members, cols * rank_max), jnp.bfloat16),
                 pltpu.VMEM((members * 8, 128), f32),
                 pltpu.VMEM((rows, members, cells), f32),
                 pltpu.VMEM((rows, cols - EARLY, rank_max, cells), right_factors.dtype),
                 pltpu.VMEM(left_factors.shape, left_factors.dtype),
-                pltpu.VMEM(own_diag.shape, own_diag.dtype),
+                pltpu.VMEM((rows, *own_diag.shape), own_diag.dtype),
                 pltpu.SemaphoreType.DMA((CHUNKS + 2 * rows,)),
+                pltpu.SemaphoreType.DMA((devices // members,)),
             ],
             compiler_params=limit(24),
         )(
@@ -382,6 +388,7 @@
         )
 
     with jax.named_scope("member_exchange"):
+        partial_sums = partial_sums.reshape(devices, 8, 128)
         got = lax.all_to_all(partial_sums, BOTH, 0, 0, tiled=True)
 
     with jax.named_scope("place"):

time: 69.7 us -> 69.7 us (level)
  no operation moved by 1% of the time
where the time goes in v12:
time: 69.7 us; the launch traced here: 69.3 us
  starting transfers between devices  30.8 us (44%)
  blocking collectives  13 us (19%)
  waiting for transfers between devices  12.3 us (18%)
  Pallas kernels  11.9 us (17%)
  local copies, waits for them, and re-layouts  0.97 us (1%)
    all_to_all x1, blocking collectives, per_device(): lax.all_to_all(blocks, BOTH, 0, 0, axis_index_groups=slabs, tiled=True)  13 us
    all_to_all x1, starting transfers between devices, per_device(): got = lax.all_to_all(partial_sums, BOTH, 0, 0, tiled=True)  9.92 us
    pallas_call x1, Pallas kernels, per_device(): pl.pallas_call(factor_kernel, out_shape=pltpu.HBM((devices // members, me...  8.52 us
    all_to_all x1, waiting for transfers between devices, per_device(): got = lax.all_to_all(partial_sums, BOTH, 0, 0, tiled=True)  7.72 us
    ppermute x2, starting transfers between devices, per_device(): swapped, partner = [lax.ppermute(noise, BOTH, swap) for swap in swaps]  6.84 us
    ppermute x1, starting transfers between devices, per_device(): lax.ppermute(own, BOTH, [((z * group + r) * narrow + b, ((z + step) % nar...  5.15 us
    all_to_all x1, starting transfers between devices, per_device(): lax.all_to_all(sending, 'wide', 0, 0, axis_index_groups=lines, tiled=True)  4.18 us
    all_to_all x1, waiting for transfers between devices, per_device(): lax.all_to_all(sending, 'wide', 0, 0, axis_index_groups=lines, tiled=True)  2.9 us
  transfers between devices with their start and end apart: 8, of which 4 were waited for; matrix products, arithmetic and copies ran while one was open for 2% of the time, Pallas kernels for 2%

profile of v12, /device:TPU:1, one launch (start us, length us, event | category | flops | bytes accessed | tf_op | source)
XLA Modules:
  0.0 69.3 jit_solution(13638769437704299172)
XLA Ops:
  0.0 5.5 %collective-permute-start = (bf16[4,32,256]{2,1,0:T(8,128)(2,1)}, bf16[4,32,256]{2,1,0:T(8,128)(2,1)S(1)}, u32[]{:S(2)}, u32[]{:S(2)}) collective-permute-start(bf16[4,32,256]{2,1,0:T(8,128)(2,1)} %param.10), channel_id=1, source_target_pairs={{3,4},{1,36},{0,68},{2,100},{7,0},{5,32},{4,64},{6,96},{11,12},{9,... | collective-permute-start | bytes 196616 | tf_op jit(solution)/shard_map/noise_gather/ppermute | solution.py:310
  5.5 1.4 %collective-permute-start.1 = (bf16[4,32,256]{2,1,0:T(8,128)(2,1)}, bf16[4,32,256]{2,1,0:T(8,128)(2,1)S(1)}, u32[]{:S(2)}, u32[]{:S(2)}) collective-permute-start(bf16[4,32,256]{2,1,0:T(8,128)(2,1)} %param.10), channel_id=1, source_target_pairs={{3,0},{1,32},{0,64},{2,96},{7,4},{5,36},{4,68},{6,100},{11,8},{9,4... | collective-permute-start | bytes 196616 | tf_op jit(solution)/shard_map/noise_gather/ppermute | solution.py:310
  6.8 1.0 %collective-permute-start.2 = (bf16[256,256]{1,0:T(8,128)(2,1)}, bf16[256,256]{1,0:T(8,128)(2,1)S(1)}, u32[]{:S(2)}, u32[]{:S(2)}) collective-permute-start(bf16[256,256]{1,0:T(8,128)(2,1)} %bitcast.23), channel_id=1, source_target_pairs={{0,1},{1,0},{2,3},{3,2},{4,5},{5,4},{6,7},{7,6},{8,9},{9,8},{10,11... | collective-permute-start | bytes 393224 | tf_op jit(solution)/shard_map/diagonal_gather/ppermute | solution.py:304
  7.8 1.4 %collective-permute-start.3 = (bf16[256,256]{1,0:T(8,128)(2,1)}, bf16[256,256]{1,0:T(8,128)(2,1)S(1)}, u32[]{:S(2)}, u32[]{:S(2)}) collective-permute-start(bf16[256,256]{1,0:T(8,128)(2,1)} %bitcast.24), channel_id=1, source_target_pairs={{0,2},{1,3},{2,0},{3,1},{4,6},{5,7},{6,4},{7,5},{8,10},{9,11},{10,... | collective-permute-start | bytes 393224 | tf_op jit(solution)/shard_map/diagonal_gather/ppermute | solution.py:301
  9.2 0.1 broadcast_bitcast_fusion
  9.3 1.0 %collective-permute-done.1 = bf16[4,32,256]{2,1,0:T(8,128)(2,1)S(1)} collective-permute-done((bf16[4,32,256]{2,1,0:T(8,128)(2,1)}, bf16[4,32,256]{2,1,0:T(8,128)(2,1)S(1)}, u32[]{:S(2)}, u32[]{:S(2)}) %collective-permute-start.1) | collective-permute-done | bytes 65568 | tf_op jit(solution)/shard_map/noise_gather/ppermute | solution.py:310
  10.4 0.9 %broadcast_in_dim.5 = bf16[4,2,4,32,256]{4,3,2,1,0:T(8,128)(2,1)} broadcast(bf16[2,4,32,256]{3,2,1,0:T(8,128)(2,1)S(1)} %pad_maximum_fusion), dimensions={1,2,3,4} | broadcast | bytes 655360 | tf_op jit(solution)/shard_map/noise_gather/broadcast_in_dim | solution.py:337
  11.2 4.2 %all-to-all-start = ((bf16[4,2,4,32,256]{4,3,2,1,0:T(8,128)(2,1)}), bf16[4,2,4,32,256]{4,3,2,1,0:T(8,128)(2,1)S(1)}, u32[]{:S(2)}, u32[]{:S(2)}) async-start(bf16[4,2,4,32,256]{4,3,2,1,0:T(8,128)(2,1)} %broadcast_in_dim.5), calls=%async_computation | async-start | bytes 1048576 | tf_op jit(solution)/shard_map/noise_gather/all_to_all | solution.py:355
  15.4 0.0 collective-permute-done.3.d2
  15.4 2.4 %collective-permute-start.4 = (bf16[256,256]{1,0:T(8,128)(2,1)S(1)}, bf16[256,256]{1,0:T(8,128)(2,1)S(1)}, u32[]{:S(2)}, u32[]{:S(2)}) collective-permute-start(bf16[256,256]{1,0:T(8,128)(2,1)S(1)} %collective-permute-done.3.d2), channel_id=1, source_target_pairs={{0,1},{1,0},{2,3},{3,2},{4,5},{5,4},{6,7},{7,6},{8,9},{9,8},{10,11... | collective-permute-start | bytes 393224 | tf_op jit(solution)/shard_map/diagonal_gather/ppermute | solution.py:306
  17.8 0.1 fusion.keep
  17.9 1.6 %noise_gather.1 = (bf16[4,8,128,256]{3,2,1,0:T(8,128)(2,1)S(1)}, bf16[256,256]{1,0:T(8,128)(2,1)S(1)}) custom-call(bf16[4,32,128,256]{3,2,1,0:T(8,128)(2,1)} %right_far.1, bf16[256,256]{1,0:T(8,128)(2,1)} %bitcast.25), custom_call_target="tpu_custom_call" | custom-call | bytes 4194304 | tf_op jit(solution)/shard_map/noise_gather/pallas_call | solution.py:341
  19.5 0.0 collective-permute-done.2.d1
  19.5 2.9 %all-to-all-done = bf16[4,2,4,32,256]{4,3,2,1,0:T(8,128)(2,1)S(1)} async-done(((bf16[4,2,4,32,256]{4,3,2,1,0:T(8,128)(2,1)}), bf16[4,2,4,32,256]{4,3,2,1,0:T(8,128)(2,1)S(1)}, u32[]{:S(2)}, u32[]{:S(2)}) %all-to-all-start) | async-done | bytes 524320 | tf_op jit(solution)/shard_map/noise_gather/all_to_all | solution.py:355
  22.4 0.0 copy-start.5
  22.4 8.5 %factors.1 = f32[4,256,128]{2,1,0:T(8,128)} custom-call(s32[128]{0:T(128)} %owner.1, f32[4,4096]{1,0:T(4,128)S(1)} %fusion.keep, bf16[32,32,256]{2,1,0:T(8,128)(2,1)S(1)} %bitcast.20, bf16[4,8,128,256]{3,2,1,0:T(8,128)(2,1)S(1)} %get-tuple-element.13.early, bf16[256,256]{1,0:T(8,128)(2,1)S(1)} %get-tuple-element.14.d0, bf16[4,32,128,256]{3,2,1,0:T(8,128)(2,1)} %right_far.1, ...), custom_call_target="tpu_custom_call" | custom-call | tf_op jit(solution)/shard_map/factors/pallas_call | solution.py:363
  30.9 9.9 %all-to-all-start.1 = ((f32[128,8,128]{2,1,0:T(8,128)}), f32[128,8,128]{2,1,0:T(8,128)S(1)}, u32[]{:S(2)}, u32[]{:S(2)}) async-start(f32[128,8,128]{2,1,0:T(8,128)} %bitcast.22), calls=%async_computation.1 | async-start | bytes 1048576 | tf_op jit(solution)/shard_map/member_exchange/all_to_all | solution.py:392
  40.9 0.1 pad_maximum_fusion.1.own
  41.0 5.2 %collective-permute-start.5 = (f32[4,128]{1,0:T(4,128)S(1)}, f32[4,128]{1,0:T(4,128)S(1)}, u32[]{:S(2)}, u32[]{:S(2)}) collective-permute-start(f32[4,128]{1,0:T(4,128)S(1)} %pad_maximum_fusion.1.own), channel_id=1, source_target_pairs={{0,96},{1,97},{2,98},{3,99},{28,60},{29,61},{30,62},{31,63},{32,0}... | collective-permute-start | bytes 6152 | tf_op jit(solution)/shard_map/coefficient_halo/ppermute | solution.py:321
  46.2 0.7 collective-permute-done.5.forwarded
  46.9 7.7 %all-to-all-done.1 = f32[128,8,128]{2,1,0:T(8,128)S(1)} async-done(((f32[128,8,128]{2,1,0:T(8,128)}), f32[128,8,128]{2,1,0:T(8,128)S(1)}, u32[]{:S(2)}, u32[]{:S(2)}) %all-to-all-start.1) | async-done | bytes 524320 | tf_op jit(solution)/shard_map/member_exchange/all_to_all | solution.py:392
  54.6 0.6 place.1
  55.2 13.0 %all_to_all.15.slots = f32[32,16,128]{2,1,0:T(8,128)S(1)} all-to-all(f32[32,16,128]{2,1,0:T(8,128)S(1)} %place.1), channel_id=1, replica_groups={{0,1,2,3,4,5,6,7,8,9,10,11,12,13,14,15,16,17,18,19,20,21,22,23,24,25,26..., dimensions={0} | all-to-all | bytes 524288 | tf_op jit(solution)/shard_map/block_exchange/all_to_all | solution.py:409
  68.2 1.2 %stencil.1 = f32[32,4,64]{2,1,0:T(4,128)} custom-call(f32[32,16,128]{2,1,0:T(8,128)S(1)} %all_to_all.15.slots, f32[512,128]{1,0:T(8,128)S(1)} %bitcast.19), custom_call_target="tpu_custom_call" | custom-call | tf_op jit(solution)/shard_map/stencil/pallas_call | solution.py:412
  (18 shorter events, 0.1 us)
Async XLA Ops:
  0.0 9.2 %copy-start = (s32[4,32]{1,0:T(4,128)S(1)}, s32[4,32]{1,0:T(4,128)}, u32[]{:S(2)}) copy-start(s32[4,32]{1,0:T(4,128)} %param.14) | copy-start | bytes 1540
  0.0 9.3 %collective-permute-start = (bf16[4,32,256]{2,1,0:T(8,128)(2,1)}, bf16[4,32,256]{2,1,0:T(8,128)(2,1)S(1)}, u32[]{:S(2)}, u32[]{:S(2)}) collective-permute-start(bf16[4,32,256]{2,1,0:T(8,128)(2,1)} %param.10), channel_id=1, source_target_pairs={{3,4},{1,36},{0,68},{2,100},{7,0},{5,32},{4,64},{6,96},{11,12},{9,... | collective-permute-start | bytes 196616 | tf_op jit(solution)/shard_map/noise_gather/ppermute | solution.py:310
  5.5 4.8 %collective-permute-start.1 = (bf16[4,32,256]{2,1,0:T(8,128)(2,1)}, bf16[4,32,256]{2,1,0:T(8,128)(2,1)S(1)}, u32[]{:S(2)}, u32[]{:S(2)}) collective-permute-start(bf16[4,32,256]{2,1,0:T(8,128)(2,1)} %param.10), channel_id=1, source_target_pairs={{3,0},{1,32},{0,64},{2,96},{7,4},{5,36},{4,68},{6,100},{11,8},{9,4... | collective-permute-start | bytes 196616 | tf_op jit(solution)/shard_map/noise_gather/ppermute | solution.py:310
  6.8 12.6 %collective-permute-start.2 = (bf16[256,256]{1,0:T(8,128)(2,1)}, bf16[256,256]{1,0:T(8,128)(2,1)S(1)}, u32[]{:S(2)}, u32[]{:S(2)}) collective-permute-start(bf16[256,256]{1,0:T(8,128)(2,1)} %bitcast.23), channel_id=1, source_target_pairs={{0,1},{1,0},{2,3},{3,2},{4,5},{5,4},{6,7},{7,6},{8,9},{9,8},{10,11... | collective-permute-start | bytes 393224 | tf_op jit(solution)/shard_map/diagonal_gather/ppermute | solution.py:304
  7.8 7.6 %collective-permute-start.3 = (bf16[256,256]{1,0:T(8,128)(2,1)}, bf16[256,256]{1,0:T(8,128)(2,1)S(1)}, u32[]{:S(2)}, u32[]{:S(2)}) collective-permute-start(bf16[256,256]{1,0:T(8,128)(2,1)} %bitcast.24), channel_id=1, source_target_pairs={{0,2},{1,3},{2,0},{3,1},{4,6},{5,7},{6,4},{7,5},{8,10},{9,11},{10,... | collective-permute-start | bytes 393224 | tf_op jit(solution)/shard_map/diagonal_gather/ppermute | solution.py:301
  11.2 11.1 %all-to-all-start = ((bf16[4,2,4,32,256]{4,3,2,1,0:T(8,128)(2,1)}), bf16[4,2,4,32,256]{4,3,2,1,0:T(8,128)(2,1)S(1)}, u32[]{:S(2)}, u32[]{:S(2)}) async-start(bf16[4,2,4,32,256]{4,3,2,1,0:T(8,128)(2,1)} %broadcast_in_dim.5), calls=%async_computation | async-start | bytes 1048576 | tf_op jit(solution)/shard_map/noise_gather/all_to_all | solution.py:355
  15.4 4.0 %collective-permute-start.4 = (bf16[256,256]{1,0:T(8,128)(2,1)S(1)}, bf16[256,256]{1,0:T(8,128)(2,1)S(1)}, u32[]{:S(2)}, u32[]{:S(2)}) collective-permute-start(bf16[256,256]{1,0:T(8,128)(2,1)S(1)} %collective-permute-done.3.d2), channel_id=1, source_target_pairs={{0,1},{1,0},{2,3},{3,2},{4,5},{5,4},{6,7},{7,6},{8,9},{9,8},{10,11... | collective-permute-start | bytes 393224 | tf_op jit(solution)/shard_map/diagonal_gather/ppermute | solution.py:306
  22.4 18.5 %copy-start.1 = (f32[4,64]{1,0:T(4,128)S(1)}, f32[4,64]{1,0:T(4,128)}, u32[]{:S(2)}) copy-start(f32[4,64]{1,0:T(4,128)} %param.17) | copy-start | bytes 3076
  22.4 18.5 %copy-start.2 = (s32[4,64]{1,0:T(4,128)S(1)}, s32[4,64]{1,0:T(4,128)}, u32[]{:S(2)}) copy-start(s32[4,64]{1,0:T(4,128)} %param.19) | copy-start | bytes 3076
  22.4 18.5 %copy-start.3 = (f32[4,64]{1,0:T(4,128)S(1)}, f32[4,64]{1,0:T(4,128)}, u32[]{:S(2)}) copy-start(f32[4,64]{1,0:T(4,128)} %param.16) | copy-start | bytes 3076
  22.4 18.5 %copy-start.4 = (s32[4,64]{1,0:T(4,128)S(1)}, s32[4,64]{1,0:T(4,128)}, u32[]{:S(2)}) copy-start(s32[4,64]{1,0:T(4,128)} %param.18) | copy-start | bytes 3076
  22.4 23.8 %copy-start.5 = (s32[128]{0:T(128)S(1)}, s32[128]{0:T(128)}, u32[]{:S(2)}) copy-start(s32[128]{0:T(128)} %owner.1) | copy-start | bytes 1540
  30.9 23.7 %all-to-all-start.1 = ((f32[128,8,128]{2,1,0:T(8,128)}), f32[128,8,128]{2,1,0:T(8,128)S(1)}, u32[]{:S(2)}, u32[]{:S(2)}) async-start(f32[128,8,128]{2,1,0:T(8,128)} %bitcast.22), calls=%async_computation.1 | async-start | bytes 1048576 | tf_op jit(solution)/shard_map/member_exchange/all_to_all | solution.py:392
  41.0 5.9 %collective-permute-start.5 = (f32[4,128]{1,0:T(4,128)S(1)}, f32[4,128]{1,0:T(4,128)S(1)}, u32[]{:S(2)}, u32[]{:S(2)}) collective-permute-start(f32[4,128]{1,0:T(4,128)S(1)} %pad_maximum_fusion.1.own), channel_id=1, source_target_pairs={{0,96},{1,97},{2,98},{3,99},{28,60},{29,61},{30,62},{31,63},{32,0}... | collective-permute-start | bytes 6152 | tf_op jit(solution)/shard_map/coefficient_halo/ppermute | solution.py:321

commit v13 on v11

--- a/solution.py
+++ b/solution.py
@@ -36,6 +36,19 @@
 
 def halves(count):
     return slice(0, count // 2), slice(count // 2, count)
+
+
+def spread_kernel(mine, partner, out, done):
+    odd = lax.axis_index("wide") % 2
+    copies = [
+        pltpu.make_async_copy(source, out.at[i, odd ^ j], done.at[i, j])
+        for i in range(out.shape[0])
+        for j, source in enumerate((mine, partner))
+    ]
+    for copy in copies:
+        copy.start()
+    for copy in copies:
+        copy.wait()
 
 
 def fetch_kernel(right_far, diag_far, right, diag, done):
@@ -325,11 +338,14 @@
         )
 
     with jax.named_scope("noise_gather"):
-        odd = lax.axis_index("wide") % 2 == 1
-        both = jnp.stack(
-            [jnp.where(odd, partner, swapped), jnp.where(odd, swapped, partner)]
-        )
-        sending = jnp.broadcast_to(both[None], (group // 2, *both.shape))
+        sending = pl.pallas_call(
+            spread_kernel,
+            out_shape=pltpu.HBM((group // 2, 2, *noise.shape), noise.dtype),
+            in_specs=specs(VMEM, VMEM),
+            out_specs=pl.BlockSpec(memory_space=pltpu.HBM),
+            scratch_shapes=[pltpu.SemaphoreType.DMA((group // 2, 2))],
+            compiler_params=limit(1),
+        )(near(swapped), near(partner))
         sending, right_factors, own_diag = lax.optimization_barrier(
             (sending, right_factors, own_diag)
         )

time: 69.7 us -> 70.3 us (level)
  starting transfers between devices: 30.8 us -> 32.7 us
  waiting for transfers between devices: 12.3 us -> 11.1 us
  local copies, waits for them, and re-layouts: 0.97 us -> 0.1 us
  Pallas kernels: 11.9 us -> 12.7 us
    all_to_all x1, starting transfers between devices: 9.92 us -> 12.2 us  [per_device(): got = lax.all_to_all(partial_sums, BOTH, 0, 0, tiled=True)]
    ppermute x2, waiting for transfers between devices: 1.04 us -> 0.01 us  [per_device(): swapped, partner = [lax.ppermute(noise, BOTH, swap) for swap in swaps]]
    pallas_call x0 -> x1, Pallas kernels: none -> 0.88 us  [per_device(): pl.pallas_call(spread_kernel, out_shape=pltpu.HBM((group // 2, 2, *noise....]
    broadcast_in_dim x1 -> x0, local copies, waits for them, and re-layouts: 0.87 us -> none  [per_device(): sending = jnp.broadcast_to(both[None], (group // 2, *both.shape))]
  transfers between devices with their start and end apart: 8 -> 8, of which waited for: 4 -> 3; matrix products, arithmetic and copies ran while one was open for 2% -> 0% of each run, Pallas kernels for 2% -> 4%
where the time goes in v13:
time: 70.3 us; the launch traced here: 70 us
  starting transfers between devices  32.7 us (47%)
  blocking collectives  13 us (18%)
  Pallas kernels  12.7 us (18%)
  waiting for transfers between devices  11.1 us (16%)
    all_to_all x1, blocking collectives, per_device(): lax.all_to_all(blocks, BOTH, 0, 0, axis_index_groups=slabs, tiled=True)  13 us
    all_to_all x1, starting transfers between devices, per_device(): got = lax.all_to_all(partial_sums, BOTH, 0, 0, tiled=True)  12.2 us
    pallas_call x1, Pallas kernels, per_device(): pl.pallas_call(factor_kernel, out_shape=pltpu.VMEM((devices, 8, 128), f32...  8.51 us
    all_to_all x1, waiting for transfers between devices, per_device(): got = lax.all_to_all(partial_sums, BOTH, 0, 0, tiled=True)  7.72 us
    ppermute x2, starting transfers between devices, per_device(): swapped, partner = [lax.ppermute(noise, BOTH, swap) for swap in swaps]  6.84 us
    ppermute x1, starting transfers between devices, per_device(): lax.ppermute(own, BOTH, [((z * group + r) * narrow + b, ((z + step) % nar...  5.15 us
    all_to_all x1, starting transfers between devices, per_device(): lax.all_to_all(sending, 'wide', 0, 0, axis_index_groups=lines, tiled=True)  4.2 us
    all_to_all x1, waiting for transfers between devices, per_device(): lax.all_to_all(sending, 'wide', 0, 0, axis_index_groups=lines, tiled=True)  2.7 us
  transfers between devices with their start and end apart: 8, of which 3 were waited for; matrix products, arithmetic and copies ran while one was open for 0% of the time, Pallas kernels for 4%

profile of v13, /device:TPU:1, one launch (start us, length us, event | category | flops | bytes accessed | tf_op | source)
XLA Modules:
  0.0 70.0 jit_solution(13239008352240620918)
XLA Ops:
  0.0 3.0 %collective-permute-start = (bf16[4,32,256]{2,1,0:T(8,128)(2,1)}, bf16[4,32,256]{2,1,0:T(8,128)(2,1)S(1)}, u32[]{:S(2)}, u32[]{:S(2)}) collective-permute-start(bf16[4,32,256]{2,1,0:T(8,128)(2,1)} %param.10), channel_id=1, source_target_pairs={{3,0},{1,32},{0,64},{2,96},{7,4},{5,36},{4,68},{6,100},{11,8},{9,4... | collective-permute-start | bytes 196616 | tf_op jit(solution)/shard_map/noise_gather/ppermute | solution.py:318
  3.0 3.8 %collective-permute-start.1 = (bf16[4,32,256]{2,1,0:T(8,128)(2,1)}, bf16[4,32,256]{2,1,0:T(8,128)(2,1)S(1)}, u32[]{:S(2)}, u32[]{:S(2)}) collective-permute-start(bf16[4,32,256]{2,1,0:T(8,128)(2,1)} %param.10), channel_id=1, source_target_pairs={{3,4},{1,36},{0,68},{2,100},{7,0},{5,32},{4,64},{6,96},{11,12},{9,... | collective-permute-start | bytes 196616 | tf_op jit(solution)/shard_map/noise_gather/ppermute | solution.py:318
  6.8 0.8 %collective-permute-start.3 = (bf16[256,256]{1,0:T(8,128)(2,1)}, bf16[256,256]{1,0:T(8,128)(2,1)S(1)}, u32[]{:S(2)}, u32[]{:S(2)}) collective-permute-start(bf16[256,256]{1,0:T(8,128)(2,1)} %bitcast.17), channel_id=1, source_target_pairs={{0,2},{1,3},{2,0},{3,1},{4,6},{5,7},{6,4},{7,5},{8,10},{9,11},{10,... | collective-permute-start | bytes 393224 | tf_op jit(solution)/shard_map/diagonal_gather/ppermute | solution.py:309
  7.7 0.9 %collective-permute-start.2 = (bf16[256,256]{1,0:T(8,128)(2,1)}, bf16[256,256]{1,0:T(8,128)(2,1)S(1)}, u32[]{:S(2)}, u32[]{:S(2)}) collective-permute-start(bf16[256,256]{1,0:T(8,128)(2,1)} %bitcast.18), channel_id=1, source_target_pairs={{0,1},{1,0},{2,3},{3,2},{4,5},{5,4},{6,7},{7,6},{8,9},{9,8},{10,11... | collective-permute-start | bytes 393224 | tf_op jit(solution)/shard_map/diagonal_gather/ppermute | solution.py:312
  8.6 0.1 broadcast_bitcast_fusion
  8.7 0.0 collective-permute-done.mine
  8.7 0.9 %noise_gather.2 = bf16[4,2,4,32,256]{4,3,2,1,0:T(8,128)(2,1)} custom-call(bf16[4,32,256]{2,1,0:T(8,128)(2,1)S(1)} %collective-permute-done.mine, bf16[4,32,256]{2,1,0:T(8,128)(2,1)S(1)} %collective-permute-done.1.partner), custom_call_target="tpu_custom_call" | custom-call | tf_op jit(solution)/shard_map/noise_gather/pallas_call | solution.py:341
  9.6 4.2 %all-to-all-start = ((bf16[4,2,4,32,256]{4,3,2,1,0:T(8,128)(2,1)}), bf16[4,2,4,32,256]{4,3,2,1,0:T(8,128)(2,1)S(1)}, u32[]{:S(2)}, u32[]{:S(2)}) async-start(bf16[4,2,4,32,256]{4,3,2,1,0:T(8,128)(2,1)} %noise_gather.2), calls=%async_computation | async-start | bytes 1048576 | tf_op jit(solution)/shard_map/noise_gather/all_to_all | solution.py:366
  13.8 2.6 %collective-permute-start.4 = (bf16[256,256]{1,0:T(8,128)(2,1)S(1)}, bf16[256,256]{1,0:T(8,128)(2,1)S(1)}, u32[]{:S(2)}, u32[]{:S(2)}) collective-permute-start(bf16[256,256]{1,0:T(8,128)(2,1)S(1)} %collective-permute-done.3.d2), channel_id=1, source_target_pairs={{0,1},{1,0},{2,3},{3,2},{4,5},{5,4},{6,7},{7,6},{8,9},{9,8},{10,11... | collective-permute-start | bytes 393224 | tf_op jit(solution)/shard_map/diagonal_gather/ppermute | solution.py:314
  16.4 0.1 fusion.keep
  16.4 1.6 %noise_gather.3 = (bf16[4,8,128,256]{3,2,1,0:T(8,128)(2,1)S(1)}, bf16[256,256]{1,0:T(8,128)(2,1)S(1)}) custom-call(bf16[4,32,128,256]{3,2,1,0:T(8,128)(2,1)} %right_far.1, bf16[256,256]{1,0:T(8,128)(2,1)} %bitcast.19), custom_call_target="tpu_custom_call" | custom-call | bytes 4194304 | tf_op jit(solution)/shard_map/noise_gather/pallas_call | solution.py:352
  18.0 0.0 collective-permute-done.2.d1
  18.0 0.0 collective-permute-done.4.d3
  18.0 2.7 %all-to-all-done = bf16[4,2,4,32,256]{4,3,2,1,0:T(8,128)(2,1)S(1)} async-done(((bf16[4,2,4,32,256]{4,3,2,1,0:T(8,128)(2,1)}), bf16[4,2,4,32,256]{4,3,2,1,0:T(8,128)(2,1)S(1)}, u32[]{:S(2)}, u32[]{:S(2)}) %all-to-all-start) | async-done | bytes 524320 | tf_op jit(solution)/shard_map/noise_gather/all_to_all | solution.py:366
  20.7 0.0 copy-start.5
  20.8 8.5 %factors.1 = f32[128,8,128]{2,1,0:T(8,128)} custom-call(s32[128]{0:T(128)} %owner.1, f32[4,4096]{1,0:T(4,128)S(1)} %fusion.keep, bf16[32,32,256]{2,1,0:T(8,128)(2,1)S(1)} %bitcast.15, bf16[4,8,128,256]{3,2,1,0:T(8,128)(2,1)S(1)} %get-tuple-element.13.early, bf16[256,256]{1,0:T(8,128)(2,1)S(1)} %get-tuple-element.14.d0, bf16[4,32,128,256]{3,2,1,0:T(8,128)(2,1)} %right_far.1, ...), custom_call_target="tpu_custom_call" | custom-call | tf_op jit(solution)/shard_map/factors/pallas_call | solution.py:374
  29.3 12.2 %all-to-all-start.1 = ((f32[128,8,128]{2,1,0:T(8,128)}), f32[128,8,128]{2,1,0:T(8,128)S(1)}, u32[]{:S(2)}, u32[]{:S(2)}) async-start(f32[128,8,128]{2,1,0:T(8,128)} %factors.1), calls=%async_computation.1 | async-start | bytes 1048576 | tf_op jit(solution)/shard_map/member_exchange/all_to_all | solution.py:401
  41.5 0.1 pad_maximum_fusion.own
  41.6 5.2 %collective-permute-start.5 = (f32[4,128]{1,0:T(4,128)S(1)}, f32[4,128]{1,0:T(4,128)S(1)}, u32[]{:S(2)}, u32[]{:S(2)}) collective-permute-start(f32[4,128]{1,0:T(4,128)S(1)} %pad_maximum_fusion.own), channel_id=1, source_target_pairs={{0,96},{1,97},{2,98},{3,99},{28,60},{29,61},{30,62},{31,63},{32,0}... | collective-permute-start | bytes 6152 | tf_op jit(solution)/shard_map/coefficient_halo/ppermute | solution.py:329
  46.8 0.7 collective-permute-done.5.forwarded
  47.5 7.7 %all-to-all-done.1 = f32[128,8,128]{2,1,0:T(8,128)S(1)} async-done(((f32[128,8,128]{2,1,0:T(8,128)}), f32[128,8,128]{2,1,0:T(8,128)S(1)}, u32[]{:S(2)}, u32[]{:S(2)}) %all-to-all-start.1) | async-done | bytes 524320 | tf_op jit(solution)/shard_map/member_exchange/all_to_all | solution.py:401
  55.2 0.6 place.1
  55.8 13.0 %all_to_all.15.slots = f32[32,16,128]{2,1,0:T(8,128)S(1)} all-to-all(f32[32,16,128]{2,1,0:T(8,128)S(1)} %place.1), channel_id=1, replica_groups={{0,1,2,3,4,5,6,7,8,9,10,11,12,13,14,15,16,17,18,19,20,21,22,23,24,25,26..., dimensions={0} | all-to-all | bytes 524288 | tf_op jit(solution)/shard_map/block_exchange/all_to_all | solution.py:418
  68.8 1.2 %stencil.1 = f32[32,4,64]{2,1,0:T(4,128)} custom-call(f32[32,16,128]{2,1,0:T(8,128)S(1)} %all_to_all.15.slots, f32[512,128]{1,0:T(8,128)S(1)} %bitcast.14), custom_call_target="tpu_custom_call" | custom-call | tf_op jit(solution)/shard_map/stencil/pallas_call | solution.py:421
  (16 shorter events, 0.0 us)
Async XLA Ops:
  0.0 8.6 %copy-start = (s32[4,32]{1,0:T(4,128)S(1)}, s32[4,32]{1,0:T(4,128)}, u32[]{:S(2)}) copy-start(s32[4,32]{1,0:T(4,128)} %param.14) | copy-start | bytes 1540
  0.0 8.7 %collective-permute-start = (bf16[4,32,256]{2,1,0:T(8,128)(2,1)}, bf16[4,32,256]{2,1,0:T(8,128)(2,1)S(1)}, u32[]{:S(2)}, u32[]{:S(2)}) collective-permute-start(bf16[4,32,256]{2,1,0:T(8,128)(2,1)} %param.10), channel_id=1, source_target_pairs={{3,0},{1,32},{0,64},{2,96},{7,4},{5,36},{4,68},{6,100},{11,8},{9,4... | collective-permute-start | bytes 196616 | tf_op jit(solution)/shard_map/noise_gather/ppermute | solution.py:318
  3.0 5.7 %collective-permute-start.1 = (bf16[4,32,256]{2,1,0:T(8,128)(2,1)}, bf16[4,32,256]{2,1,0:T(8,128)(2,1)S(1)}, u32[]{:S(2)}, u32[]{:S(2)}) collective-permute-start(bf16[4,32,256]{2,1,0:T(8,128)(2,1)} %param.10), channel_id=1, source_target_pairs={{3,4},{1,36},{0,68},{2,100},{7,0},{5,32},{4,64},{6,96},{11,12},{9,... | collective-permute-start | bytes 196616 | tf_op jit(solution)/shard_map/noise_gather/ppermute | solution.py:318
  6.8 6.9 %collective-permute-start.3 = (bf16[256,256]{1,0:T(8,128)(2,1)}, bf16[256,256]{1,0:T(8,128)(2,1)S(1)}, u32[]{:S(2)}, u32[]{:S(2)}) collective-permute-start(bf16[256,256]{1,0:T(8,128)(2,1)} %bitcast.17), channel_id=1, source_target_pairs={{0,2},{1,3},{2,0},{3,1},{4,6},{5,7},{6,4},{7,5},{8,10},{9,11},{10,... | collective-permute-start | bytes 393224 | tf_op jit(solution)/shard_map/diagonal_gather/ppermute | solution.py:309
  7.7 10.3 %collective-permute-start.2 = (bf16[256,256]{1,0:T(8,128)(2,1)}, bf16[256,256]{1,0:T(8,128)(2,1)S(1)}, u32[]{:S(2)}, u32[]{:S(2)}) collective-permute-start(bf16[256,256]{1,0:T(8,128)(2,1)} %bitcast.18), channel_id=1, source_target_pairs={{0,1},{1,0},{2,3},{3,2},{4,5},{5,4},{6,7},{7,6},{8,9},{9,8},{10,11... | collective-permute-start | bytes 393224 | tf_op jit(solution)/shard_map/diagonal_gather/ppermute | solution.py:312
  9.6 11.1 %all-to-all-start = ((bf16[4,2,4,32,256]{4,3,2,1,0:T(8,128)(2,1)}), bf16[4,2,4,32,256]{4,3,2,1,0:T(8,128)(2,1)S(1)}, u32[]{:S(2)}, u32[]{:S(2)}) async-start(bf16[4,2,4,32,256]{4,3,2,1,0:T(8,128)(2,1)} %noise_gather.2), calls=%async_computation | async-start | bytes 1048576 | tf_op jit(solution)/shard_map/noise_gather/all_to_all | solution.py:366
  13.8 4.2 %collective-permute-start.4 = (bf16[256,256]{1,0:T(8,128)(2,1)S(1)}, bf16[256,256]{1,0:T(8,128)(2,1)S(1)}, u32[]{:S(2)}, u32[]{:S(2)}) collective-permute-start(bf16[256,256]{1,0:T(8,128)(2,1)S(1)} %collective-permute-done.3.d2), channel_id=1, source_target_pairs={{0,1},{1,0},{2,3},{3,2},{4,5},{5,4},{6,7},{7,6},{8,9},{9,8},{10,11... | collective-permute-start | bytes 393224 | tf_op jit(solution)/shard_map/diagonal_gather/ppermute | solution.py:314
  20.7 20.7 %copy-start.1 = (f32[4,64]{1,0:T(4,128)S(1)}, f32[4,64]{1,0:T(4,128)}, u32[]{:S(2)}) copy-start(f32[4,64]{1,0:T(4,128)} %param.17) | copy-start | bytes 3076
  20.7 20.8 %copy-start.2 = (s32[4,64]{1,0:T(4,128)S(1)}, s32[4,64]{1,0:T(4,128)}, u32[]{:S(2)}) copy-start(s32[4,64]{1,0:T(4,128)} %param.19) | copy-start | bytes 3076
  20.7 20.8 %copy-start.3 = (f32[4,64]{1,0:T(4,128)S(1)}, f32[4,64]{1,0:T(4,128)}, u32[]{:S(2)}) copy-start(f32[4,64]{1,0:T(4,128)} %param.16) | copy-start | bytes 3076
  20.7 20.8 %copy-start.4 = (s32[4,64]{1,0:T(4,128)S(1)}, s32[4,64]{1,0:T(4,128)}, u32[]{:S(2)}) copy-start(s32[4,64]{1,0:T(4,128)} %param.18) | copy-start | bytes 3076
  20.7 26.0 %copy-start.5 = (s32[128]{0:T(128)S(1)}, s32[128]{0:T(128)}, u32[]{:S(2)}) copy-start(s32[128]{0:T(128)} %owner.1) | copy-start | bytes 1540
  29.3 25.9 %all-to-all-start.1 = ((f32[128,8,128]{2,1,0:T(8,128)}), f32[128,8,128]{2,1,0:T(8,128)S(1)}, u32[]{:S(2)}, u32[]{:S(2)}) async-start(f32[128,8,128]{2,1,0:T(8,128)} %factors.1), calls=%async_computation.1 | async-start | bytes 1048576 | tf_op jit(solution)/shard_map/member_exchange/all_to_all | solution.py:401
  41.6 5.9 %collective-permute-start.5 = (f32[4,128]{1,0:T(4,128)S(1)}, f32[4,128]{1,0:T(4,128)S(1)}, u32[]{:S(2)}, u32[]{:S(2)}) collective-permute-start(f32[4,128]{1,0:T(4,128)S(1)} %pad_maximum_fusion.own), channel_id=1, source_target_pairs={{0,96},{1,97},{2,98},{3,99},{28,60},{29,61},{30,62},{31,63},{32,0}... | collective-permute-start | bytes 6152 | tf_op jit(solution)/shard_map/coefficient_halo/ppermute | solution.py:329

commit v14 on v11

--- a/solution.py
+++ b/solution.py
@@ -312,6 +312,7 @@
             ],
             axis=1,
         )
+        swapped, partner, own = lax.optimization_barrier((swapped, partner, own))
         last = group - 1
         forwarded = lax.ppermute(
             own,
@@ -350,6 +351,7 @@
         columns = lax.all_to_all(
             sending, "wide", 0, 0, axis_index_groups=lines, tiled=True
         ).reshape(cols, members, cells)
+        columns, forwarded = lax.optimization_barrier((columns, forwarded))
 
     with jax.named_scope("factors"):
         keep = (

time: 69.7 us -> 72.6 us (1.042)
  waiting for transfers between devices: 12.3 us -> 18.7 us
  starting transfers between devices: 30.8 us -> 26.7 us
  other arithmetic: 0.18 us -> 0.92 us
    all_to_all x1, waiting for transfers between devices: 7.72 us -> 13.7 us  [per_device(): got = lax.all_to_all(partial_sums, BOTH, 0, 0, tiled=True)]
    all_to_all x1, starting transfers between devices: 9.92 us -> 7.14 us  [per_device(): got = lax.all_to_all(partial_sums, BOTH, 0, 0, tiled=True)]
    all_to_all x1, waiting for transfers between devices: 2.9 us -> 4.76 us  [per_device(): lax.all_to_all(sending, 'wide', 0, 0, axis_index_groups=lines, tiled=True)]
    ppermute x1, starting transfers between devices: 1.35 us -> 2.35 us  [per_device(): opposite = lax.ppermute(own_diag, 'narrow', across)]
    ppermute x1, starting transfers between devices: 1 us -> 0.01 us  [per_device(): lax.ppermute(own_diag, 'narrow', beside)]
    ppermute x1, starting transfers between devices: 2.39 us -> 1.42 us  [per_device(): lax.ppermute(opposite, 'narrow', beside)]
    ppermute x2, waiting for transfers between devices: 1.04 us -> 0.23 us  [per_device(): swapped, partner = [lax.ppermute(noise, BOTH, swap) for swap in swaps]]
    select_n x1, other arithmetic: 0.01 us -> 0.75 us  [per_device(): jnp.where(flag == 1, value, -value)]
  transfers between devices with their start and end apart: 8 -> 8, of which waited for: 4 -> 3; matrix products, arithmetic and copies ran while one was open for 2% -> 3% of each run, Pallas kernels for 2% -> 2%
where the time goes in v14:
time: 72.6 us; the launch traced here: 72.2 us
  starting transfers between devices  26.7 us (37%)
  waiting for transfers between devices  18.7 us (26%)
  blocking collectives  13 us (18%)
  Pallas kernels  11.9 us (16%)
  local copies, waits for them, and re-layouts  0.94 us (1%)
  other arithmetic  0.92 us (1%)
    all_to_all x1, waiting for transfers between devices, per_device(): got = lax.all_to_all(partial_sums, BOTH, 0, 0, tiled=True)  13.7 us
    all_to_all x1, blocking collectives, per_device(): lax.all_to_all(blocks, BOTH, 0, 0, axis_index_groups=slabs, tiled=True)  13 us
    pallas_call x1, Pallas kernels, per_device(): pl.pallas_call(factor_kernel, out_shape=pltpu.VMEM((devices, 8, 128), f32...  8.52 us
    all_to_all x1, starting transfers between devices, per_device(): got = lax.all_to_all(partial_sums, BOTH, 0, 0, tiled=True)  7.14 us
    ppermute x2, starting transfers between devices, per_device(): swapped, partner = [lax.ppermute(noise, BOTH, swap) for swap in swaps]  6.84 us
    ppermute x1, starting transfers between devices, per_device(): lax.ppermute(own, BOTH, [((z * group + r) * narrow + b, ((z + step) % nar...  5.5 us
    all_to_all x1, waiting for transfers between devices, per_device(): lax.all_to_all(sending, 'wide', 0, 0, axis_index_groups=lines, tiled=True)  4.76 us
    all_to_all x1, starting transfers between devices, per_device(): lax.all_to_all(sending, 'wide', 0, 0, axis_index_groups=lines, tiled=True)  3.47 us
  transfers between devices with their start and end apart: 8, of which 3 were waited for; matrix products, arithmetic and copies ran while one was open for 3% of the time, Pallas kernels for 2%

profile of v14, /device:TPU:1, one launch (start us, length us, event | category | flops | bytes accessed | tf_op | source)
XLA Modules:
  0.0 72.2 jit_solution(5137106168318007530)
XLA Ops:
  0.0 5.5 %collective-permute-start.1 = (bf16[4,32,256]{2,1,0:T(8,128)(2,1)}, bf16[4,32,256]{2,1,0:T(8,128)(2,1)S(1)}, u32[]{:S(2)}, u32[]{:S(2)}) collective-permute-start(bf16[4,32,256]{2,1,0:T(8,128)(2,1)} %param.10), channel_id=1, source_target_pairs={{3,4},{1,36},{0,68},{2,100},{7,0},{5,32},{4,64},{6,96},{11,12},{9,... | collective-permute-start | bytes 196616 | tf_op jit(solution)/shard_map/noise_gather/ppermute | solution.py:305
  5.5 1.4 %collective-permute-start = (bf16[4,32,256]{2,1,0:T(8,128)(2,1)}, bf16[4,32,256]{2,1,0:T(8,128)(2,1)S(1)}, u32[]{:S(2)}, u32[]{:S(2)}) collective-permute-start(bf16[4,32,256]{2,1,0:T(8,128)(2,1)} %param.10), channel_id=1, source_target_pairs={{3,0},{1,32},{0,64},{2,96},{7,4},{5,36},{4,68},{6,100},{11,8},{9,4... | collective-permute-start | bytes 196616 | tf_op jit(solution)/shard_map/noise_gather/ppermute | solution.py:305
  6.8 2.3 %collective-permute-start.4 = (bf16[256,256]{1,0:T(8,128)(2,1)}, bf16[256,256]{1,0:T(8,128)(2,1)S(1)}, u32[]{:S(2)}, u32[]{:S(2)}) collective-permute-start(bf16[256,256]{1,0:T(8,128)(2,1)} %bitcast.21), channel_id=1, source_target_pairs={{0,2},{1,3},{2,0},{3,1},{4,6},{5,7},{6,4},{7,5},{8,10},{9,11},{10,... | collective-permute-start | bytes 393224 | tf_op jit(solution)/shard_map/diagonal_gather/ppermute | solution.py:296
  9.2 0.0 collective-permute-start.3
  9.2 0.1 broadcast_bitcast_fusion
  9.3 0.7 %negate_select_fusion = (f32[4,64]{1,0:T(4,128)S(1)}, f32[4,64]{1,0:T(4,128)S(1)}) fusion(f32[4,64]{1,0:T(4,128)} %param.17, s32[4,64]{1,0:T(4,128)} %param.19, f32[4,64]{1,0:T(4,128)} %param.16, s32[4,64]{1,0:T(4,128)} %param.18), kind=kLoop, calls=%fused_computation.7 | loop fusion | flops 1536 | bytes 6144 | tf_op jit(solution)/shard_map/coefficient_halo/jit(_where)/select_n | solution.py:310
  10.0 0.1 pad_maximum_fusion.1.own
  10.1 0.0 collective-permute-done.1
  10.1 0.2 collective-permute-done
  10.3 5.5 %collective-permute-start.2 = (f32[4,128]{1,0:T(4,128)S(1)}, f32[4,128]{1,0:T(4,128)S(1)}, u32[]{:S(2)}, u32[]{:S(2)}) collective-permute-start(f32[4,128]{1,0:T(4,128)S(1)} %pad_maximum_fusion.1.own), channel_id=1, source_target_pairs={{0,96},{1,97},{2,98},{3,99},{28,60},{29,61},{30,62},{31,63},{32,0}... | collective-permute-start | bytes 6152 | tf_op jit(solution)/shard_map/coefficient_halo/ppermute | solution.py:317
  15.9 0.9 %broadcast_in_dim.5 = bf16[4,2,4,32,256]{4,3,2,1,0:T(8,128)(2,1)} broadcast(bf16[2,4,32,256]{3,2,1,0:T(8,128)(2,1)S(1)} %pad_maximum_fusion), dimensions={1,2,3,4} | broadcast | bytes 655360 | tf_op jit(solution)/shard_map/noise_gather/broadcast_in_dim | solution.py:333
  16.7 3.5 %all-to-all-start = ((bf16[4,2,4,32,256]{4,3,2,1,0:T(8,128)(2,1)}), bf16[4,2,4,32,256]{4,3,2,1,0:T(8,128)(2,1)S(1)}, u32[]{:S(2)}, u32[]{:S(2)}) async-start(bf16[4,2,4,32,256]{4,3,2,1,0:T(8,128)(2,1)} %broadcast_in_dim.5), calls=%async_computation | async-start | bytes 1048576 | tf_op jit(solution)/shard_map/noise_gather/all_to_all | solution.py:351
  20.2 0.0 collective-permute-done.4.d2
  20.2 1.4 %collective-permute-start.5 = (bf16[256,256]{1,0:T(8,128)(2,1)S(1)}, bf16[256,256]{1,0:T(8,128)(2,1)S(1)}, u32[]{:S(2)}, u32[]{:S(2)}) collective-permute-start(bf16[256,256]{1,0:T(8,128)(2,1)S(1)} %collective-permute-done.4.d2), channel_id=1, source_target_pairs={{0,1},{1,0},{2,3},{3,2},{4,5},{5,4},{6,7},{7,6},{8,9},{9,8},{10,11... | collective-permute-start | bytes 393224 | tf_op jit(solution)/shard_map/diagonal_gather/ppermute | solution.py:301
  21.7 0.1 fusion.keep
  21.7 1.6 %noise_gather.1 = (bf16[4,8,128,256]{3,2,1,0:T(8,128)(2,1)S(1)}, bf16[256,256]{1,0:T(8,128)(2,1)S(1)}) custom-call(bf16[4,32,128,256]{3,2,1,0:T(8,128)(2,1)} %right_far.1, bf16[256,256]{1,0:T(8,128)(2,1)} %bitcast.23), custom_call_target="tpu_custom_call" | custom-call | bytes 4194304 | tf_op jit(solution)/shard_map/noise_gather/pallas_call | solution.py:337
  23.3 4.8 %all-to-all-done = bf16[4,2,4,32,256]{4,3,2,1,0:T(8,128)(2,1)S(1)} async-done(((bf16[4,2,4,32,256]{4,3,2,1,0:T(8,128)(2,1)}), bf16[4,2,4,32,256]{4,3,2,1,0:T(8,128)(2,1)S(1)}, u32[]{:S(2)}, u32[]{:S(2)}) %all-to-all-start) | async-done | bytes 524320 | tf_op jit(solution)/shard_map/noise_gather/all_to_all | solution.py:351
  28.1 0.0 collective-permute-done.5.d3
  28.1 8.5 %factors.1 = f32[128,8,128]{2,1,0:T(8,128)} custom-call(s32[128]{0:T(128)} %owner.1, f32[4,4096]{1,0:T(4,128)S(1)} %fusion.keep, bf16[32,32,256]{2,1,0:T(8,128)(2,1)S(1)} %bitcast.19, bf16[4,8,128,256]{3,2,1,0:T(8,128)(2,1)S(1)} %get-tuple-element.22.early, bf16[256,256]{1,0:T(8,128)(2,1)S(1)} %get-tuple-element.23.d0, bf16[4,32,128,256]{3,2,1,0:T(8,128)(2,1)} %right_far.1, ...), custom_call_target="tpu_custom_call" | custom-call | tf_op jit(solution)/shard_map/factors/pallas_call | solution.py:360
  36.6 7.1 %all-to-all-start.1 = ((f32[128,8,128]{2,1,0:T(8,128)}), f32[128,8,128]{2,1,0:T(8,128)S(1)}, u32[]{:S(2)}, u32[]{:S(2)}) async-start(f32[128,8,128]{2,1,0:T(8,128)} %factors.1), calls=%async_computation.1 | async-start | bytes 1048576 | tf_op jit(solution)/shard_map/member_exchange/all_to_all | solution.py:387
  43.8 13.7 %all-to-all-done.1 = f32[128,8,128]{2,1,0:T(8,128)S(1)} async-done(((f32[128,8,128]{2,1,0:T(8,128)}), f32[128,8,128]{2,1,0:T(8,128)S(1)}, u32[]{:S(2)}, u32[]{:S(2)}) %all-to-all-start.1) | async-done | bytes 524320 | tf_op jit(solution)/shard_map/member_exchange/all_to_all | solution.py:387
  57.5 0.6 place.1
  58.1 13.0 %all_to_all.15.slots = f32[32,16,128]{2,1,0:T(8,128)S(1)} all-to-all(f32[32,16,128]{2,1,0:T(8,128)S(1)} %place.1), channel_id=1, replica_groups={{0,1,2,3,4,5,6,7,8,9,10,11,12,13,14,15,16,17,18,19,20,21,22,23,24,25,26..., dimensions={0} | all-to-all | bytes 524288 | tf_op jit(solution)/shard_map/block_exchange/all_to_all | solution.py:404
  71.0 1.2 %stencil.1 = f32[32,4,64]{2,1,0:T(4,128)} custom-call(f32[32,16,128]{2,1,0:T(8,128)S(1)} %all_to_all.15.slots, f32[512,128]{1,0:T(8,128)S(1)} %bitcast.18), custom_call_target="tpu_custom_call" | custom-call | tf_op jit(solution)/shard_map/stencil/pallas_call | solution.py:407
  (10 shorter events, 0.1 us)
Async XLA Ops:
  0.0 9.2 %copy-start = (s32[4,32]{1,0:T(4,128)S(1)}, s32[4,32]{1,0:T(4,128)}, u32[]{:S(2)}) copy-start(s32[4,32]{1,0:T(4,128)} %param.14) | copy-start | bytes 1540
  0.0 10.1 %collective-permute-start.1 = (bf16[4,32,256]{2,1,0:T(8,128)(2,1)}, bf16[4,32,256]{2,1,0:T(8,128)(2,1)S(1)}, u32[]{:S(2)}, u32[]{:S(2)}) collective-permute-start(bf16[4,32,256]{2,1,0:T(8,128)(2,1)} %param.10), channel_id=1, source_target_pairs={{3,4},{1,36},{0,68},{2,100},{7,0},{5,32},{4,64},{6,96},{11,12},{9,... | collective-permute-start | bytes 196616 | tf_op jit(solution)/shard_map/noise_gather/ppermute | solution.py:305
  5.5 4.8 %collective-permute-start = (bf16[4,32,256]{2,1,0:T(8,128)(2,1)}, bf16[4,32,256]{2,1,0:T(8,128)(2,1)S(1)}, u32[]{:S(2)}, u32[]{:S(2)}) collective-permute-start(bf16[4,32,256]{2,1,0:T(8,128)(2,1)} %param.10), channel_id=1, source_target_pairs={{3,0},{1,32},{0,64},{2,96},{7,4},{5,36},{4,68},{6,100},{11,8},{9,4... | collective-permute-start | bytes 196616 | tf_op jit(solution)/shard_map/noise_gather/ppermute | solution.py:305
  6.8 13.4 %collective-permute-start.4 = (bf16[256,256]{1,0:T(8,128)(2,1)}, bf16[256,256]{1,0:T(8,128)(2,1)S(1)}, u32[]{:S(2)}, u32[]{:S(2)}) collective-permute-start(bf16[256,256]{1,0:T(8,128)(2,1)} %bitcast.21), channel_id=1, source_target_pairs={{0,2},{1,3},{2,0},{3,1},{4,6},{5,7},{6,4},{7,5},{8,10},{9,11},{10,... | collective-permute-start | bytes 393224 | tf_op jit(solution)/shard_map/diagonal_gather/ppermute | solution.py:296
  9.2 18.9 %collective-permute-start.3 = (bf16[256,256]{1,0:T(8,128)(2,1)}, bf16[256,256]{1,0:T(8,128)(2,1)S(1)}, u32[]{:S(2)}, u32[]{:S(2)}) collective-permute-start(bf16[256,256]{1,0:T(8,128)(2,1)} %bitcast.22), channel_id=1, source_target_pairs={{0,1},{1,0},{2,3},{3,2},{4,5},{5,4},{6,7},{7,6},{8,9},{9,8},{10,11... | collective-permute-start | bytes 393224 | tf_op jit(solution)/shard_map/diagonal_gather/ppermute | solution.py:299
  10.3 13.0 %collective-permute-start.2 = (f32[4,128]{1,0:T(4,128)S(1)}, f32[4,128]{1,0:T(4,128)S(1)}, u32[]{:S(2)}, u32[]{:S(2)}) collective-permute-start(f32[4,128]{1,0:T(4,128)S(1)} %pad_maximum_fusion.1.own), channel_id=1, source_target_pairs={{0,96},{1,97},{2,98},{3,99},{28,60},{29,61},{30,62},{31,63},{32,0}... | collective-permute-start | bytes 6152 | tf_op jit(solution)/shard_map/coefficient_halo/ppermute | solution.py:317
  16.7 11.3 %all-to-all-start = ((bf16[4,2,4,32,256]{4,3,2,1,0:T(8,128)(2,1)}), bf16[4,2,4,32,256]{4,3,2,1,0:T(8,128)(2,1)S(1)}, u32[]{:S(2)}, u32[]{:S(2)}) async-start(bf16[4,2,4,32,256]{4,3,2,1,0:T(8,128)(2,1)} %broadcast_in_dim.5), calls=%async_computation | async-start | bytes 1048576 | tf_op jit(solution)/shard_map/noise_gather/all_to_all | solution.py:351
  20.2 7.8 %collective-permute-start.5 = (bf16[256,256]{1,0:T(8,128)(2,1)S(1)}, bf16[256,256]{1,0:T(8,128)(2,1)S(1)}, u32[]{:S(2)}, u32[]{:S(2)}) collective-permute-start(bf16[256,256]{1,0:T(8,128)(2,1)S(1)} %collective-permute-done.4.d2), channel_id=1, source_target_pairs={{0,1},{1,0},{2,3},{3,2},{4,5},{5,4},{6,7},{7,6},{8,9},{9,8},{10,11... | collective-permute-start | bytes 393224 | tf_op jit(solution)/shard_map/diagonal_gather/ppermute | solution.py:301
  28.1 15.7 %copy-start.1 = (s32[128]{0:T(128)S(1)}, s32[128]{0:T(128)}, u32[]{:S(2)}) copy-start(s32[128]{0:T(128)} %owner.1) | copy-start | bytes 1540
  36.6 20.9 %all-to-all-start.1 = ((f32[128,8,128]{2,1,0:T(8,128)}), f32[128,8,128]{2,1,0:T(8,128)S(1)}, u32[]{:S(2)}, u32[]{:S(2)}) async-start(f32[128,8,128]{2,1,0:T(8,128)} %factors.1), calls=%async_computation.1 | async-start | bytes 1048576 | tf_op jit(solution)/shard_map/member_exchange/all_to_all | solution.py:387
